TPU v7x, 32 devices: a whole 2x2x4 slice. The times are simulated.
32 devices in a mesh: dp: 8 (over z, y), head: 4 (over x, core).
Axes of the slice: x: 2, y: 2, z: 4, core: 2. Of those that a mesh axis runs over, the one named last changes fastest.
Arguments:
- inputs: bfloat16 [8192, 2048], P('dp', 'head'), may hold values from -6 to 6
- cotangent: bfloat16 [8192, 2048], P('dp', 'head'), may hold values from -6 to 6
- token_valid: int32 [8192], P('dp'), may hold values from 0 to 1, as said below
- block_opens: int32 [32], P('dp'), may hold values from 0 to 1, as said below
- block_widths: int32 [32], P('dp'), may hold values from 16 to 64, as said below
- weight_inner: float32 [2048, 2, 4096], P('dp', None, 'head'), may hold values from -0.125 to 0.125
- weight_step: float32 [2048, 64], P('dp', 'head'), may hold values from -0.125 to 0.125
- weight_output: float32 [4096, 2048], P('head', 'dp'), may hold values from -0.09375 to 0.09375
- weight_state: float32 [2048, 256], P(('dp', 'head')), may hold values from -0.125 to 0.125
- norm_gain: float32 [2048], P(('dp', 'head')), may hold values from 0.5 to 1.5
- channel_table: float32 [6, 4096], P(None, 'head'), may hold values from -1.5 to 1.5, as said below
- head_table: float32 [3, 64], P(None, 'head'), may hold values from -9 to 1.5
- state_filter: float32 [256, 5], P(('dp', 'head')), may hold values from -2.5 to 2.5
- momentum_inner: float32 [2048, 2, 4096], P('dp', None, 'head'), may hold values from -112 to 112
- momentum_step: float32 [2048, 64], P('dp', 'head'), may hold values from -160 to 160
- momentum_output: float32 [4096, 2048], P('head', 'dp'), may hold values from -256 to 256
- momentum_state: float32 [2048, 256], P(('dp', 'head')), may hold values from -56 to 56
- momentum_gain: float32 [2048], P(('dp', 'head')), may hold values from -512 to 512
- momentum_channel: float32 [6, 4096], P(None, 'head'), may hold values from -256 to 256
- momentum_head: float32 [3, 64], P(None, 'head'), may hold values from -1024 to 1024
- momentum_filter: float32 [256, 5], P(('dp', 'head')), may hold values from -256 to 256
- average_inner: float32 [2048, 2, 4096], P('dp', None, 'head'), may hold values from -0.125 to 0.125
- average_step: float32 [2048, 64], P('dp', 'head'), may hold values from -0.125 to 0.125
- average_output: float32 [4096, 2048], P('head', 'dp'), may hold values from -0.09375 to 0.09375
- average_state: float32 [2048, 256], P(('dp', 'head')), may hold values from -0.125 to 0.125
- average_gain: float32 [2048], P(('dp', 'head')), may hold values from 0.5 to 1.5
- average_channel: float32 [6, 4096], P(None, 'head'), may hold values from -3 to 3
- average_head: float32 [3, 64], P(None, 'head'), may hold values from -6 to 6
- average_filter: float32 [256, 5], P(('dp', 'head')), may hold values from -3 to 3
Outputs:
- layer_output: bfloat16 [8192, 2048], P('dp', 'head')
- grad_input: float32 [8192, 2048], P('dp', 'head')
- updated_inner: float32 [2048, 2, 4096], P('dp', None, 'head')
- carried_inner: float32 [2048, 2, 4096], P('dp', None, 'head')
- smoothed_inner: float32 [2048, 2, 4096], P('dp', None, 'head')
- updated_step: float32 [2048, 64], P('dp', 'head')
- carried_step: float32 [2048, 64], P('dp', 'head')
- smoothed_step: float32 [2048, 64], P('dp', 'head')
- updated_output: float32 [4096, 2048], P('head', 'dp')
- carried_output: float32 [4096, 2048], P('head', 'dp')
- smoothed_output: float32 [4096, 2048], P('head', 'dp')
- updated_state: float32 [2048, 256], P(('dp', 'head'))
- carried_state: float32 [2048, 256], P(('dp', 'head'))
- smoothed_state: float32 [2048, 256], P(('dp', 'head'))
- updated_gain: float32 [2048], P(('dp', 'head'))
- carried_gain: float32 [2048], P(('dp', 'head'))
- smoothed_gain: float32 [2048], P(('dp', 'head'))
- updated_channel: float32 [6, 4096], P(None, 'head')
- carried_channel: float32 [6, 4096], P(None, 'head')
- smoothed_channel: float32 [6, 4096], P(None, 'head')
- updated_head: float32 [3, 64], P(None, 'head')
- carried_head: float32 [3, 64], P(None, 'head')
- smoothed_head: float32 [3, 64], P(None, 'head')
- updated_filter: float32 [256, 5], P(('dp', 'head'))
- carried_filter: float32 [256, 5], P(('dp', 'head'))
- smoothed_filter: float32 [256, 5], P(('dp', 'head'))
Inputs may be any that keep to these rules, and one draw needn't show every extreme that they name: `block_opens`: the first block of each index of dp's 1024 tokens begins a sequence; some index of dp holds one sequence of all its 1024 tokens. `block_widths`: the same for all blocks of a sequence, a multiple of 16. `token_valid`: 1 on a prefix of each sequence that covers all its blocks but the last, and 128 or more tokens of the last; 0 on the rest of that block. `channel_table`: rows 0 to 3 taps, row 4 biases, row 5 gains.
All inputs are finite; a program needn't handle non-finite values.
Results may differ from a plain program's by a relative error of at most 0.0095.
The roundings to bfloat16 on the way count: a program that leaves them out, or rounds other values in their place, can miss the bound.
Values may be sent and summed in bfloat16 or wider, within the bound.
No kernel may reach another device: no remote copies, remote signals or barrier semaphores. Data moves between devices by JAX's collectives and lax.ppermute only.
A program may use at most 192 MiB of HBM per device.

v0:
```python
import math

import jax
import jax.numpy as jnp
from jax import lax
from jax.sharding import PartitionSpec as P

D = 2048
H = 64
P_SIZE = 64
NS = 128
KC = 4
BLK = 256


EPS = 1e-05
MOMENTUM = 0.9
DECAY = 0.0001
AVERAGE = 0.75
RATE_MATRIX = 0.02
RATE_VECTOR = 0.1
HIGHEST = lax.Precision.HIGHEST


def rounded(value):
    return lax.optimization_barrier(value.astype(jnp.bfloat16)).astype(jnp.float32)


def convolve(inner_x, state_bc, taps_x, taps_bc, openings):
    joined = jnp.concatenate([inner_x, state_bc], axis=1)
    filters = jnp.concatenate([taps_x, taps_bc], axis=1)
    within = jnp.arange(joined.shape[0]) % BLK
    conv_total = filters[KC][None, :] + filters[KC - 1][None, :] * joined
    for offset in range(1, KC):
        shifted = jnp.concatenate(
            [jnp.zeros((offset, joined.shape[1]), jnp.float32), joined[:-offset]], axis=0
        )
        allowed = 1.0 - openings * (within < offset).astype(jnp.float32)
        conv_total = conv_total + filters[KC - 1 - offset][None, :] * shifted * allowed[:, None]
    active = jax.nn.silu(conv_total)
    split_at = inner_x.shape[1]
    return (active[:, :split_at], active[:, split_at:])


def state_mixer(signal_x, signal_bc, step_raw, gate_values, table, head_used, block_open):
    token_count, channels = signal_x.shape
    heads_here = table.shape[1]
    blocks_here = token_count // BLK
    step_rates = jax.nn.softplus(step_raw + table[0][None, :])
    log_rates = step_rates * (-jnp.exp(table[1]))[None, :]
    cumulated = jnp.cumsum(log_rates.reshape(blocks_here, BLK, heads_here), axis=1)
    rates_block = step_rates.reshape(blocks_here, BLK, heads_here)
    values = signal_x.reshape(blocks_here, BLK, heads_here, P_SIZE)
    inputs_map = signal_bc[:, :NS].reshape(blocks_here, BLK, NS)
    outputs_map = signal_bc[:, NS:].reshape(blocks_here, BLK, NS)
    lower_mask = (jnp.arange(BLK)[:, None] >= jnp.arange(BLK)[None, :])[None, :, :, None]
    spread = cumulated[:, :, None, :] - cumulated[:, None, :, :]
    decays = jnp.where(lower_mask, jnp.exp(jnp.where(lower_mask, spread, 0.0)), 0.0)
    intersection = jnp.einsum("nts,nus->ntu", outputs_map, inputs_map, precision=HIGHEST)
    mixing = intersection[..., None] * decays * rates_block[:, None, :, :]
    inner_part = jnp.einsum("ntuh,nuhp->nthp", mixing, values, precision=HIGHEST)
    ending = jnp.exp(cumulated[:, -1:, :] - cumulated) * rates_block
    pieces = jnp.einsum("nuh,nuhp,nus->nhps", ending, values, inputs_map, precision=HIGHEST)
    totals = jnp.exp(cumulated[:, -1, :])

    def carry_state(state_now, entries):
        piece_state, total_decay, opening = entries
        entering = state_now * (1.0 - opening)
        return (total_decay[:, None, None] * entering + piece_state, entering)

    initial = jnp.zeros((heads_here, P_SIZE, NS), jnp.float32)
    finals, entered = lax.scan(carry_state, initial, (pieces, totals, block_open))
    outer_part = jnp.exp(cumulated)[..., None] * jnp.einsum(
        "nhps,nts->nthp", entered, outputs_map, precision=HIGHEST
    )
    mixed = (inner_part + outer_part + table[2][None, None, :, None] * values) * head_used.reshape(
        blocks_here, BLK, heads_here
    )[..., None]
    gated = mixed.reshape(token_count, channels) * jax.nn.silu(gate_values)
    return (gated, jnp.sum(gated * gated, axis=1))


def gated_norm(gated, total_sq, gate_gain, norm_counts):
    norm_scale = lax.rsqrt(total_sq / norm_counts + EPS)
    return gated * norm_scale[:, None] * gate_gain[None, :]


def advance(weight, gradient, moment, average, rate):
    adjusted = gradient + DECAY * weight
    moment_next = MOMENTUM * moment + adjusted
    weight_next = weight - rate * (adjusted + MOMENTUM * moment_next)
    average_next = AVERAGE * average + (1.0 - AVERAGE) * weight_next
    return (weight_next, moment_next, average_next)


def body(
    inputs,
    cotangent,
    token_valid,
    block_opens,
    block_widths,
    weight_inner,
    weight_step,
    weight_output,
    weight_state,
    norm_gain,
    channel_table,
    head_table,
    state_filter,
    momentum_inner,
    momentum_step,
    momentum_output,
    momentum_state,
    momentum_gain,
    momentum_channel,
    momentum_head,
    momentum_filter,
    average_inner,
    average_step,
    average_output,
    average_state,
    average_gain,
    average_channel,
    average_head,
    average_filter,
):
    inner_full, step_full, output_full = (
        lax.all_gather(weight_inner.astype(jnp.bfloat16), "dp", axis=0, tiled=True),
        lax.all_gather(weight_step.astype(jnp.bfloat16), "dp", axis=0, tiled=True),
        lax.all_gather(weight_output.astype(jnp.bfloat16), "dp", axis=1, tiled=True),
    )
    state_full, gain_full, filter_full = (
        lax.all_gather(weight_state.astype(jnp.bfloat16), ("dp", "head"), axis=0, tiled=True),
        lax.all_gather(norm_gain.astype(jnp.bfloat16), ("dp", "head"), axis=0, tiled=True),
        lax.all_gather(state_filter.astype(jnp.bfloat16), ("dp", "head"), axis=0, tiled=True),
    )
    channel_used = rounded(channel_table)
    head_values = rounded(head_table)
    gathered = lax.all_gather(inputs, "head", axis=1, tiled=True)
    tokens_full = gathered.astype(jnp.float32)
    inverse = lax.rsqrt(jnp.mean(tokens_full * tokens_full, axis=1) + EPS)
    gain_float = gain_full.astype(jnp.float32)
    normed = (tokens_full * inverse[:, None] * gain_float[None, :]).astype(jnp.bfloat16)
    inner_pair = jnp.einsum("td,dkc->tkc", normed, inner_full, preferred_element_type=jnp.float32)
    gate_values = inner_pair[:, 0]
    inner_x = inner_pair[:, 1]
    state_bc = jnp.dot(normed, state_full, preferred_element_type=jnp.float32)
    step_raw = jnp.dot(normed, step_full, preferred_element_type=jnp.float32)
    block_open = block_opens.astype(jnp.float32)
    openings = jnp.repeat(block_open, BLK)
    widths = jnp.repeat(block_widths, BLK)
    heads_local = step_full.shape[1]
    head_used = (jnp.arange(heads_local)[None, :] * H < widths[:, None] * heads_local).astype(
        jnp.float32
    )
    norm_counts = widths.astype(jnp.float32) * P_SIZE
    valid_rows = token_valid.astype(jnp.float32)
    taps_x = channel_used[: KC + 1]
    gate_gain = channel_used[KC + 1]
    taps_bc = filter_full.astype(jnp.float32).T

    def conv_part(inner_value, state_value, taps_first, taps_second):
        return convolve(inner_value, state_value, taps_first, taps_second, openings)

    (conv_x, conv_bc), conv_back = jax.vjp(conv_part, inner_x, state_bc, taps_x, taps_bc)
    signal_x = rounded(conv_x)
    signal_bc = rounded(conv_bc)

    def mix_part(signal_first, signal_second, raw_steps, gate_part, table):
        return state_mixer(
            signal_first, signal_second, raw_steps, gate_part, table, head_used, block_open
        )

    (gated, local_sq), mix_back = jax.vjp(
        mix_part, signal_x, signal_bc, step_raw, gate_values, head_values
    )
    total_sq = lax.psum(local_sq, "head")

    def norm_part(gated_value, sum_value, gain_value):
        return gated_norm(gated_value, sum_value, gain_value, norm_counts)

    normalized, norm_back_fn = jax.vjp(norm_part, gated, total_sq, gate_gain)
    projected = normalized.astype(jnp.bfloat16)
    partial_out = jnp.dot(projected, output_full, preferred_element_type=jnp.float32)
    branch = lax.psum_scatter(
        partial_out.astype(jnp.bfloat16), "head", scatter_dimension=1, tiled=True
    ).astype(jnp.float32)
    own_inputs = inputs.astype(jnp.float32)
    layer_output = (own_inputs + valid_rows[:, None] * branch).astype(jnp.bfloat16)
    masked = cotangent * token_valid.astype(jnp.bfloat16)[:, None]
    shard_piece = lax.all_gather(masked, "head", axis=1, tiled=True)
    grad_normal = jnp.einsum(
        "tw,cw->tc", shard_piece, output_full, preferred_element_type=jnp.float32
    )
    block_grad = jnp.einsum("tc,tw->cw", projected, shard_piece, preferred_element_type=jnp.float32)
    grad_gated, grad_sq_part, grad_gate_gain = norm_back_fn(grad_normal)
    grad_sq = lax.psum(grad_sq_part, "head")
    grad_sx, grad_sbc, grad_raw, grad_gate, grad_head = mix_back((grad_gated, grad_sq))
    grad_inner_x, grad_state_bc, grad_taps_x, grad_taps_bc = conv_back((grad_sx, grad_sbc))
    pair_low = jnp.stack([grad_gate, grad_inner_x], axis=1).astype(jnp.bfloat16)
    state_low = grad_state_bc.astype(jnp.bfloat16)
    step_low = grad_raw.astype(jnp.bfloat16)
    grad_inner = jnp.einsum("td,tkc->dkc", normed, pair_low, preferred_element_type=jnp.float32)
    grad_state = jnp.einsum("td,ts->ds", normed, state_low, preferred_element_type=jnp.float32)
    grad_step = jnp.einsum("td,th->dh", normed, step_low, preferred_element_type=jnp.float32)
    grad_normed = jnp.einsum(
        "tkc,dkc->td", pair_low, inner_full, preferred_element_type=jnp.float32
    )
    grad_normed = grad_normed + jnp.einsum(
        "ts,ds->td", state_low, state_full, preferred_element_type=jnp.float32
    )
    grad_normed = grad_normed + jnp.einsum(
        "th,dh->td", step_low, step_full, preferred_element_type=jnp.float32
    )
    own_grad = lax.psum_scatter(
        grad_normed.astype(jnp.bfloat16), "head", scatter_dimension=1, tiled=True
    ).astype(jnp.float32)
    own_width = inputs.shape[1]
    start_column = lax.axis_index("head") * own_width
    own_gain = lax.dynamic_slice_in_dim(gain_float, start_column, own_width)
    scaled = own_grad * own_gain[None, :]
    row_part = jnp.sum(scaled * own_inputs, axis=1)
    grad_gain_own = jnp.sum(own_grad * own_inputs * inverse[:, None], axis=0)
    row_total = lax.psum(row_part, "head")
    inverse_cube = inverse * inverse * inverse
    grad_input = (
        cotangent.astype(jnp.float32)
        + inverse[:, None] * scaled
        - own_inputs * (inverse_cube * row_total / D)[:, None]
    )
    grad_gain_full = lax.dynamic_update_slice_in_dim(
        jnp.zeros((D,), jnp.float32), grad_gain_own, start_column, 0
    )
    grad_channel = jnp.concatenate([grad_taps_x, grad_gate_gain[None, :]], axis=0)
    grad_filter = grad_taps_bc.T
    inner_reduced, step_reduced, output_reduced = (
        lax.psum_scatter(grad_inner, "dp", scatter_dimension=0, tiled=True),
        lax.psum_scatter(grad_step, "dp", scatter_dimension=0, tiled=True),
        lax.psum_scatter(block_grad, "dp", scatter_dimension=1, tiled=True),
    )
    state_reduced, gain_reduced, filter_reduced = (
        lax.psum_scatter(grad_state, ("dp", "head"), scatter_dimension=0, tiled=True),
        lax.psum_scatter(grad_gain_full, ("dp", "head"), scatter_dimension=0, tiled=True),
        lax.psum_scatter(grad_filter, ("dp", "head"), scatter_dimension=0, tiled=True),
    )
    channel_reduced, head_reduced = lax.psum((grad_channel, grad_head), "dp")
    total_tokens = inputs.shape[0] * lax.axis_size("dp")
    matrix_rate = RATE_MATRIX / math.sqrt(total_tokens)
    vector_rate = RATE_VECTOR / math.sqrt(total_tokens)
    new_inner = advance(weight_inner, inner_reduced, momentum_inner, average_inner, matrix_rate)
    new_step = advance(weight_step, step_reduced, momentum_step, average_step, matrix_rate)
    new_output = advance(
        weight_output, output_reduced, momentum_output, average_output, matrix_rate
    )
    new_state = advance(weight_state, state_reduced, momentum_state, average_state, matrix_rate)
    new_gain = advance(norm_gain, gain_reduced, momentum_gain, average_gain, vector_rate)
    new_channel = advance(
        channel_table, channel_reduced, momentum_channel, average_channel, vector_rate
    )
    new_head = advance(head_table, head_reduced, momentum_head, average_head, vector_rate)
    new_filter = advance(state_filter, filter_reduced, momentum_filter, average_filter, vector_rate)
    return (
        layer_output,
        grad_input,
        new_inner[0],
        new_inner[1],
        new_inner[2],
        new_step[0],
        new_step[1],
        new_step[2],
        new_output[0],
        new_output[1],
        new_output[2],
        new_state[0],
        new_state[1],
        new_state[2],
        new_gain[0],
        new_gain[1],
        new_gain[2],
        new_channel[0],
        new_channel[1],
        new_channel[2],
        new_head[0],
        new_head[1],
        new_head[2],
        new_filter[0],
        new_filter[1],
        new_filter[2],
    )


def solution(mesh):
    in_specs = (
        P("dp", "head"),
        P("dp", "head"),
        P("dp"),
        P("dp"),
        P("dp"),
        P("dp", None, "head"),
        P("dp", "head"),
        P("head", "dp"),
        P(("dp", "head"), None),
        P(("dp", "head")),
        P(None, "head"),
        P(None, "head"),
        P(("dp", "head"), None),
        P("dp", None, "head"),
        P("dp", "head"),
        P("head", "dp"),
        P(("dp", "head"), None),
        P(("dp", "head")),
        P(None, "head"),
        P(None, "head"),
        P(("dp", "head"), None),
        P("dp", None, "head"),
        P("dp", "head"),
        P("head", "dp"),
        P(("dp", "head"), None),
        P(("dp", "head")),
        P(None, "head"),
        P(None, "head"),
        P(("dp", "head"), None),
    )
    out_specs = (
        P("dp", "head"),
        P("dp", "head"),
        P("dp", None, "head"),
        P("dp", None, "head"),
        P("dp", None, "head"),
        P("dp", "head"),
        P("dp", "head"),
        P("dp", "head"),
        P("head", "dp"),
        P("head", "dp"),
        P("head", "dp"),
        P(("dp", "head"), None),
        P(("dp", "head"), None),
        P(("dp", "head"), None),
        P(("dp", "head")),
        P(("dp", "head")),
        P(("dp", "head")),
        P(None, "head"),
        P(None, "head"),
        P(None, "head"),
        P(None, "head"),
        P(None, "head"),
        P(None, "head"),
        P(("dp", "head"), None),
        P(("dp", "head"), None),
        P(("dp", "head"), None),
    )
    return jax.shard_map(body, mesh=mesh, in_specs=in_specs, out_specs=out_specs, check_vma=False)
```

profile of v0, /device:TPU:0, one launch (start us, length us, event | category | flops | bytes accessed | tf_op | source)
XLA Modules:
  0.0 1317.7 jit_solution(10096558258720219206)
XLA Ops:
  9.6 3.1 copy.409
  16.7 42.3 %all-reduce.20 = bf16[2048]{0:T(1024)(128)(2,1)S(1)} all-reduce(bf16[2048]{0:T(1024)(128)(2,1)S(1)} %dynamic-update-slice), channel_id=1, replica_groups=mesh['dp'=8,'head'=4] {'dp','head'}, use_global_device_ids=true, to_apply=%add.20 | all-reduce | flops 2048 | bytes 8192
  59.1 40.5 %all_gather.24 = bf16[256,5]{1,0:T(8,128)(2,1)S(1)} all-gather(bf16[8,5]{1,0:T(8,128)(2,1)S(1)} %convert_element_type.103), channel_id=1, replica_groups=mesh['dp'=8,'head'=4] {'dp','head'}, dimensions={0}, use_global_device_ids=true | all-gather | bytes 2640 | tf_op jit(solution)/shard_map/all_gather | solution.py:135
  100.0 4.6 mul.844.clone
  104.6 7.7 reshape.331
  112.9 30.9 %all_gather.29 = bf16[2048,16]{0,1:T(8,128)(2,1)S(1)} all-gather(bf16[256,16]{0,1:T(8,128)(2,1)S(1)} %convert_element_type.111), channel_id=1, replica_groups=mesh['dp'=8,'head'=4] {'dp'}, dimensions={0}, use_global_device_ids=true | all-gather | bytes 73728 | tf_op jit(solution)/shard_map/all_gather | solution.py:129
  144.0 3.2 fusion.15
  157.6 4.7 fusion.137
  162.3 69.6 %all-gather.8.cloned.1.call-done = bf16[2048,2,1024]{2,0,1:T(8,128)(2,1)} async-done(((bf16[256,2,1024]{2,0,1:T(8,128)(2,1)}), bf16[2048,2,1024]{2,0,1:T(8,128)(2,1)}) %all-gather.8.cloned.1.call-update) | async-done | bytes 8388624 | tf_op jit(solution)/shard_map/all_gather | solution.py:128
  231.9 12.5 fusion.50
  244.4 3.7 fusion.134
  250.2 3.2 fusion.32
  256.1 8.3 multiply_convert_fusion
  265.5 4.7 reshape.328
  272.7 7.4 reshape.335
  280.1 7.7 copy.278
  287.9 7.7 copy.273
  295.6 3.5 reshape.292
  302.5 4.4 fusion.53
  307.2 23.2 %while.36 = (s32[]{:T(128)}, f32[16,64,128]{2,1,0:T(8,128)S(1)}, f32[4,16,64,128]{3,2,1,0:T(8,128)S(1)}, f32[4]{0:T(128)}, f32[4,16,1,1]{1,3,2,0:T(1,128)}, /*in...) while((s32[]{:T(128)}, f32[16,64,128]{2,1,0:T(8,128)S(1)}, ...), condition=%wide.region_4.5_spmd.clone, body=%wide.region_3.4_spmd.clone.sunk | while | flops 786436 | bytes 2622828 | solution.py:72
  330.4 3.0 fusion.139
  333.4 18.0 %multiply_reduce_fusion.10 = (f32[4,256]{1,0:T(4,128)S(1)}, f32[4,256,16,64]{1,3,2,0:T(8,128)}) fusion(f32[4,256,16,64]{1,3,2,0:T(8,128)S(1)} %copy-done.25, f32[4,256,16]{1,2,0:T(8,128)S(1)} %compare_convert_fusion, f32[4,256,16,64]{1,3,2,0:T(8,128)} %copy.273, f32[16]{0:T(128)S(1)} %copy-done.99, f32[4,256,16,64]{1,3,2,0:T(8,128)S(1)} %fusion.139, ...), kind=kOutput, calls=%fused_computation.102 | convolution fusion | flops 3254778880 | bytes 20254784 | tf_op jit(solution)/shard_map/jvp(ntuh,nuhp->nthp)/dot_general | solution.py:61
  351.4 8.2 copy.333
  359.6 7.6 reshape.334
  367.2 6.3 psum.35
  373.6 14.9 %multiply_reduce_fusion.7 = (f32[1024]{0:T(1024)}, f32[1024]{0:T(1024)S(1)}, f32[1024,1024]{1,0:T(8,128)}, f32[1024,1024]{1,0:T(8,128)}) fusion(f32[1024]{0:T(1024)S(1)} %fusion.121, f32[1024]{0:T(1024)S(1)} %bitcast.298, f32[1024,1024]{1,0:T(8,128)} %reshape.334, f32[1024,2,1024]{2,0,1:T(8,128)} %copy-done.11, ...), kind=kOutput, calls=%fused_computation.98 | convolution fusion | flops 4306499584 | bytes 25182208 | tf_op jit(solution)/shard_map/tw,cw->tc/dot_general | solution.py:192
  388.5 6.1 psum.36
  394.6 12.6 multiply_reduce_fusion.6
  407.2 7.2 reshape.329
  414.4 7.7 copy.281
  422.2 5.7 fusion.54
  429.5 16.6 %while.37 = (s32[]{:T(128)}, f32[16,64,128]{2,1,0:T(8,128)S(1)}, f32[4,16,64,128]{3,2,1,0:T(8,128)}, f32[4,16]{1,0:T(4,128)S(1)}, f32[4,16,64,128]{3,2,1,0:T(8,1...) while((s32[]{:T(128)}, f32[16,64,128]{2,1,0:T(8,128)S(1)}, ...), condition=%wide.region_13.14_spmd.clone, body=%wide.region_11.13_spmd.clone.sunk | while | flops 917492 | bytes 3146284 | solution.py:72
  446.1 3.6 fusion.140
  449.7 7.6 fusion.92
  457.3 22.4 %fusion.14 = (f32[4,256,16]{1,2,0:T(8,128)}, f32[4,256,16]{1,2,0:T(8,128)}, f32[4,256,16]{1,2,0:T(8,128)}, f32[4,256,256]{2,1,0:T(8,128)}) fusion(f32[4,256,16]{1,2,0:T(8,128)S(1)} %bitcast.307, f32[4,256,16]{1,2,0:T(8,128)S(1)} %copy-done.44, f32[4,256,256]{2,1,0:T(8,128)S(1)} %copy-done.37, pred[256,256]{1,0:T(8,128)(4,1)S(1)} %copy-done.68, ...), kind=kOutput, calls=%fused_computation.33 | convolution fusion | flops 3284877312 | bytes 8847360 | tf_op jit(solution)/shard_map/transpose(jvp(ntuh,nuhp->nthp))/dot_general | solution.py:61
  479.7 7.6 fusion.93
  487.3 16.8 %bitcast_add_fusion.3 = f32[4,256,16,64]{1,3,2,0:T(8,128)} fusion(f32[4,256,16,64]{1,3,2,0:T(8,128)S(1)} %fusion.140, f32[4,256,16,64]{1,3,2,0:T(8,128)S(1)} %copy-done.1, f32[4,256,16]{1,2,0:T(8,128)S(1)} %bitcast.308, f32[4,256,16]{1,2,0:T(8,128)S(1)} %copy-done.44, f32[4,256,256]{2,1,0:T(8,128)S(1)} %copy-done.37, pred[256,256]{1,0:T(8,128)(4,1)S(1)} %copy-done.68, ...), kind=kOutput, calls=%fused_computation.79 | convolution fusion | flops 3248488448 | bytes 13959232 | tf_op jit(solution)/shard_map/transpose(jvp(ntuh,nuhp->nthp))/dot_general | solution.py:61
  504.1 3.7 multiply_reduce_fusion.5
  509.2 8.1 copy.328
  517.3 7.6 reshape.330
  531.4 6.2 multiply_reduce_fusion.4
  537.6 5.8 multiply_reduce_fusion.3
  543.5 5.4 slice_multiply_fusion
  555.3 9.9 reduce-window.16
  565.7 3.5 fusion.105
  569.3 9.8 multiply_reduce_fusion.1
  588.1 11.5 fusion.66
  599.6 3.4 fusion.19
  603.1 10.1 convolution_convert_fusion
  613.2 11.4 fusion.128
  624.7 15.2 %fusion.48 = f32[2048,2,1024]{2,0,1:T(8,128)} fusion(bf16[1024,2048]{1,0:T(8,128)(2,1)} %copy-done.5, bf16[1024,1,1024]{2,0,1:T(8,128)(2,1)} %copy-done.33, bf16[1024,1,1024]{2,0,1:T(8,128)(2,1)S(1)} %copy-done.32), kind=kOutput, calls=%fused_computation.92 | convolution fusion | flops 8598323200 | bytes 25165824 | tf_op jit(solution)/shard_map/td,tkc->dkc/dot_general | solution.py:203
  642.0 35.3 %all-reduce.24 = (f32[6,1024]{1,0:T(8,128)S(1)}, f32[3,16]{1,0:T(4,128)S(1)}) all-reduce(f32[6,1024]{1,0:T(8,128)S(1)} %pad_maximum_fusion.4, f32[3,16]{1,0:T(4,128)S(1)} %pad_add_fusion.2), channel_id=1, replica_groups=mesh['dp'=8,'head'=4] {'dp'}, use_global_device_ids=true, to_apply=%region_36.37 | all-reduce | flops 6192 | bytes 49536 | tf_op jit(solution)/shard_map/psum | solution.py:246
  679.9 87.6 %reduce-scatter.18.cloned.1.call-done = f32[64,256]{1,0:T(8,128)} async-done(((f32[2048,256]{1,0:T(8,128)}), f32[64,256]{1,0:T(8,128)}) %reduce-scatter.18.cloned.1.call-update) | async-done | bytes 65552 | tf_op jit(solution)/shard_map/reduce_scatter | solution.py:242
  769.0 41.6 %reduce-scatter.10.cloned.1.call-done = bf16[1024,512]{1,0:T(8,128)(2,1)} async-done(((bf16[1024,2048]{1,0:T(8,128)(2,1)}), bf16[1024,512]{1,0:T(8,128)(2,1)}) %reduce-scatter.10.cloned.1.call-update) | async-done | bytes 1048592 | tf_op jit(solution)/shard_map/reduce_scatter | solution.py:215
  813.1 39.7 %all-reduce.23 = (f32[2048]{0:T(1024)S(1)}, f32[256,5]{0,1:T(8,128)S(1)}) all-reduce(f32[2048]{0:T(1024)S(1)} %dynamic_update_slice.34, f32[256,5]{0,1:T(8,128)S(1)} %add_bitcast_fusion.4), channel_id=8, replica_groups=mesh['dp'=8,'head'=4] {'dp','head'}, use_global_device_ids=true, to_apply=%region_29.30.clone | all-reduce | flops 3328 | bytes 26624
  854.9 6.5 psum.37
  862.1 3.6 fusion.71
  865.8 146.0 %reduce-scatter.16.cloned.1.call-done = f32[1024,256]{1,0:T(8,128)} async-done(((f32[1024,2048]{1,0:T(8,128)}), f32[1024,256]{1,0:T(8,128)}) %reduce-scatter.16.cloned.1.call-update) | async-done | bytes 1048592 | tf_op jit(solution)/shard_map/reduce_scatter | solution.py:239
  1011.8 3.9 multiply_add_fusion.2
  1015.6 280.9 %reduce-scatter.12.cloned.1.call-done = f32[256,2,1024]{2,0,1:T(8,128)} async-done(((f32[2048,2,1024]{2,0,1:T(8,128)}), f32[256,2,1024]{2,0,1:T(8,128)}) %reduce-scatter.12.cloned.1.call-update) | async-done | bytes 2097168 | tf_op jit(solution)/shard_map/reduce_scatter | solution.py:237
  1296.5 5.4 fusion.76
  1301.9 2.9 copy.306
  1304.9 2.9 copy.307
  1307.8 2.9 copy.308
  (408 shorter events, 105.3 us)
Async XLA Ops:
  7.2 7.5 copy-start.26
  7.2 136.8 %all-gather.6.cloned.1.call-start = ((), (), s32[]{:S(2)}) async-start(), calls=%async_computation.6 | async-start | bytes 5242880 | tf_op jit(solution)/shard_map/all_gather | solution.py:139
  8.0 149.6 %all-gather.10.cloned.1.call-start = ((), (), s32[]{:S(2)}) async-start(), calls=%async_computation.8 | async-start | bytes 1081344 | tf_op jit(solution)/shard_map/all_gather | solution.py:133
  9.5 6.8 copy-start.104
  9.5 6.8 copy-start.45
  9.5 6.8 copy-start.100
  9.5 49.4 %copy-start.105 = (s32[4]{0:T(128)S(1)}, s32[4]{0:T(128)}, u32[]{:S(2)}) copy-start(s32[4]{0:T(128)} %param.36) | copy-start | bytes 52
  9.6 49.5 %copy-start.86 = (f32[8,5]{1,0:T(8,128)S(1)}, f32[8,5]{1,0:T(8,128)}, u32[]{:S(2)}) copy-start(f32[8,5]{1,0:T(8,128)} %param.45) | copy-start | bytes 484
  9.6 222.4 %all-gather.8.cloned.1.call-start = ((), (), s32[]{:S(2)}) async-start(), calls=%async_computation.7 | async-start | bytes 9437184 | tf_op jit(solution)/shard_map/all_gather | solution.py:128
  12.8 360.8 %all-gather.14.cloned.1.call-start = ((), (), s32[]{:S(2)}) async-start(), calls=%async_computation.11 | async-start | bytes 5242880 | tf_op jit(solution)/shard_map/all_gather | solution.py:191
  14.6 359.0 %all-gather.12.cloned.1.call-start = ((), (), s32[]{:S(2)}) async-start(), calls=%async_computation.9 | async-start | bytes 4718592 | tf_op jit(solution)/shard_map/all_gather | solution.py:130
  15.6 663.0 %reduce-scatter.14.cloned.1.call-start = ((), (), s32[]{:S(2)}) async-start(), calls=%async_computation.14 | async-start | bytes 147456 | tf_op jit(solution)/shard_map/reduce_scatter | solution.py:238
  59.0 40.7 %copy-start.78 = (bf16[2048]{0:T(1024)(128)(2,1)}, bf16[2048]{0:T(1024)(128)(2,1)S(1)}, u32[]{:S(2)}) copy-start(bf16[2048]{0:T(1024)(128)(2,1)S(1)} %all-reduce.20) | copy-start | bytes 12292
  59.0 40.7 %copy-start.80 = (f32[4]{0:T(128)}, f32[4]{0:T(128)S(1)}, u32[]{:S(2)}) copy-start(f32[4]{0:T(128)S(1)} %convert_element_type.110) | copy-start | bytes 52
  59.1 194.3 %copy-start.72 = (f32[1024]{0:T(1024)}, f32[1024]{0:T(1024)S(1)}, u32[]{:S(2)}) copy-start(f32[1024]{0:T(1024)S(1)} %get-tuple-element.532) | copy-start | bytes 12292
  59.1 194.3 %copy-start.74 = (f32[1024]{0:T(1024)}, f32[1024]{0:T(1024)S(1)}, u32[]{:S(2)}) copy-start(f32[1024]{0:T(1024)S(1)} %get-tuple-element.534) | copy-start | bytes 12292
  104.6 7.7 copy-start.90
  104.6 8.2 copy-start.66
  112.8 35.7 %copy-start.88 = (f32[16]{0:T(128)}, f32[16]{0:T(128)S(1)}, u32[]{:S(2)}) copy-start(f32[16]{0:T(128)S(1)} %get-tuple-element.536) | copy-start | bytes 196
  143.9 109.5 %copy-start.51 = (f32[1280]{0:T(1024)}, f32[1280]{0:T(1024)S(1)}, u32[]{:S(2)}) copy-start(f32[1280]{0:T(1024)S(1)} %get-tuple-element.434) | copy-start | bytes 15364
  143.9 109.5 %copy-start.53 = (f32[1280]{0:T(1024)}, f32[1280]{0:T(1024)S(1)}, u32[]{:S(2)}) copy-start(f32[1280]{0:T(1024)S(1)} %get-tuple-element.431) | copy-start | bytes 15364
  143.9 109.5 %copy-start.55 = (f32[1280]{0:T(1024)}, f32[1280]{0:T(1024)S(1)}, u32[]{:S(2)}) copy-start(f32[1280]{0:T(1024)S(1)} %get-tuple-element.432) | copy-start | bytes 15364
  144.0 109.5 %copy-start.57 = (f32[1280]{0:T(1024)}, f32[1280]{0:T(1024)S(1)}, u32[]{:S(2)}) copy-start(f32[1280]{0:T(1024)S(1)} %get-tuple-element.433) | copy-start | bytes 15364
  162.3 91.1 %copy-start.8 = (f32[1024,256]{1,0:T(8,128)}, f32[1024,256]{1,0:T(8,128)S(1)}, u32[]{:S(2)}) copy-start(f32[1024,256]{1,0:T(8,128)S(1)} %fusion.137) | copy-start | bytes 3145732
  333.3 18.1 %copy-start.16 = (f32[4,256,16,64]{1,3,2,0:T(8,128)}, f32[4,256,16,64]{1,3,2,0:T(8,128)S(1)}, u32[]{:S(2)}) copy-start(f32[4,256,16,64]{1,3,2,0:T(8,128)S(1)} %fusion.139) | copy-start | bytes 12582916
  414.4 7.7 copy-start.24
  422.2 7.3 copy-start.106
  449.7 7.6 copy-start.1
  449.7 7.6 copy-start.37
  524.9 12.6 slice-start
  524.9 12.7 slice-start.2
  551.8 13.7 %copy-start.40 = (f32[1024,16]{0,1:T(8,128)S(1)}, f32[1024,16]{0,1:T(8,128)}, u32[]{:S(2)}) copy-start(f32[1024,16]{0,1:T(8,128)} %get-tuple-element.538) | copy-start | bytes 196612
  551.8 13.7 %copy-start.89 = (f32[16]{0:T(128)S(1)}, f32[16]{0:T(128)}, u32[]{:S(2)}) copy-start(f32[16]{0:T(128)} %copy-done.88) | copy-start | bytes 196
  554.7 14.6 %copy-start.9 = (f32[1024,256]{1,0:T(8,128)S(1)}, f32[1024,256]{1,0:T(8,128)}, u32[]{:S(2)}) copy-start(f32[1024,256]{1,0:T(8,128)} %copy-done.8) | copy-start | bytes 3145732
  554.7 14.6 %copy-start.58 = (f32[1280]{0:T(1024)S(1)}, f32[1280]{0:T(1024)}, u32[]{:S(2)}) copy-start(f32[1280]{0:T(1024)} %copy-done.57) | copy-start | bytes 15364
  569.2 198.3 %reduce-scatter.18.cloned.1.call-start = ((), (), s32[]{:S(2)}) async-start(), calls=%async_computation.16 | async-start | bytes 2162688 | tf_op jit(solution)/shard_map/reduce_scatter | solution.py:242
  569.3 11.3 copy-start.6
  583.3 227.3 %reduce-scatter.10.cloned.1.call-start = ((), (), s32[]{:S(2)}) async-start(), calls=%async_computation.12 | async-start | bytes 5242880 | tf_op jit(solution)/shard_map/reduce_scatter | solution.py:215
  588.1 11.5 copy-start.39
  603.0 259.1 %reduce-scatter.8.cloned.1.call-start = ((), (), s32[]{:S(2)}) async-start(), calls=%async_computation.10 | async-start | bytes 5242880 | tf_op jit(solution)/shard_map/reduce_scatter | solution.py:185
  613.2 398.6 %reduce-scatter.16.cloned.1.call-start = ((), (), s32[]{:S(2)}) async-start(), calls=%async_computation.15 | async-start | bytes 9437184 | tf_op jit(solution)/shard_map/reduce_scatter | solution.py:239
  624.7 671.8 %reduce-scatter.12.cloned.1.call-start = ((), (), s32[]{:S(2)}) async-start(), calls=%async_computation.13 | async-start | bytes 18874368 | tf_op jit(solution)/shard_map/reduce_scatter | solution.py:237
  640.0 37.3 %copy-start.91 = (f32[3,16]{1,0:T(4,128)S(1)}, f32[3,16]{1,0:T(4,128)}, u32[]{:S(2)}) copy-start(f32[3,16]{1,0:T(4,128)} %param.44) | copy-start | bytes 580
  640.0 37.3 %copy-start.97 = (f32[3,16]{1,0:T(4,128)S(1)}, f32[3,16]{1,0:T(4,128)}, u32[]{:S(2)}) copy-start(f32[3,16]{1,0:T(4,128)} %param.60) | copy-start | bytes 580
  640.0 37.3 %copy-start.98 = (f32[3,16]{1,0:T(4,128)S(1)}, f32[3,16]{1,0:T(4,128)}, u32[]{:S(2)}) copy-start(f32[3,16]{1,0:T(4,128)} %param.52) | copy-start | bytes 580
  640.0 37.9 %copy-start.46 = (f32[6,1024]{1,0:T(8,128)S(1)}, f32[6,1024]{1,0:T(8,128)}, u32[]{:S(2)}) copy-start(f32[6,1024]{1,0:T(8,128)} %param.43) | copy-start | bytes 73732
  640.0 37.8 %copy-start.76 = (f32[6,1024]{1,0:T(8,128)S(1)}, f32[6,1024]{1,0:T(8,128)}, u32[]{:S(2)}) copy-start(f32[6,1024]{1,0:T(8,128)} %param.59) | copy-start | bytes 73732
  640.0 37.8 %copy-start.77 = (f32[6,1024]{1,0:T(8,128)S(1)}, f32[6,1024]{1,0:T(8,128)}, u32[]{:S(2)}) copy-start(f32[6,1024]{1,0:T(8,128)} %param.51) | copy-start | bytes 73732
  640.0 38.5 %copy-start.67 = (f32[256,16]{0,1:T(8,128)S(1)}, f32[256,16]{0,1:T(8,128)}, u32[]{:S(2)}) copy-start(f32[256,16]{0,1:T(8,128)} %param.39) | copy-start | bytes 49156
  640.0 38.5 %copy-start.84 = (f32[256,16]{0,1:T(8,128)S(1)}, f32[256,16]{0,1:T(8,128)}, u32[]{:S(2)}) copy-start(f32[256,16]{0,1:T(8,128)} %param.55) | copy-start | bytes 49156
  640.1 38.5 %copy-start.85 = (f32[256,16]{0,1:T(8,128)S(1)}, f32[256,16]{0,1:T(8,128)}, u32[]{:S(2)}) copy-start(f32[256,16]{0,1:T(8,128)} %param.47) | copy-start | bytes 49156
  640.1 127.4 %copy-start.42 = (f32[64,256]{1,0:T(8,128)S(1)}, f32[64,256]{1,0:T(8,128)}, u32[]{:S(2)}) copy-start(f32[64,256]{1,0:T(8,128)} %param.41) | copy-start | bytes 196612
  640.1 127.4 %copy-start.61 = (f32[64,256]{1,0:T(8,128)S(1)}, f32[64,256]{1,0:T(8,128)}, u32[]{:S(2)}) copy-start(f32[64,256]{1,0:T(8,128)} %param.57) | copy-start | bytes 196612
  640.1 127.4 %copy-start.62 = (f32[64,256]{1,0:T(8,128)S(1)}, f32[64,256]{1,0:T(8,128)}, u32[]{:S(2)}) copy-start(f32[64,256]{1,0:T(8,128)} %param.49) | copy-start | bytes 196612
  640.1 170.5 %copy-start.20 = (bf16[1024,512]{1,0:T(8,128)(2,1)S(1)}, bf16[1024,512]{1,0:T(8,128)(2,1)}, u32[]{:S(2)}) copy-start(bf16[1024,512]{1,0:T(8,128)(2,1)} %param.33) | copy-start | bytes 3145732
  640.1 170.5 %copy-start.60 = (f32[1024]{0:T(1024)S(1)}, f32[1024]{0:T(1024)}, u32[]{:S(2)}) copy-start(f32[1024]{0:T(1024)} %copy-done.59) | copy-start | bytes 12292
  640.1 221.3 %copy-start.101 = (f32[64]{0:T(128)S(1)}, f32[64]{0:T(128)}, u32[]{:S(2)}) copy-start(f32[64]{0:T(128)} %param.42) | copy-start | bytes 772
  640.1 221.3 %copy-start.102 = (f32[64]{0:T(128)S(1)}, f32[64]{0:T(128)}, u32[]{:S(2)}) copy-start(f32[64]{0:T(128)} %param.58) | copy-start | bytes 772
  640.2 221.3 %copy-start.103 = (f32[64]{0:T(128)S(1)}, f32[64]{0:T(128)}, u32[]{:S(2)}) copy-start(f32[64]{0:T(128)} %param.50) | copy-start | bytes 772
  640.2 221.9 %copy-start.71 = (f32[1024]{0:T(1024)S(1)}, f32[1024]{0:T(1024)}, u32[]{:S(2)}) copy-start(f32[1024]{0:T(1024)} %copy-done.70) | copy-start | bytes 12292
  640.2 221.9 %copy-start.83 = (f32[1024]{0:T(1024)S(1)}, f32[1024]{0:T(1024)}, u32[]{:S(2)}) copy-start(f32[1024]{0:T(1024)} %get-tuple-element.530) | copy-start | bytes 12292
  640.2 221.9 %copy-start.29 = (bf16[1024,512]{1,0:T(8,128)(2,1)S(1)}, bf16[1024,512]{1,0:T(8,128)(2,1)}, u32[]{:S(2)}) copy-start(bf16[1024,512]{1,0:T(8,128)(2,1)} %param.34) | copy-start | bytes 3145732
  812.8 199.0 %copy-start.27 = (f32[1024,256]{1,0:T(8,128)S(1)}, f32[1024,256]{1,0:T(8,128)}, u32[]{:S(2)}) copy-start(f32[1024,256]{1,0:T(8,128)} %param.40) | copy-start | bytes 3145732
  865.7 430.8 %copy-start.21 = (f32[256,2,1024]{2,1,0:T(2,128)S(1)}, f32[256,2,1024]{2,1,0:T(2,128)}, u32[]{:S(2)}) copy-start(f32[256,2,1024]{2,1,0:T(2,128)} %param.38) | copy-start | bytes 6291460
  (58 other events, 199.5 us)
Sparse Core Ops, SparseCore 0:
  9.6 37.8 all-gather.5
  51.0 53.7 all-gather.9
  107.6 124.3 all-gather.7
  233.9 32.6 all-gather.13
  269.1 75.0 all-gather.11
  569.3 59.1 reduce-scatter.13
  631.4 136.0 reduce-scatter.17
  770.2 40.3 reduce-scatter.9
  813.1 45.2 reduce-scatter.7
  862.3 149.4 reduce-scatter.15
  1015.6 280.9 reduce-scatter.11
where the time goes:
time: 1330 us; the launch traced here: 1320 us
  waiting for transfers between devices  627 us (47%)
  blocking collectives  208 us (16%)
  matrix products  190 us (14%)
  local copies, waits for them, and re-layouts  141 us (11%)
  other arithmetic  135 us (10%)
  between operations  16 us (1%)
    reduce_scatter x1, waiting for transfers between devices, body(): lax.psum_scatter(grad_inner, 'dp', scatter_dimension=0, tiled=True)  281 us
    reduce_scatter x1, waiting for transfers between devices, body(): lax.psum_scatter(block_grad, 'dp', scatter_dimension=1, tiled=True)  146 us
    reduce_scatter x1, waiting for transfers between devices, body(): lax.psum_scatter(grad_state, ('dp', 'head'), scatter_dimension=0, tiled=T...  87.6 us
    unnamed x2, blocking collectives  82 us
    all_gather x1, waiting for transfers between devices, body(): lax.all_gather(weight_inner.astype(jnp.bfloat16), 'dp', axis=0, tiled=True)  69.6 us
    dot_general x3, matrix products, state_mixer(): jnp.einsum('ntuh,nuhp->nthp', mixing, values, precision=HIGHEST)  57.2 us
    reduce_scatter x1, waiting for transfers between devices, body(): lax.psum_scatter(grad_normed.astype(jnp.bfloat16), 'head', scatter_dimens...  41.6 us
    all_gather x1, blocking collectives, body(): lax.all_gather(state_filter.astype(jnp.bfloat16), ('dp', 'head'), axis=0,...  40.5 us
  transfers between devices with their start and end apart: 11, of which 5 were waited for; matrix products, arithmetic and copies ran while one was open for 19% of the time, Pallas kernels for 0%

commit v1 on v0

--- a/solution.py
+++ b/solution.py
@@ -91,6 +91,97 @@
     weight_next = weight - rate * (adjusted + MOMENTUM * moment_next)
     average_next = AVERAGE * average + (1.0 - AVERAGE) * weight_next
     return (weight_next, moment_next, average_next)
+
+
+Y_SIZE = 2
+
+
+def swap_pairs(size):
+    return [(i, i ^ 1) for i in range(size)]
+
+
+def gather_dp(shard, axis):
+    count = lax.axis_size("dp")
+    if count != 8:
+        return lax.all_gather(shard, "dp", axis=axis, tiled=True)
+    rows = count // Y_SIZE
+    index = lax.axis_index("dp")
+    row, column = index // Y_SIZE, index % Y_SIZE
+    width = shard.shape[axis]
+    held = {0: shard}
+    for shift in range(1, rows):
+        perm = [(i, (i + shift * Y_SIZE) % count) for i in range(count)]
+        held[shift] = lax.ppermute(shard, "dp", perm)
+    shape = list(shard.shape)
+    shape[axis] = width * count
+    full = jnp.zeros(shape, shard.dtype)
+    for shift in range(rows):
+        other = lax.ppermute(held[shift], "dp", swap_pairs(count))
+        base = ((row - shift) % rows) * Y_SIZE
+        full = lax.dynamic_update_slice_in_dim(full, held[shift], (base + column) * width, axis)
+        full = lax.dynamic_update_slice_in_dim(full, other, (base + 1 - column) * width, axis)
+    return full
+
+
+def reduce_dp(value, axis):
+    count = lax.axis_size("dp")
+    low = jnp.bfloat16
+    if count != 8:
+        return lax.psum_scatter(
+            value.astype(low), "dp", scatter_dimension=axis, tiled=True
+        ).astype(jnp.float32)
+    rows = count // Y_SIZE
+    index = lax.axis_index("dp")
+    row, column = index // Y_SIZE, index % Y_SIZE
+    width = value.shape[axis] // count
+    total = None
+    for shift in (1, 2, 3, 0):
+        base = ((row + shift) % rows) * Y_SIZE
+        away = lax.dynamic_slice_in_dim(value, (base + 1 - column) * width, width, axis)
+        kept = lax.dynamic_slice_in_dim(value, (base + column) * width, width, axis)
+        came = lax.ppermute(away.astype(low), "dp", swap_pairs(count))
+        pair = kept + came.astype(jnp.float32)
+        if shift:
+            perm = [(i, (i + shift * Y_SIZE) % count) for i in range(count)]
+            pair = lax.ppermute(pair.astype(low), "dp", perm).astype(jnp.float32)
+        total = pair if total is None else total + pair
+    return total
+
+
+def reduce_head(value):
+    count = lax.axis_size("head")
+    low = jnp.bfloat16
+    if count != 4:
+        return lax.psum_scatter(value, "head", scatter_dimension=0, tiled=False)
+    index = lax.axis_index("head")
+    side, core = index // 2, index % 2
+    both = value.reshape(2, 2, *value.shape[1:])
+    away = lax.dynamic_index_in_dim(both, 1 - core, 1, keepdims=False)
+    kept = lax.dynamic_index_in_dim(both, core, 1, keepdims=False)
+    came = lax.ppermute(away.astype(low), "head", swap_pairs(count))
+    pair = kept + came.astype(jnp.float32)
+    away = lax.dynamic_index_in_dim(pair, 1 - side, 0, keepdims=False)
+    kept = lax.dynamic_index_in_dim(pair, side, 0, keepdims=False)
+    came = lax.ppermute(away.astype(low), "head", [(i, (i + 2) % 4) for i in range(count)])
+    return kept + came.astype(jnp.float32)
+
+
+def gather_head(piece, axis):
+    count = lax.axis_size("head")
+    if count != 4:
+        return lax.all_gather(piece, "head", axis=axis, tiled=True)
+    index = lax.axis_index("head")
+    width = piece.shape[axis]
+    near = lax.ppermute(piece, "head", swap_pairs(count))
+    first = index % 2 == 0
+    pair = jnp.concatenate(
+        [jnp.where(first, piece, near), jnp.where(first, near, piece)], axis=axis
+    )
+    far = lax.ppermute(pair, "head", [(i, (i + 2) % 4) for i in range(count)])
+    lower = index < 2
+    return jnp.concatenate(
+        [jnp.where(lower, pair, far), jnp.where(lower, far, pair)], axis=axis
+    )
 
 
 def body(
@@ -124,16 +215,27 @@
     average_head,
     average_filter,
 ):
-    inner_full, step_full, output_full = (
-        lax.all_gather(weight_inner.astype(jnp.bfloat16), "dp", axis=0, tiled=True),
-        lax.all_gather(weight_step.astype(jnp.bfloat16), "dp", axis=0, tiled=True),
-        lax.all_gather(weight_output.astype(jnp.bfloat16), "dp", axis=1, tiled=True),
-    )
-    state_full, gain_full, filter_full = (
-        lax.all_gather(weight_state.astype(jnp.bfloat16), ("dp", "head"), axis=0, tiled=True),
-        lax.all_gather(norm_gain.astype(jnp.bfloat16), ("dp", "head"), axis=0, tiled=True),
-        lax.all_gather(state_filter.astype(jnp.bfloat16), ("dp", "head"), axis=0, tiled=True),
-    )
+    low = jnp.bfloat16
+    count_dp = lax.axis_size("dp")
+    heads_own = weight_step.shape[1]
+    rows_all, state_rows = weight_state.shape[0], state_filter.shape[0]
+    filter_block = jnp.pad(state_filter.astype(low), ((0, rows_all - state_rows), (0, 0)))
+    shared_piece = jnp.concatenate(
+        [weight_state.astype(low), norm_gain.astype(low)[:, None], filter_block], axis=1
+    )
+    shared_rows = gather_head(shared_piece, 0)
+    small_rows = jnp.concatenate([shared_rows, weight_step.astype(low)], axis=1)
+    small_rows = jnp.pad(small_rows, ((0, 0), (0, -small_rows.shape[1] % 128)))
+    inner_value = gather_dp(weight_inner[:, 1].astype(low), 0)
+    small_full = gather_dp(small_rows, 0)
+    inner_gate = gather_dp(weight_inner[:, 0].astype(low), 0)
+    output_full = gather_dp(weight_output.astype(low), 1)
+    width_state = weight_state.shape[1]
+    state_full = small_full[:, :width_state]
+    gain_full = small_full[:, width_state]
+    filter_full = small_full[:, width_state + 1 : width_state + 1 + KC + 1]
+    filter_full = filter_full.reshape(-1, rows_all, KC + 1)[:, :state_rows].reshape(-1, KC + 1)
+    step_full = small_full[:, width_state + KC + 2 : width_state + KC + 2 + heads_own]
     channel_used = rounded(channel_table)
     head_values = rounded(head_table)
     gathered = lax.all_gather(inputs, "head", axis=1, tiled=True)
@@ -141,9 +243,8 @@
     inverse = lax.rsqrt(jnp.mean(tokens_full * tokens_full, axis=1) + EPS)
     gain_float = gain_full.astype(jnp.float32)
     normed = (tokens_full * inverse[:, None] * gain_float[None, :]).astype(jnp.bfloat16)
-    inner_pair = jnp.einsum("td,dkc->tkc", normed, inner_full, preferred_element_type=jnp.float32)
-    gate_values = inner_pair[:, 0]
-    inner_x = inner_pair[:, 1]
+    gate_values = jnp.dot(normed, inner_gate, preferred_element_type=jnp.float32)
+    inner_x = jnp.dot(normed, inner_value, preferred_element_type=jnp.float32)
     state_bc = jnp.dot(normed, state_full, preferred_element_type=jnp.float32)
     step_raw = jnp.dot(normed, step_full, preferred_element_type=jnp.float32)
     block_open = block_opens.astype(jnp.float32)
@@ -197,14 +298,17 @@
     grad_sq = lax.psum(grad_sq_part, "head")
     grad_sx, grad_sbc, grad_raw, grad_gate, grad_head = mix_back((grad_gated, grad_sq))
     grad_inner_x, grad_state_bc, grad_taps_x, grad_taps_bc = conv_back((grad_sx, grad_sbc))
-    pair_low = jnp.stack([grad_gate, grad_inner_x], axis=1).astype(jnp.bfloat16)
+    gate_low = grad_gate.astype(jnp.bfloat16)
+    inner_low = grad_inner_x.astype(jnp.bfloat16)
     state_low = grad_state_bc.astype(jnp.bfloat16)
     step_low = grad_raw.astype(jnp.bfloat16)
-    grad_inner = jnp.einsum("td,tkc->dkc", normed, pair_low, preferred_element_type=jnp.float32)
+    grad_gate_w = jnp.einsum("td,tc->dc", normed, gate_low, preferred_element_type=jnp.float32)
+    grad_inner_w = jnp.einsum("td,tc->dc", normed, inner_low, preferred_element_type=jnp.float32)
     grad_state = jnp.einsum("td,ts->ds", normed, state_low, preferred_element_type=jnp.float32)
     grad_step = jnp.einsum("td,th->dh", normed, step_low, preferred_element_type=jnp.float32)
-    grad_normed = jnp.einsum(
-        "tkc,dkc->td", pair_low, inner_full, preferred_element_type=jnp.float32
+    grad_normed = jnp.einsum("tc,dc->td", gate_low, inner_gate, preferred_element_type=jnp.float32)
+    grad_normed = grad_normed + jnp.einsum(
+        "tc,dc->td", inner_low, inner_value, preferred_element_type=jnp.float32
     )
     grad_normed = grad_normed + jnp.einsum(
         "ts,ds->td", state_low, state_full, preferred_element_type=jnp.float32
@@ -233,17 +337,37 @@
     )
     grad_channel = jnp.concatenate([grad_taps_x, grad_gate_gain[None, :]], axis=0)
     grad_filter = grad_taps_bc.T
-    inner_reduced, step_reduced, output_reduced = (
-        lax.psum_scatter(grad_inner, "dp", scatter_dimension=0, tiled=True),
-        lax.psum_scatter(grad_step, "dp", scatter_dimension=0, tiled=True),
-        lax.psum_scatter(block_grad, "dp", scatter_dimension=1, tiled=True),
-    )
-    state_reduced, gain_reduced, filter_reduced = (
-        lax.psum_scatter(grad_state, ("dp", "head"), scatter_dimension=0, tiled=True),
-        lax.psum_scatter(grad_gain_full, ("dp", "head"), scatter_dimension=0, tiled=True),
-        lax.psum_scatter(grad_filter, ("dp", "head"), scatter_dimension=0, tiled=True),
-    )
-    channel_reduced, head_reduced = lax.psum((grad_channel, grad_head), "dp")
+    output_reduced = reduce_dp(block_grad, 1)
+    gate_reduced = reduce_dp(grad_gate_w, 0)
+    inner_reduced = reduce_dp(grad_inner_w, 0)
+    inner_reduced = jnp.stack([gate_reduced, inner_reduced], axis=1)
+    count_head = lax.axis_size("head")
+    filter_part = jnp.pad(
+        grad_filter.reshape(count_dp, count_head, state_rows * (KC + 1)),
+        ((0, 0), (0, 0), (0, rows_all - state_rows * (KC + 1))),
+    ).reshape(D, 1)
+    shared_part = jnp.concatenate(
+        [grad_state, grad_gain_full[:, None], filter_part], axis=1
+    ).reshape(count_dp, count_head, rows_all, width_state + 2)
+    shared_own = reduce_head(jnp.swapaxes(shared_part, 0, 1))
+    table_part = jnp.concatenate([grad_channel.reshape(-1), grad_head.reshape(-1)])
+    table_width = -(-table_part.shape[0] // rows_all)
+    table_part = jnp.pad(table_part, (0, table_width * rows_all - table_part.shape[0]))
+    table_part = jnp.broadcast_to(
+        table_part.reshape(1, rows_all, table_width), (count_dp, rows_all, table_width)
+    )
+    step_part = grad_step.reshape(count_dp, rows_all, -1)
+    small_part = jnp.concatenate([shared_own, step_part, table_part], axis=2)
+    small_own = reduce_dp(small_part.reshape(count_dp * rows_all, -1), 0)
+    state_reduced = small_own[:, :width_state]
+    gain_reduced = small_own[:, width_state]
+    filter_reduced = small_own[: state_rows * (KC + 1), width_state + 1].reshape(state_rows, KC + 1)
+    at = width_state + 2
+    step_reduced = small_own[:, at : at + step_part.shape[2]].reshape(-1, heads_own)
+    table_own = small_own[:, at + step_part.shape[2] :].reshape(-1)
+    channel_size = grad_channel.shape[0] * grad_channel.shape[1]
+    channel_reduced = table_own[:channel_size].reshape(grad_channel.shape)
+    head_reduced = table_own[channel_size : channel_size + grad_head.size].reshape(grad_head.shape)
     total_tokens = inputs.shape[0] * lax.axis_size("dp")
     matrix_rate = RATE_MATRIX / math.sqrt(total_tokens)
     vector_rate = RATE_VECTOR / math.sqrt(total_tokens)

time: 1330 us -> 878 us (0.66)
  waiting for transfers between devices: 627 us -> 205 us
  blocking collectives: 208 us -> 20.1 us
  starting transfers between devices: 0.45 us -> 128 us
  other arithmetic: 135 us -> 155 us
    reduce_scatter x4 -> x0, waiting for transfers between devices: 515 us -> none  [the longest x1 281 us: body(): lax.psum_scatter(grad_inner, 'dp', scatter_dimension=0, tiled=True)]
    ppermute x0 -> x60, waiting for transfers between devices: none -> 204 us  [the longest x12 67.6 us: gather_dp(): held[shift] = lax.ppermute(shard, 'dp', perm)]
    ppermute x0 -> x60, starting transfers between devices: none -> 128 us  [the longest x12 46.3 us: reduce_dp(): pair = lax.ppermute(pair.astype(low), 'dp', perm).astype(jnp.float32)]
    unnamed x2 -> x0, blocking collectives: 82 us -> none
    all_gather x2 -> x0, blocking collectives: 71.4 us -> none  [the longest x1 40.5 us: body(): lax.all_gather(state_filter.astype(jnp.bfloat16), ('dp', 'head'), axis=0,...]
    all_gather x3 -> x0, waiting for transfers between devices: 69.7 us -> none  [the longest x1 69.6 us: body(): lax.all_gather(weight_inner.astype(jnp.bfloat16), 'dp', axis=0, tiled=True)]
    reduce_scatter x1, waiting for transfers between devices: 41.6 us -> 0.02 us  [body(): lax.psum_scatter(grad_normed.astype(jnp.bfloat16), 'head', scatter_dimens...]
    psum x1 -> x0, blocking collectives: 35.3 us -> none  [body(): channel_reduced, head_reduced = lax.psum((grad_channel, grad_head), 'dp')]
  transfers between devices with their start and end apart: 11 -> 64, of which waited for: 5 -> 25; matrix products, arithmetic and copies ran while one was open for 19% -> 29% of each run, Pallas kernels for 0% -> 0%
where the time goes in v1:
time: 878 us; the launch traced here: 869 us
  waiting for transfers between devices  205 us (23%)
  matrix products  197 us (22%)
  other arithmetic  155 us (18%)
  local copies, waits for them, and re-layouts  146 us (17%)
  starting transfers between devices  128 us (15%)
  blocking collectives  20.1 us (2%)
  between operations  16.4 us (2%)
    ppermute x12, waiting for transfers between devices, gather_dp(): held[shift] = lax.ppermute(shard, 'dp', perm)  67.6 us
    ppermute x16, waiting for transfers between devices, reduce_dp(): came = lax.ppermute(away.astype(low), 'dp', swap_pairs(count))  64.8 us
    dot_general x3, matrix products, state_mixer(): jnp.einsum('ntuh,nuhp->nthp', mixing, values, precision=HIGHEST)  54.5 us
    ppermute x16, waiting for transfers between devices, gather_dp(): other = lax.ppermute(held[shift], 'dp', swap_pairs(count))  51.9 us
    ppermute x12, starting transfers between devices, reduce_dp(): pair = lax.ppermute(pair.astype(low), 'dp', perm).astype(jnp.float32)  46.3 us
    ppermute x12, starting transfers between devices, gather_dp(): held[shift] = lax.ppermute(shard, 'dp', perm)  45.8 us
    unnamed x290, local copies, waits for them, and re-layouts  35.9 us
    another operation x7, other arithmetic  20 us
  transfers between devices with their start and end apart: 64, of which 25 were waited for; matrix products, arithmetic and copies ran while one was open for 29% of the time, Pallas kernels for 0%

profile of v1, /device:TPU:0, one launch (start us, length us, event | category | flops | bytes accessed | tf_op | source)
XLA Modules:
  0.0 868.6 jit_solution(8373437666757548406)
XLA Ops:
  45.8 7.1 collective-permute-start.10
  61.7 10.6 %collective-permute-start.12 = (bf16[256,1024]{1,0:T(8,128)(2,1)}, bf16[256,1024]{1,0:T(8,128)(2,1)}, u32[]{:S(2)}, u32[]{:S(2)}) collective-permute-start(bf16[256,1024]{1,0:T(8,128)(2,1)} %get-tuple-element.573), channel_id=1, source_target_pairs={{0,16},{4,20},{8,24},{12,28},{16,0},{20,4},{24,8},{28,12},{1,17},{... | collective-permute-start | bytes 1572872 | tf_op jit(solution)/shard_map/ppermute | solution.py:114
  76.0 5.2 collective-permute-start.17
  86.4 31.4 %collective-permute-done.12 = bf16[256,1024]{1,0:T(8,128)(2,1)} collective-permute-done((bf16[256,1024]{1,0:T(8,128)(2,1)}, bf16[256,1024]{1,0:T(8,128)(2,1)}, u32[]{:S(2)}, u32[]{:S(2)}) %collective-permute-start.12) | collective-permute-done | bytes 524320 | tf_op jit(solution)/shard_map/ppermute | solution.py:114
  138.3 29.5 %collective-permute-done.19 = bf16[256,1024]{1,0:T(8,128)(2,1)S(1)} collective-permute-done((bf16[256,1024]{1,0:T(8,128)(2,1)}, bf16[256,1024]{1,0:T(8,128)(2,1)S(1)}, u32[]{:S(2)}, u32[]{:S(2)}) %collective-permute-start.19) | collective-permute-done | bytes 524320 | tf_op jit(solution)/shard_map/ppermute | solution.py:114
  167.7 13.6 %collective-permute-start.28 = (bf16[1024,256]{1,0:T(8,128)(2,1)S(1)}, bf16[1024,256]{1,0:T(8,128)(2,1)S(1)}, u32[]{:S(2)}, u32[]{:S(2)}) collective-permute-start(bf16[1024,256]{1,0:T(8,128)(2,1)S(1)} %copy-done.55), channel_id=1, source_target_pairs={{0,24},{4,28},{8,0},{12,4},{16,8},{20,12},{24,16},{28,20},{1,25},{... | collective-permute-start | bytes 1572872 | tf_op jit(solution)/shard_map/ppermute | solution.py:114
  198.3 9.1 %collective-permute-done.25 = bf16[1024,256]{1,0:T(8,128)(2,1)S(1)} collective-permute-done((bf16[1024,256]{1,0:T(8,128)(2,1)}, bf16[1024,256]{1,0:T(8,128)(2,1)S(1)}, u32[]{:S(2)}, u32[]{:S(2)}) %collective-permute-start.25) | collective-permute-done | bytes 524320 | tf_op jit(solution)/shard_map/ppermute | solution.py:119
  209.2 9.5 %collective-permute-done.27 = bf16[1024,256]{1,0:T(8,128)(2,1)S(1)} collective-permute-done((bf16[1024,256]{1,0:T(8,128)(2,1)S(1)}, bf16[1024,256]{1,0:T(8,128)(2,1)S(1)}, u32[]{:S(2)}, u32[]{:S(2)}) %collective-permute-start.27) | collective-permute-done | bytes 524320 | tf_op jit(solution)/shard_map/ppermute | solution.py:119
  220.4 9.5 %collective-permute-done.15 = bf16[256,1024]{1,0:T(8,128)(2,1)S(1)} collective-permute-done((bf16[256,1024]{1,0:T(8,128)(2,1)S(1)}, bf16[256,1024]{1,0:T(8,128)(2,1)S(1)}, u32[]{:S(2)}, u32[]{:S(2)}) %collective-permute-start.15) | collective-permute-done | bytes 524320 | tf_op jit(solution)/shard_map/ppermute | solution.py:119
  230.7 10.4 %collective-permute-done.22 = bf16[256,1024]{1,0:T(8,128)(2,1)S(1)} collective-permute-done((bf16[256,1024]{1,0:T(8,128)(2,1)S(1)}, bf16[256,1024]{1,0:T(8,128)(2,1)S(1)}, u32[]{:S(2)}, u32[]{:S(2)}) %collective-permute-start.22) | collective-permute-done | bytes 524320 | tf_op jit(solution)/shard_map/ppermute | solution.py:119
  241.9 9.0 %collective-permute-done.29 = bf16[1024,256]{1,0:T(8,128)(2,1)S(1)} collective-permute-done((bf16[1024,256]{1,0:T(8,128)(2,1)S(1)}, bf16[1024,256]{1,0:T(8,128)(2,1)S(1)}, u32[]{:S(2)}, u32[]{:S(2)}) %collective-permute-start.29) | collective-permute-done | bytes 524320 | tf_op jit(solution)/shard_map/ppermute | solution.py:119
  257.7 6.8 fusion.137
  269.7 7.5 multiply_convert_fusion
  281.2 3.4 reshape.353
  284.6 4.0 compare_select_fusion.2
  306.3 5.1 fusion.45
  311.7 23.4 %while.36 = (s32[]{:T(128)}, f32[16,64,128]{2,1,0:T(8,128)S(1)}, f32[4,16,64,128]{3,2,1,0:T(8,128)S(1)}, f32[4]{0:T(128)}, f32[4,16,1,1]{1,3,2,0:T(1,128)}, /*in...) while((s32[]{:T(128)}, f32[16,64,128]{2,1,0:T(8,128)S(1)}, ...), condition=%wide.region_4.5_spmd.clone, body=%wide.region_3.4_spmd.clone.sunk | while | flops 786436 | bytes 2623836 | solution.py:72
  340.2 14.6 %fusion.42 = f32[4,256,16,64]{1,3,2,0:T(8,128)S(1)} fusion(f32[4,256,16,64]{1,0,3,2:T(4,128)S(1)} %copy-done.33, f32[4,256,16,64]{1,3,2,0:T(8,128)S(1)} %fusion.139, f32[4,256,16]{1,2,0:T(8,128)S(1)} %bitcast.318, f32[4,256,16]{1,2,0:T(8,128)S(1)} %copy-done.74, f32[4,256,256]{2,1,0:T(8,128)} %fusion.138, pred[256,256]{1,0:T(8,128)(4,1)S(1)} %copy-done.98, ...), kind=kOutput, calls=%fused_computation.81 | convolution fusion | flops 3247439872 | bytes 16056384 | tf_op jit(solution)/shard_map/jvp(ntuh,nuhp->nthp)/dot_general | solution.py:61
  360.2 9.9 %multiply_reduce_fusion.10 = (f32[1024]{0:T(1024)S(1)}, f32[1024,1024]{0,1:T(8,128)}, f32[1024,1024]{0,1:T(8,128)}) fusion(f32[1024,1024]{0,1:T(8,128)S(1)} %bitcast.292, bf16[1024,2048]{1,0:T(8,128)(2,1)S(1)} %copy-done.5, bf16[2048,1024]{1,0:T(8,128)(2,1)} %constant_dynamic-update-slice_fusion.10), kind=kOutput, calls=%fused_computation.90 | convolution fusion | flops 4302306304 | bytes 20975616 | tf_op jit(solution)/shard_map/dot_general | solution.py:246
  370.1 5.6 psum.21
  375.8 12.1 %multiply_reduce_fusion.7 = (f32[1024]{0:T(1024)}, f32[1024]{0:T(1024)S(1)}, f32[1024,1024]{0,1:T(8,128)}) fusion(f32[1024,1024]{0,1:T(8,128)} %get-tuple-element.528, f32[1024]{0:T(1024)S(1)} %fusion.124, f32[1024]{0:T(1024)S(1)} %bitcast.328, bf16[1024,2048]{1,0:T(8,128)(2,1)} %all-gather.5.cloned.1.call-done, ...), kind=kOutput, calls=%fused_computation.86 | convolution fusion | flops 4301256704 | bytes 16793600 | tf_op jit(solution)/shard_map/tw,cw->tc/dot_general | solution.py:293
  387.9 6.6 psum.22
  394.6 13.0 %multiply_reduce_fusion.6 = (f32[1024]{0:T(1024)}, f32[1024,1024]{0,1:T(8,128)}, bf16[1024,1024]{0,1:T(8,128)(2,1)}) fusion(f32[1024,1024]{0,1:T(8,128)} %bitcast.291, bf16[1024,1024]{0,1:T(8,128)(2,1)} %copy-done.12, f32[1024,1024]{0,1:T(8,128)} %get-tuple-element.596, f32[1024,1024]{0,1:T(8,128)} %get-tuple-element.528, f32[1024]{0:T(1024)S(1)} %psum.22, ...), kind=kLoop, calls=%fused_computation.85 | loop fusion | flops 23067648 | bytes 29376512 | tf_op jit(solution)/shard_map/transpose(jvp())/reduce_sum | solution.py:76
  407.5 5.6 reshape.355
  413.1 10.0 %fusion.79 = f32[4,256,128]{2,1,0:T(8,128)} fusion(f32[4,16,64,128]{3,2,1,0:T(8,128)S(1)} %get-tuple-element.744, f32[4,256,16]{1,2,0:T(8,128)S(1)} %get-tuple-element.583, f32[4,256,16]{1,2,0:T(8,128)S(1)} %compare_convert_fusion, f32[4,256,16,64]{1,0,3,2:T(4,128)} %reshape.355), kind=kOutput, calls=%fused_computation.142 | convolution fusion | flops 1612709888 | bytes 6946816 | tf_op jit(solution)/shard_map/transpose(jvp(nhps,nts->nthp))/dot_general | solution.py:73
  423.2 22.6 %fusion.14 = (f32[4,256,16]{1,2,0:T(8,128)}, f32[4,256,16]{1,2,0:T(8,128)}, f32[4,256,16]{1,2,0:T(8,128)}, f32[4,256,256]{2,1,0:T(8,128)}) fusion(f32[4,256,16]{1,2,0:T(8,128)S(1)} %bitcast.319, f32[4,256,16]{1,2,0:T(8,128)S(1)} %copy-done.74, f32[4,256,256]{2,1,0:T(8,128)} %fusion.138, pred[256,256]{1,0:T(8,128)(4,1)S(1)} %copy-done.98, ...), kind=kOutput, calls=%fused_computation.33 | convolution fusion | flops 3284877312 | bytes 8847360 | tf_op jit(solution)/shard_map/transpose(jvp(ntuh,nuhp->nthp))/dot_general | solution.py:61
  445.8 3.8 fusion.46
  451.1 18.7 %while.37 = (s32[]{:T(128)}, f32[16,64,128]{2,1,0:T(8,128)S(1)}, f32[4,16,64,128]{3,2,1,0:T(8,128)}, f32[4,16]{1,0:T(4,128)S(1)}, f32[4,16,64,128]{3,2,1,0:T(8,1...) while((s32[]{:T(128)}, f32[16,64,128]{2,1,0:T(8,128)S(1)}, ...), condition=%wide.region_13.14_spmd.clone, body=%wide.region_11.13_spmd.clone.sunk | while | flops 917492 | bytes 3146276 | solution.py:72
  469.9 9.9 %fusion.78 = f32[4,256,128]{2,1,0:T(8,128)} fusion(f32[4,16,64,128]{3,2,1,0:T(8,128)} %get-tuple-element.234, f32[4,256,16]{1,2,0:T(8,128)S(1)} %copy-done.68, bf16[4,256,16,64]{1,0,3,2:T(4,128)(2,1)} %reshape.347), kind=kOutput, calls=%fused_computation.139 | convolution fusion | flops 1612709888 | bytes 4784128 | tf_op jit(solution)/shard_map/transpose(jvp(nuh,nuhp,nus->nhps))/dot_general | solution.py:63
  484.1 17.2 %bitcast_add_fusion.2 = f32[4,256,16,64]{1,3,2,0:T(8,128)} fusion(f32[4,256,16,64]{1,3,2,0:T(8,128)S(1)} %fusion.141, f32[16]{0:T(128)S(1)} %copy-done.126, f32[4,256,16]{1,2,0:T(8,128)S(1)} %copy-done.68, f32[4,256,16]{1,2,0:T(8,128)S(1)} %bitcast.320, f32[4,256,16]{1,2,0:T(8,128)S(1)} %copy-done.74, f32[4,256,256]{2,1,0:T(8,128)S(1)} %copy-done.54, ...), kind=kOutput, calls=%fused_computation.75 | convolution fusion | flops 3248488448 | bytes 13959232 | tf_op jit(solution)/shard_map/transpose(jvp(ntuh,nuhp->nthp))/dot_general | solution.py:61
  501.4 3.7 multiply_reduce_fusion.5
  507.3 5.0 copy.454
  515.9 8.4 multiply_reduce_fusion.4
  524.3 6.3 slice_multiply_fusion.2
  530.7 5.9 multiply_reduce_fusion.3
  536.7 6.4 slice_multiply_fusion.1
  543.1 4.3 slice_multiply_fusion
  549.1 6.9 multiply_reduce_fusion.1
  556.0 10.8 %fusion.72 = f32[1024,2048]{1,0:T(8,128)} fusion(bf16[2048,1024]{1,0:T(8,128)(2,1)} %constant_dynamic-update-slice_fusion.18, bf16[1024,1280]{0,1:T(8,128)(2,1)} %get-tuple-element.560), kind=kOutput, calls=%fused_computation.130 | convolution fusion | flops 4294967296 | bytes 14680064 | tf_op jit(solution)/shard_map/tc,dc->td/dot_general | solution.py:310
  566.9 5.8 fusion.82
  573.3 10.1 %reduce-window.16 = f32[4,16,2,128]{3,1,2,0:T(8,128)S(1)} reduce-window(f32[4,16,2,128]{3,1,2,0:T(8,128)S(1)} %bitcast.317, f32[]{:T(128)} %constant.352.clone.1), window={size=1x1x1x128 pad=0_0x0_0x0_0x0_127}, to_apply=%region_19.20 | reduce-window | flops 2080768 | bytes 131076 | tf_op jit(solution)/shard_map/reduce-window.2
  583.8 10.9 %fusion.140 = f32[1024,2048]{1,0:T(8,128)} fusion(bf16[1024,1024]{0,1:T(8,128)(2,1)} %get-tuple-element.537, bf16[2048,1024]{1,0:T(8,128)(2,1)} %constant_dynamic-update-slice_fusion.10), kind=kOutput, calls=%fused_computation.365 | convolution fusion | flops 4294967296 | bytes 14680064 | tf_op jit(solution)/shard_map/tc,dc->td/dot_general | solution.py:309
  594.9 7.0 add_convert_fusion
  602.8 8.5 fusion.129
  618.2 8.7 convolution_convert_fusion
  628.5 6.5 fusion.142
  640.4 7.2 fusion.70
  650.5 4.1 dynamic-slice_convert_fusion.7
  656.3 8.4 collective-permute-done.32
  667.4 8.6 collective-permute-done.34
  681.7 5.5 collective-permute-done.37
  687.3 11.2 %collective-permute-done.39 = bf16[256,1024]{1,0:T(8,128)(2,1)} collective-permute-done((bf16[256,1024]{1,0:T(8,128)(2,1)}, bf16[256,1024]{1,0:T(8,128)(2,1)}, u32[]{:S(2)}, u32[]{:S(2)}) %collective-permute-start.39) | collective-permute-done | bytes 524320 | tf_op jit(solution)/shard_map/ppermute | solution.py:142
  698.5 3.7 fusion.88
  702.2 7.4 collective-permute-done.41
  712.3 8.5 collective-permute-done.57
  721.2 10.9 %collective-permute-done.36 = bf16[256,1024]{1,0:T(8,128)(2,1)S(1)} collective-permute-done((bf16[256,1024]{1,0:T(8,128)(2,1)S(1)}, bf16[256,1024]{1,0:T(8,128)(2,1)S(1)}, u32[]{:S(2)}, u32[]{:S(2)}) %collective-permute-start.36) | collective-permute-done | bytes 524320 | tf_op jit(solution)/shard_map/ppermute | solution.py:142
  732.5 3.5 collective-permute-start.42
  743.3 9.7 %collective-permute-start.54 = (bf16[1024,256]{1,0:T(8,128)(2,1)}, bf16[1024,256]{1,0:T(8,128)(2,1)}, u32[]{:S(2)}, u32[]{:S(2)}) collective-permute-start(bf16[1024,256]{1,0:T(8,128)(2,1)} %get-tuple-element.538), channel_id=1, source_target_pairs={{0,8},{4,12},{8,16},{12,20},{16,24},{20,28},{24,0},{28,4},{1,9},{5... | collective-permute-start | bytes 1572872 | tf_op jit(solution)/shard_map/ppermute | solution.py:146
  753.0 12.5 %collective-permute-start.56 = (bf16[1024,256]{1,0:T(8,128)(2,1)}, bf16[1024,256]{1,0:T(8,128)(2,1)}, u32[]{:S(2)}, u32[]{:S(2)}) collective-permute-start(bf16[1024,256]{1,0:T(8,128)(2,1)} %get-tuple-element.540), channel_id=1, source_target_pairs={{0,16},{4,20},{8,24},{12,28},{16,0},{20,4},{24,8},{28,12},{1,17},{... | collective-permute-start | bytes 1572872 | tf_op jit(solution)/shard_map/ppermute | solution.py:146
  765.5 18.7 %collective-permute-done.40 = bf16[256,1024]{1,0:T(8,128)(2,1)S(1)} collective-permute-done((bf16[256,1024]{1,0:T(8,128)(2,1)S(1)}, bf16[256,1024]{1,0:T(8,128)(2,1)S(1)}, u32[]{:S(2)}, u32[]{:S(2)}) %collective-permute-start.40) | collective-permute-done | bytes 524320 | tf_op jit(solution)/shard_map/ppermute | solution.py:146
  784.2 13.2 %collective-permute-start.58 = (bf16[1024,256]{1,0:T(8,128)(2,1)}, bf16[1024,256]{1,0:T(8,128)(2,1)}, u32[]{:S(2)}, u32[]{:S(2)}) collective-permute-start(bf16[1024,256]{1,0:T(8,128)(2,1)} %get-tuple-element.539), channel_id=1, source_target_pairs={{0,24},{4,28},{8,0},{12,4},{16,8},{20,12},{24,16},{28,20},{1,25},{... | collective-permute-start | bytes 1572872 | tf_op jit(solution)/shard_map/ppermute | solution.py:146
  821.9 4.1 multiply_add_fusion.1
  825.9 7.8 psum.23
  842.1 4.7 collective-permute-start.47
  (649 shorter events, 283.9 us)
Async XLA Ops:
  7.3 244.6 %all-gather.3.cloned.1.call-start = ((), (), s32[]{:S(2)}) async-start(), calls=%async_computation.2 | async-start | bytes 5242880 | tf_op jit(solution)/shard_map/all_gather | solution.py:241
  8.0 367.8 %all-gather.5.cloned.1.call-start = ((), (), s32[]{:S(2)}) async-start(), calls=%async_computation.4 | async-start | bytes 5242880 | tf_op jit(solution)/shard_map/all_gather | solution.py:292
  11.3 71.2 %collective-permute-start.9 = (bf16[256,1024]{1,0:T(8,128)(2,1)}, bf16[256,1024]{1,0:T(8,128)(2,1)}, u32[]{:S(2)}, u32[]{:S(2)}) collective-permute-start(bf16[256,1024]{1,0:T(8,128)(2,1)} %get-tuple-element.573), channel_id=1, source_target_pairs={{0,4},{4,0},{8,12},{12,8},{16,20},{20,16},{24,28},{28,24},{1,5},{5... | collective-permute-start | bytes 1572872 | tf_op jit(solution)/shard_map/ppermute | solution.py:119
  14.5 12.6 %collective-permute-start = (bf16[64,262]{1,0:T(8,128)(2,1)S(1)}, bf16[64,262]{1,0:T(8,128)(2,1)S(1)}, u32[]{:S(2)}, u32[]{:S(2)}) collective-permute-start(bf16[64,262]{1,0:T(8,128)(2,1)S(1)} %fusion.107), channel_id=1, source_target_pairs={{0,1},{1,0},{2,3},{3,2},{4,5},{5,4},{6,7},{7,6},{8,9},{9,8},{10,11... | collective-permute-start | bytes 100616 | tf_op jit(solution)/shard_map/ppermute | solution.py:175
  16.3 782.7 %reduce-scatter.5.cloned.1.call-start = ((), (), s32[]{:S(2)}) async-start(), calls=%async_computation.5 | async-start | bytes 5242880 | tf_op jit(solution)/shard_map/reduce_scatter | solution.py:319
  27.2 7.6 collective-permute-start.1
  35.0 23.9 %collective-permute-start.2 = (bf16[256,384]{1,0:T(8,128)(2,1)S(1)}, bf16[256,384]{1,0:T(8,128)(2,1)}, u32[]{:S(2)}, u32[]{:S(2)}) collective-permute-start(bf16[256,384]{1,0:T(8,128)(2,1)S(1)} %fusion.96), channel_id=1, source_target_pairs={{0,4},{4,0},{8,12},{12,8},{16,20},{20,16},{24,28},{28,24},{1,5},{5... | collective-permute-start | bytes 589832 | tf_op jit(solution)/shard_map/ppermute | solution.py:119
  35.2 9.9 %collective-permute-start.3 = (bf16[256,384]{1,0:T(8,128)(2,1)S(1)}, bf16[256,384]{1,0:T(8,128)(2,1)S(1)}, u32[]{:S(2)}, u32[]{:S(2)}) collective-permute-start(bf16[256,384]{1,0:T(8,128)(2,1)S(1)} %fusion.96), channel_id=1, source_target_pairs={{0,8},{4,12},{8,16},{12,20},{16,24},{20,28},{24,0},{28,4},{1,9},{5... | collective-permute-start | bytes 589832 | tf_op jit(solution)/shard_map/ppermute | solution.py:114
  37.2 16.7 %collective-permute-start.5 = (bf16[256,384]{1,0:T(8,128)(2,1)S(1)}, bf16[256,384]{1,0:T(8,128)(2,1)}, u32[]{:S(2)}, u32[]{:S(2)}) collective-permute-start(bf16[256,384]{1,0:T(8,128)(2,1)S(1)} %fusion.96), channel_id=1, source_target_pairs={{0,16},{4,20},{8,24},{12,28},{16,0},{20,4},{24,8},{28,12},{1,17},{... | collective-permute-start | bytes 589832 | tf_op jit(solution)/shard_map/ppermute | solution.py:114
  39.8 16.8 %collective-permute-start.7 = (bf16[256,384]{1,0:T(8,128)(2,1)S(1)}, bf16[256,384]{1,0:T(8,128)(2,1)S(1)}, u32[]{:S(2)}, u32[]{:S(2)}) collective-permute-start(bf16[256,384]{1,0:T(8,128)(2,1)S(1)} %fusion.96), channel_id=1, source_target_pairs={{0,24},{4,28},{8,0},{12,4},{16,8},{20,12},{24,16},{28,20},{1,25},{... | collective-permute-start | bytes 589832 | tf_op jit(solution)/shard_map/ppermute | solution.py:114
  45.8 38.3 %collective-permute-start.10 = (bf16[256,1024]{1,0:T(8,128)(2,1)}, bf16[256,1024]{1,0:T(8,128)(2,1)}, u32[]{:S(2)}, u32[]{:S(2)}) collective-permute-start(bf16[256,1024]{1,0:T(8,128)(2,1)} %get-tuple-element.573), channel_id=1, source_target_pairs={{0,8},{4,12},{8,16},{12,20},{16,24},{20,28},{24,0},{28,4},{1,9},{5... | collective-permute-start | bytes 1572872 | tf_op jit(solution)/shard_map/ppermute | solution.py:114
  53.9 7.7 collective-permute-start.4
  57.3 16.1 %collective-permute-start.6 = (bf16[256,384]{1,0:T(8,128)(2,1)}, bf16[256,384]{1,0:T(8,128)(2,1)}, u32[]{:S(2)}, u32[]{:S(2)}) collective-permute-start(bf16[256,384]{1,0:T(8,128)(2,1)} %collective-permute-done.5), channel_id=1, source_target_pairs={{0,4},{4,0},{8,12},{12,8},{16,20},{20,16},{24,28},{28,24},{1,5},{5... | collective-permute-start | bytes 589832 | tf_op jit(solution)/shard_map/ppermute | solution.py:119
  58.9 17.1 %collective-permute-start.8 = (bf16[256,384]{1,0:T(8,128)(2,1)}, bf16[256,384]{1,0:T(8,128)(2,1)}, u32[]{:S(2)}, u32[]{:S(2)}) collective-permute-start(bf16[256,384]{1,0:T(8,128)(2,1)} %copy-done.71), channel_id=1, source_target_pairs={{0,4},{4,0},{8,12},{12,8},{16,20},{20,16},{24,28},{28,24},{1,5},{5... | collective-permute-start | bytes 589832 | tf_op jit(solution)/shard_map/ppermute | solution.py:119
  61.7 56.2 %collective-permute-start.12 = (bf16[256,1024]{1,0:T(8,128)(2,1)}, bf16[256,1024]{1,0:T(8,128)(2,1)}, u32[]{:S(2)}, u32[]{:S(2)}) collective-permute-start(bf16[256,1024]{1,0:T(8,128)(2,1)} %get-tuple-element.573), channel_id=1, source_target_pairs={{0,16},{4,20},{8,24},{12,28},{16,0},{20,4},{24,8},{28,12},{1,17},{... | collective-permute-start | bytes 1572872 | tf_op jit(solution)/shard_map/ppermute | solution.py:114
  73.4 47.9 %collective-permute-start.16 = (bf16[256,1024]{1,0:T(8,128)(2,1)}, bf16[256,1024]{1,0:T(8,128)(2,1)}, u32[]{:S(2)}, u32[]{:S(2)}) collective-permute-start(bf16[256,1024]{1,0:T(8,128)(2,1)} %get-tuple-element.572), channel_id=1, source_target_pairs={{0,4},{4,0},{8,12},{12,8},{16,20},{20,16},{24,28},{28,24},{1,5},{5... | collective-permute-start | bytes 1572872 | tf_op jit(solution)/shard_map/ppermute | solution.py:119
  76.0 45.3 %collective-permute-start.17 = (bf16[256,1024]{1,0:T(8,128)(2,1)}, bf16[256,1024]{1,0:T(8,128)(2,1)}, u32[]{:S(2)}, u32[]{:S(2)}) collective-permute-start(bf16[256,1024]{1,0:T(8,128)(2,1)} %get-tuple-element.572), channel_id=1, source_target_pairs={{0,8},{4,12},{8,16},{12,20},{16,24},{20,28},{24,0},{28,4},{1,9},{5... | collective-permute-start | bytes 1572872 | tf_op jit(solution)/shard_map/ppermute | solution.py:114
  82.4 39.0 %collective-permute-start.23 = (bf16[1024,256]{1,0:T(8,128)(2,1)}, bf16[1024,256]{1,0:T(8,128)(2,1)}, u32[]{:S(2)}, u32[]{:S(2)}) collective-permute-start(bf16[1024,256]{1,0:T(8,128)(2,1)} %get-tuple-element.532), channel_id=1, source_target_pairs={{0,4},{4,0},{8,12},{12,8},{16,20},{20,16},{24,28},{28,24},{1,5},{5... | collective-permute-start | bytes 1572872 | tf_op jit(solution)/shard_map/ppermute | solution.py:119
  84.2 41.6 %collective-permute-start.24 = (bf16[1024,256]{1,0:T(8,128)(2,1)}, bf16[1024,256]{1,0:T(8,128)(2,1)}, u32[]{:S(2)}, u32[]{:S(2)}) collective-permute-start(bf16[1024,256]{1,0:T(8,128)(2,1)} %get-tuple-element.532), channel_id=1, source_target_pairs={{0,8},{4,12},{8,16},{12,20},{16,24},{20,28},{24,0},{28,4},{1,9},{5... | collective-permute-start | bytes 1572872 | tf_op jit(solution)/shard_map/ppermute | solution.py:114
  117.9 15.1 %collective-permute-start.11 = (bf16[256,1024]{1,0:T(8,128)(2,1)}, bf16[256,1024]{1,0:T(8,128)(2,1)S(1)}, u32[]{:S(2)}, u32[]{:S(2)}) collective-permute-start(bf16[256,1024]{1,0:T(8,128)(2,1)} %collective-permute-done.10), channel_id=1, source_target_pairs={{0,4},{4,0},{8,12},{12,8},{16,20},{20,16},{24,28},{28,24},{1,5},{5... | collective-permute-start | bytes 1572872 | tf_op jit(solution)/shard_map/ppermute | solution.py:119
  121.3 14.7 %collective-permute-start.14 = (bf16[256,1024]{1,0:T(8,128)(2,1)}, bf16[256,1024]{1,0:T(8,128)(2,1)S(1)}, u32[]{:S(2)}, u32[]{:S(2)}) collective-permute-start(bf16[256,1024]{1,0:T(8,128)(2,1)} %get-tuple-element.573), channel_id=1, source_target_pairs={{0,24},{4,28},{8,0},{12,4},{16,8},{20,12},{24,16},{28,20},{1,25},{... | collective-permute-start | bytes 1572872 | tf_op jit(solution)/shard_map/ppermute | solution.py:114
  121.3 46.4 %collective-permute-start.19 = (bf16[256,1024]{1,0:T(8,128)(2,1)}, bf16[256,1024]{1,0:T(8,128)(2,1)S(1)}, u32[]{:S(2)}, u32[]{:S(2)}) collective-permute-start(bf16[256,1024]{1,0:T(8,128)(2,1)} %get-tuple-element.572), channel_id=1, source_target_pairs={{0,16},{4,20},{8,24},{12,28},{16,0},{20,4},{24,8},{28,12},{1,17},{... | collective-permute-start | bytes 1572872 | tf_op jit(solution)/shard_map/ppermute | solution.py:114
  121.4 59.9 %collective-permute-start.18 = (bf16[256,1024]{1,0:T(8,128)(2,1)}, bf16[256,1024]{1,0:T(8,128)(2,1)S(1)}, u32[]{:S(2)}, u32[]{:S(2)}) collective-permute-start(bf16[256,1024]{1,0:T(8,128)(2,1)} %collective-permute-done.17), channel_id=1, source_target_pairs={{0,4},{4,0},{8,12},{12,8},{16,20},{20,16},{24,28},{28,24},{1,5},{5... | collective-permute-start | bytes 1572872 | tf_op jit(solution)/shard_map/ppermute | solution.py:119
  125.7 58.8 %collective-permute-start.13 = (bf16[256,1024]{1,0:T(8,128)(2,1)}, bf16[256,1024]{1,0:T(8,128)(2,1)S(1)}, u32[]{:S(2)}, u32[]{:S(2)}) collective-permute-start(bf16[256,1024]{1,0:T(8,128)(2,1)} %collective-permute-done.12), channel_id=1, source_target_pairs={{0,4},{4,0},{8,12},{12,8},{16,20},{20,16},{24,28},{28,24},{1,5},{5... | collective-permute-start | bytes 1572872 | tf_op jit(solution)/shard_map/ppermute | solution.py:119
  132.9 54.8 %collective-permute-start.26 = (bf16[1024,256]{1,0:T(8,128)(2,1)S(1)}, bf16[1024,256]{1,0:T(8,128)(2,1)S(1)}, u32[]{:S(2)}, u32[]{:S(2)}) collective-permute-start(bf16[1024,256]{1,0:T(8,128)(2,1)S(1)} %copy-done.55), channel_id=1, source_target_pairs={{0,16},{4,20},{8,24},{12,28},{16,0},{20,4},{24,8},{28,12},{1,17},{... | collective-permute-start | bytes 1572872 | tf_op jit(solution)/shard_map/ppermute | solution.py:114
  136.0 53.0 %collective-permute-start.21 = (bf16[256,1024]{1,0:T(8,128)(2,1)S(1)}, bf16[256,1024]{1,0:T(8,128)(2,1)S(1)}, u32[]{:S(2)}, u32[]{:S(2)}) collective-permute-start(bf16[256,1024]{1,0:T(8,128)(2,1)S(1)} %copy-done.56), channel_id=1, source_target_pairs={{0,24},{4,28},{8,0},{12,4},{16,8},{20,12},{24,16},{28,20},{1,25},{... | collective-permute-start | bytes 1572872 | tf_op jit(solution)/shard_map/ppermute | solution.py:114
  167.7 25.4 %collective-permute-start.28 = (bf16[1024,256]{1,0:T(8,128)(2,1)S(1)}, bf16[1024,256]{1,0:T(8,128)(2,1)S(1)}, u32[]{:S(2)}, u32[]{:S(2)}) collective-permute-start(bf16[1024,256]{1,0:T(8,128)(2,1)S(1)} %copy-done.55), channel_id=1, source_target_pairs={{0,24},{4,28},{8,0},{12,4},{16,8},{20,12},{24,16},{28,20},{1,25},{... | collective-permute-start | bytes 1572872 | tf_op jit(solution)/shard_map/ppermute | solution.py:114
  181.3 14.8 %collective-permute-start.20 = (bf16[256,1024]{1,0:T(8,128)(2,1)S(1)}, bf16[256,1024]{1,0:T(8,128)(2,1)S(1)}, u32[]{:S(2)}, u32[]{:S(2)}) collective-permute-start(bf16[256,1024]{1,0:T(8,128)(2,1)S(1)} %collective-permute-done.19), channel_id=1, source_target_pairs={{0,4},{4,0},{8,12},{12,8},{16,20},{20,16},{24,28},{28,24},{1,5},{5... | collective-permute-start | bytes 1572872 | tf_op jit(solution)/shard_map/ppermute | solution.py:119
  184.5 22.9 %collective-permute-start.25 = (bf16[1024,256]{1,0:T(8,128)(2,1)}, bf16[1024,256]{1,0:T(8,128)(2,1)S(1)}, u32[]{:S(2)}, u32[]{:S(2)}) collective-permute-start(bf16[1024,256]{1,0:T(8,128)(2,1)} %collective-permute-done.24), channel_id=1, source_target_pairs={{0,4},{4,0},{8,12},{12,8},{16,20},{20,16},{24,28},{28,24},{1,5},{5... | collective-permute-start | bytes 1572872 | tf_op jit(solution)/shard_map/ppermute | solution.py:119
  187.7 30.9 %collective-permute-start.27 = (bf16[1024,256]{1,0:T(8,128)(2,1)S(1)}, bf16[1024,256]{1,0:T(8,128)(2,1)S(1)}, u32[]{:S(2)}, u32[]{:S(2)}) collective-permute-start(bf16[1024,256]{1,0:T(8,128)(2,1)S(1)} %collective-permute-done.26), channel_id=1, source_target_pairs={{0,4},{4,0},{8,12},{12,8},{16,20},{20,16},{24,28},{28,24},{1,5},{5... | collective-permute-start | bytes 1572872 | tf_op jit(solution)/shard_map/ppermute | solution.py:119
  189.0 40.8 %collective-permute-start.15 = (bf16[256,1024]{1,0:T(8,128)(2,1)S(1)}, bf16[256,1024]{1,0:T(8,128)(2,1)S(1)}, u32[]{:S(2)}, u32[]{:S(2)}) collective-permute-start(bf16[256,1024]{1,0:T(8,128)(2,1)S(1)} %collective-permute-done.14), channel_id=1, source_target_pairs={{0,4},{4,0},{8,12},{12,8},{16,20},{20,16},{24,28},{28,24},{1,5},{5... | collective-permute-start | bytes 1572872 | tf_op jit(solution)/shard_map/ppermute | solution.py:119
  193.1 48.0 %collective-permute-start.22 = (bf16[256,1024]{1,0:T(8,128)(2,1)S(1)}, bf16[256,1024]{1,0:T(8,128)(2,1)S(1)}, u32[]{:S(2)}, u32[]{:S(2)}) collective-permute-start(bf16[256,1024]{1,0:T(8,128)(2,1)S(1)} %collective-permute-done.21), channel_id=1, source_target_pairs={{0,4},{4,0},{8,12},{12,8},{16,20},{20,16},{24,28},{28,24},{1,5},{5... | collective-permute-start | bytes 1572872 | tf_op jit(solution)/shard_map/ppermute | solution.py:119
  196.2 54.8 %collective-permute-start.29 = (bf16[1024,256]{1,0:T(8,128)(2,1)S(1)}, bf16[1024,256]{1,0:T(8,128)(2,1)S(1)}, u32[]{:S(2)}, u32[]{:S(2)}) collective-permute-start(bf16[1024,256]{1,0:T(8,128)(2,1)S(1)} %collective-permute-done.28), channel_id=1, source_target_pairs={{0,4},{4,0},{8,12},{12,8},{16,20},{20,16},{24,28},{28,24},{1,5},{5... | collective-permute-start | bytes 1572872 | tf_op jit(solution)/shard_map/ppermute | solution.py:119
  601.9 247.3 %reduce-scatter.3.cloned.1.call-start = ((), (), s32[]{:S(2)}) async-start(), calls=%async_computation.3 | async-start | bytes 5242880 | tf_op jit(solution)/shard_map/reduce_scatter | solution.py:286
  616.1 63.1 %collective-permute-start.53 = (bf16[1024,256]{1,0:T(8,128)(2,1)}, bf16[1024,256]{1,0:T(8,128)(2,1)S(1)}, u32[]{:S(2)}, u32[]{:S(2)}) collective-permute-start(bf16[1024,256]{1,0:T(8,128)(2,1)} %get-tuple-element.541), channel_id=1, source_target_pairs={{0,4},{4,0},{8,12},{12,8},{16,20},{20,16},{24,28},{28,24},{1,5},{5... | collective-permute-start | bytes 1572872 | tf_op jit(solution)/shard_map/ppermute | solution.py:142
  616.2 64.8 %collective-permute-start.55 = (bf16[1024,256]{1,0:T(8,128)(2,1)}, bf16[1024,256]{1,0:T(8,128)(2,1)S(1)}, u32[]{:S(2)}, u32[]{:S(2)}) collective-permute-start(bf16[1024,256]{1,0:T(8,128)(2,1)} %get-tuple-element.544), channel_id=1, source_target_pairs={{0,4},{4,0},{8,12},{12,8},{16,20},{20,16},{24,28},{28,24},{1,5},{5... | collective-permute-start | bytes 1572872 | tf_op jit(solution)/shard_map/ppermute | solution.py:142
  636.3 18.3 %collective-permute-start.30 = (bf16[256,1024]{1,0:T(8,128)(2,1)}, bf16[256,1024]{1,0:T(8,128)(2,1)S(1)}, u32[]{:S(2)}, u32[]{:S(2)}) collective-permute-start(bf16[256,1024]{1,0:T(8,128)(2,1)} %get-tuple-element.548), channel_id=1, source_target_pairs={{0,4},{4,0},{8,12},{12,8},{16,20},{20,16},{24,28},{28,24},{1,5},{5... | collective-permute-start | bytes 1572872 | tf_op jit(solution)/shard_map/ppermute | solution.py:142
  637.1 27.6 %collective-permute-start.32 = (bf16[256,1024]{1,0:T(8,128)(2,1)}, bf16[256,1024]{1,0:T(8,128)(2,1)S(1)}, u32[]{:S(2)}, u32[]{:S(2)}) collective-permute-start(bf16[256,1024]{1,0:T(8,128)(2,1)} %get-tuple-element.551), channel_id=1, source_target_pairs={{0,4},{4,0},{8,12},{12,8},{16,20},{20,16},{24,28},{28,24},{1,5},{5... | collective-permute-start | bytes 1572872 | tf_op jit(solution)/shard_map/ppermute | solution.py:142
  648.2 27.8 %collective-permute-start.34 = (bf16[256,1024]{1,0:T(8,128)(2,1)}, bf16[256,1024]{1,0:T(8,128)(2,1)}, u32[]{:S(2)}, u32[]{:S(2)}) collective-permute-start(bf16[256,1024]{1,0:T(8,128)(2,1)} %get-tuple-element.550), channel_id=1, source_target_pairs={{0,4},{4,0},{8,12},{12,8},{16,20},{20,16},{24,28},{28,24},{1,5},{5... | collective-permute-start | bytes 1572872 | tf_op jit(solution)/shard_map/ppermute | solution.py:142
  654.6 32.6 %collective-permute-start.37 = (bf16[256,1024]{1,0:T(8,128)(2,1)}, bf16[256,1024]{1,0:T(8,128)(2,1)}, u32[]{:S(2)}, u32[]{:S(2)}) collective-permute-start(bf16[256,1024]{1,0:T(8,128)(2,1)} %get-tuple-element.555), channel_id=1, source_target_pairs={{0,4},{4,0},{8,12},{12,8},{16,20},{20,16},{24,28},{28,24},{1,5},{5... | collective-permute-start | bytes 1572872 | tf_op jit(solution)/shard_map/ppermute | solution.py:142
  665.5 33.0 %collective-permute-start.39 = (bf16[256,1024]{1,0:T(8,128)(2,1)}, bf16[256,1024]{1,0:T(8,128)(2,1)}, u32[]{:S(2)}, u32[]{:S(2)}) collective-permute-start(bf16[256,1024]{1,0:T(8,128)(2,1)} %get-tuple-element.558), channel_id=1, source_target_pairs={{0,4},{4,0},{8,12},{12,8},{16,20},{20,16},{24,28},{28,24},{1,5},{5... | collective-permute-start | bytes 1572872 | tf_op jit(solution)/shard_map/ppermute | solution.py:142
  676.0 33.6 %collective-permute-start.41 = (bf16[256,1024]{1,0:T(8,128)(2,1)}, bf16[256,1024]{1,0:T(8,128)(2,1)S(1)}, u32[]{:S(2)}, u32[]{:S(2)}) collective-permute-start(bf16[256,1024]{1,0:T(8,128)(2,1)} %get-tuple-element.557), channel_id=1, source_target_pairs={{0,4},{4,0},{8,12},{12,8},{16,20},{20,16},{24,28},{28,24},{1,5},{5... | collective-permute-start | bytes 1572872 | tf_op jit(solution)/shard_map/ppermute | solution.py:142
  679.3 41.6 %collective-permute-start.57 = (bf16[1024,256]{1,0:T(8,128)(2,1)S(1)}, bf16[1024,256]{1,0:T(8,128)(2,1)S(1)}, u32[]{:S(2)}, u32[]{:S(2)}) collective-permute-start(bf16[1024,256]{1,0:T(8,128)(2,1)S(1)} %copy-done.62), channel_id=1, source_target_pairs={{0,4},{4,0},{8,12},{12,8},{16,20},{20,16},{24,28},{28,24},{1,5},{5... | collective-permute-start | bytes 1572872 | tf_op jit(solution)/shard_map/ppermute | solution.py:142
  681.0 51.1 %collective-permute-start.36 = (bf16[256,1024]{1,0:T(8,128)(2,1)S(1)}, bf16[256,1024]{1,0:T(8,128)(2,1)S(1)}, u32[]{:S(2)}, u32[]{:S(2)}) collective-permute-start(bf16[256,1024]{1,0:T(8,128)(2,1)S(1)} %get-tuple-element.549), channel_id=1, source_target_pairs={{0,4},{4,0},{8,12},{12,8},{16,20},{20,16},{24,28},{28,24},{1,5},{5... | collective-permute-start | bytes 1572872 | tf_op jit(solution)/shard_map/ppermute | solution.py:142
  687.2 44.8 %collective-permute-start.31 = (bf16[256,1024]{1,0:T(8,128)(2,1)S(1)}, bf16[256,1024]{1,0:T(8,128)(2,1)S(1)}, u32[]{:S(2)}, u32[]{:S(2)}) collective-permute-start(bf16[256,1024]{1,0:T(8,128)(2,1)S(1)} %get-tuple-element.545), channel_id=1, source_target_pairs={{0,8},{4,12},{8,16},{12,20},{16,24},{20,28},{24,0},{28,4},{1,9},{5... | collective-permute-start | bytes 1572872 | tf_op jit(solution)/shard_map/ppermute | solution.py:146
  698.5 34.0 %collective-permute-start.33 = (bf16[256,1024]{1,0:T(8,128)(2,1)S(1)}, bf16[256,1024]{1,0:T(8,128)(2,1)S(1)}, u32[]{:S(2)}, u32[]{:S(2)}) collective-permute-start(bf16[256,1024]{1,0:T(8,128)(2,1)S(1)} %get-tuple-element.547), channel_id=1, source_target_pairs={{0,16},{4,20},{8,24},{12,28},{16,0},{20,4},{24,8},{28,12},{1,17},{... | collective-permute-start | bytes 1572872 | tf_op jit(solution)/shard_map/ppermute | solution.py:146
  709.6 29.7 %collective-permute-start.35 = (bf16[256,1024]{1,0:T(8,128)(2,1)S(1)}, bf16[256,1024]{1,0:T(8,128)(2,1)S(1)}, u32[]{:S(2)}, u32[]{:S(2)}) collective-permute-start(bf16[256,1024]{1,0:T(8,128)(2,1)S(1)} %get-tuple-element.546), channel_id=1, source_target_pairs={{0,24},{4,28},{8,0},{12,4},{16,8},{20,12},{24,16},{28,20},{1,25},{... | collective-permute-start | bytes 1572872 | tf_op jit(solution)/shard_map/ppermute | solution.py:146
  720.9 22.5 %collective-permute-start.43 = (bf16[256,1024]{1,0:T(8,128)(2,1)S(1)}, bf16[256,1024]{1,0:T(8,128)(2,1)S(1)}, u32[]{:S(2)}, u32[]{:S(2)}) collective-permute-start(bf16[256,1024]{1,0:T(8,128)(2,1)S(1)} %copy-done.63), channel_id=1, source_target_pairs={{0,4},{4,0},{8,12},{12,8},{16,20},{20,16},{24,28},{28,24},{1,5},{5... | collective-permute-start | bytes 1572872 | tf_op jit(solution)/shard_map/ppermute | solution.py:142
  732.1 20.9 %collective-permute-start.38 = (bf16[256,1024]{1,0:T(8,128)(2,1)S(1)}, bf16[256,1024]{1,0:T(8,128)(2,1)S(1)}, u32[]{:S(2)}, u32[]{:S(2)}) collective-permute-start(bf16[256,1024]{1,0:T(8,128)(2,1)S(1)} %get-tuple-element.552), channel_id=1, source_target_pairs={{0,8},{4,12},{8,16},{12,20},{16,24},{20,28},{24,0},{28,4},{1,9},{5... | collective-permute-start | bytes 1572872 | tf_op jit(solution)/shard_map/ppermute | solution.py:146
  732.1 52.1 %collective-permute-start.40 = (bf16[256,1024]{1,0:T(8,128)(2,1)S(1)}, bf16[256,1024]{1,0:T(8,128)(2,1)S(1)}, u32[]{:S(2)}, u32[]{:S(2)}) collective-permute-start(bf16[256,1024]{1,0:T(8,128)(2,1)S(1)} %get-tuple-element.554), channel_id=1, source_target_pairs={{0,16},{4,20},{8,24},{12,28},{16,0},{20,4},{24,8},{28,12},{1,17},{... | collective-permute-start | bytes 1572872 | tf_op jit(solution)/shard_map/ppermute | solution.py:146
  732.5 64.9 %collective-permute-start.42 = (bf16[256,1024]{1,0:T(8,128)(2,1)S(1)}, bf16[256,1024]{1,0:T(8,128)(2,1)S(1)}, u32[]{:S(2)}, u32[]{:S(2)}) collective-permute-start(bf16[256,1024]{1,0:T(8,128)(2,1)S(1)} %get-tuple-element.553), channel_id=1, source_target_pairs={{0,24},{4,28},{8,0},{12,4},{16,8},{20,12},{24,16},{28,20},{1,25},{... | collective-permute-start | bytes 1572872 | tf_op jit(solution)/shard_map/ppermute | solution.py:146
  739.3 82.6 %collective-permute-start.59 = (bf16[1024,256]{1,0:T(8,128)(2,1)}, bf16[1024,256]{1,0:T(8,128)(2,1)}, u32[]{:S(2)}, u32[]{:S(2)}) collective-permute-start(bf16[1024,256]{1,0:T(8,128)(2,1)} %get-tuple-element.542), channel_id=1, source_target_pairs={{0,4},{4,0},{8,12},{12,8},{16,20},{20,16},{24,28},{28,24},{1,5},{5... | collective-permute-start | bytes 1572872 | tf_op jit(solution)/shard_map/ppermute | solution.py:142
  743.3 78.5 %collective-permute-start.54 = (bf16[1024,256]{1,0:T(8,128)(2,1)}, bf16[1024,256]{1,0:T(8,128)(2,1)}, u32[]{:S(2)}, u32[]{:S(2)}) collective-permute-start(bf16[1024,256]{1,0:T(8,128)(2,1)} %get-tuple-element.538), channel_id=1, source_target_pairs={{0,8},{4,12},{8,16},{12,20},{16,24},{20,28},{24,0},{28,4},{1,9},{5... | collective-permute-start | bytes 1572872 | tf_op jit(solution)/shard_map/ppermute | solution.py:146
  753.0 68.8 %collective-permute-start.56 = (bf16[1024,256]{1,0:T(8,128)(2,1)}, bf16[1024,256]{1,0:T(8,128)(2,1)}, u32[]{:S(2)}, u32[]{:S(2)}) collective-permute-start(bf16[1024,256]{1,0:T(8,128)(2,1)} %get-tuple-element.540), channel_id=1, source_target_pairs={{0,16},{4,20},{8,24},{12,28},{16,0},{20,4},{24,8},{28,12},{1,17},{... | collective-permute-start | bytes 1572872 | tf_op jit(solution)/shard_map/ppermute | solution.py:146
  784.2 37.7 %collective-permute-start.58 = (bf16[1024,256]{1,0:T(8,128)(2,1)}, bf16[1024,256]{1,0:T(8,128)(2,1)}, u32[]{:S(2)}, u32[]{:S(2)}) collective-permute-start(bf16[1024,256]{1,0:T(8,128)(2,1)} %get-tuple-element.539), channel_id=1, source_target_pairs={{0,24},{4,28},{8,0},{12,4},{16,8},{20,12},{24,16},{28,20},{1,25},{... | collective-permute-start | bytes 1572872 | tf_op jit(solution)/shard_map/ppermute | solution.py:146
  807.3 12.4 %collective-permute-start.44 = (bf16[2,8,64,258]{3,2,1,0:T(8,128)(2,1)S(1)}, bf16[2,8,64,258]{3,2,1,0:T(8,128)(2,1)S(1)}, u32[]{:S(2)}, u32[]{:S(2)}) collective-permute-start(bf16[2,8,64,258]{3,2,1,0:T(8,128)(2,1)S(1)} %fusion.86), channel_id=1, source_target_pairs={{0,1},{1,0},{2,3},{3,2},{4,5},{5,4},{6,7},{7,6},{8,9},{9,8},{10,11... | collective-permute-start | bytes 1585160 | tf_op jit(solution)/shard_map/ppermute | solution.py:161
  820.8 13.0 %collective-permute-start.45 = (bf16[8,64,258]{2,1,0:T(8,128)(2,1)}, bf16[8,64,258]{2,1,0:T(8,128)(2,1)S(1)}, u32[]{:S(2)}, u32[]{:S(2)}) collective-permute-start(bf16[8,64,258]{2,1,0:T(8,128)(2,1)} %fusion.91), channel_id=1, source_target_pairs={{0,2},{1,3},{2,0},{3,1},{4,6},{5,7},{6,4},{7,5},{8,10},{9,11},{10,... | collective-permute-start | bytes 792584 | tf_op jit(solution)/shard_map/ppermute | solution.py:165
  835.0 4.7 collective-permute-start.46
  835.7 4.9 collective-permute-start.48
  837.0 4.3 collective-permute-start.50
  837.8 14.7 %collective-permute-start.52 = (bf16[64,419]{1,0:T(8,128)(2,1)}, bf16[64,419]{1,0:T(8,128)(2,1)S(1)}, u32[]{:S(2)}, u32[]{:S(2)}) collective-permute-start(bf16[64,419]{1,0:T(8,128)(2,1)} %get-tuple-element.567), channel_id=1, source_target_pairs={{0,4},{4,0},{8,12},{12,8},{16,20},{20,16},{24,28},{28,24},{1,5},{5... | collective-permute-start | bytes 160904 | tf_op jit(solution)/shard_map/ppermute | solution.py:142
  842.1 10.5 %collective-permute-start.47 = (bf16[64,419]{1,0:T(8,128)(2,1)}, bf16[64,419]{1,0:T(8,128)(2,1)S(1)}, u32[]{:S(2)}, u32[]{:S(2)}) collective-permute-start(bf16[64,419]{1,0:T(8,128)(2,1)} %get-tuple-element.563), channel_id=1, source_target_pairs={{0,8},{4,12},{8,16},{12,20},{16,24},{20,28},{24,0},{28,4},{1,9},{5... | collective-permute-start | bytes 160904 | tf_op jit(solution)/shard_map/ppermute | solution.py:146
  846.8 5.8 collective-permute-start.49
  846.8 5.8 collective-permute-start.51
  (139 other events, 3082.7 us)
Sparse Core Ops, SparseCore 0:
  9.7 39.2 all-gather.2
  51.1 34.4 all-gather.4
  602.0 41.1 reduce-scatter.4
  645.7 44.5 reduce-scatter.2

commit v2 on v1

v2 whole, which is shorter than its diff:
```python
import functools
import math

import jax
import jax.numpy as jnp
from jax import lax
from jax.experimental import pallas as pl
from jax.experimental.pallas import tpu as pltpu
from jax.sharding import PartitionSpec as P

D = 2048
H = 64
P_SIZE = 64
NS = 128
KC = 4
BLK = 256


EPS = 1e-05
MOMENTUM = 0.9
DECAY = 0.0001
AVERAGE = 0.75
RATE_MATRIX = 0.02
RATE_VECTOR = 0.1
HIGHEST = lax.Precision.HIGHEST


def rounded(value):
    return lax.optimization_barrier(value.astype(jnp.bfloat16)).astype(jnp.float32)


def advance(weight, gradient, moment, average, rate):
    adjusted = gradient + DECAY * weight
    moment_next = MOMENTUM * moment + adjusted
    weight_next = weight - rate * (adjusted + MOMENTUM * moment_next)
    average_next = AVERAGE * average + (1.0 - AVERAGE) * weight_next
    return (weight_next, moment_next, average_next)


LANES = 128
FAR = -1e30
NT = (((1,), (1,)), ((), ()))
TN = (((0,), (0,)), ((), ()))


def dot32(first, second, dims=(((1,), (0,)), ((), ()))):
    return lax.dot_general(first, second, dims, preferred_element_type=jnp.float32)


def softplus(value):
    return jnp.maximum(value, 0.0) + jnp.log1p(jnp.exp(-jnp.abs(value)))


def triangle(upper):
    first = lax.broadcasted_iota(jnp.int32, (BLK, BLK), 0)
    second = lax.broadcasted_iota(jnp.int32, (BLK, BLK), 1)
    return first <= second if upper else first >= second


def filtered(window, taps, lanes):
    total = taps[KC : KC + 1, lanes] + taps[0:1, lanes] * window[5 : 5 + BLK, lanes]
    for offset in range(1, KC):
        total = total + taps[offset : offset + 1, lanes] * window[5 + offset : 5 + offset + BLK, lanes]
    return total


def step_parts(raw, table, heads):
    lane = lax.broadcasted_iota(jnp.int32, (BLK, LANES), 1)
    shifted = raw + table[0:1, :]
    rates = jnp.where(lane < heads, softplus(shifted), 0.0)
    decay = -jnp.exp(table[1:2, :])
    cumulated = jnp.dot(
        triangle(False).astype(jnp.float32),
        rates * decay,
        precision=HIGHEST,
        preferred_element_type=jnp.float32,
    )
    return shifted, rates, decay, cumulated


def spread_columns(value, out, heads):
    for head in range(heads):
        out[head] = jnp.broadcast_to(value[:, head : head + 1], (BLK, LANES))


def mixer_kernel(
    heads, opens, widths, v_ref, s_ref, tx, ts, table, mixed, entered,
    window, window_s, state, xs, cum_wide, rate_wide, cum_rows, rate_rows,
):
    block = pl.program_id(0)
    low = jnp.bfloat16

    @pl.when(opens[block] == 1)
    def _():
        window[0:8, :] = jnp.zeros_like(window[0:8, :])
        window_s[0:8, :] = jnp.zeros_like(window_s[0:8, :])
        state[...] = jnp.zeros_like(state)

    @pl.when(opens[block] != 1)
    def _():
        window[0:8, :] = window[BLK : BLK + 8, :]
        window_s[0:8, :] = window_s[BLK : BLK + 8, :]

    window[8 : 8 + BLK, :] = v_ref[...]
    window_s[8 : 8 + BLK, :] = s_ref[:, : 2 * NS]
    shared = filtered(window_s, ts, slice(None))
    shared = (shared * jax.nn.sigmoid(shared)).astype(low)
    maps_in, maps_out = shared[:, :NS], shared[:, NS:]
    maps_in_t = jnp.transpose(maps_in.astype(jnp.float32)).astype(low)
    _, rates, _, cumulated = step_parts(s_ref[:, 2 * NS :], table, heads)
    cum_rows[...] = jnp.transpose(cumulated)[: cum_rows.shape[0]]
    rate_rows[...] = jnp.transpose(rates)[: rate_rows.shape[0]]
    spread_columns(cumulated, cum_wide, heads)
    spread_columns(rates, rate_wide, heads)
    crossing = dot32(maps_out, maps_in, NT)
    width = widths[block]

    def pair(index, _):
        lanes = pl.ds(pl.multiple_of(index * LANES, LANES), LANES)
        pre = filtered(window, tx, lanes)
        values = (pre * jax.nn.sigmoid(pre)).astype(low)
        side = lax.broadcasted_iota(jnp.int32, (BLK, LANES), 1) < P_SIZE
        lower = triangle(False)
        cum_pair = jnp.where(side, cum_wide[2 * index], cum_wide[2 * index + 1])
        rate_pair = jnp.where(side, rate_wide[2 * index], rate_wide[2 * index + 1])
        now = state[:, lanes]
        entered[0, :, lanes] = now
        total = jnp.exp(cum_pair) * dot32(maps_out, now.astype(low))
        for half in range(2):
            head = 2 * index + half
            column = cum_wide[head]
            spread = jnp.concatenate([column, column], axis=1) - cum_rows[pl.ds(head, 1), :]
            decays = jnp.exp(jnp.where(lower, spread, FAR))
            mixing = (crossing * decays * rate_rows[pl.ds(head, 1), :]).astype(low)
            own = side if half == 0 else jnp.logical_not(side)
            total = total + dot32(mixing, jnp.where(own, values, jnp.zeros_like(values)))
        wide = values.astype(jnp.float32)
        total = total + tx[6:7, lanes] * wide
        row = lax.broadcasted_iota(jnp.int32, (1, LANES), 1)
        head_row = 2 * index + (row >= P_SIZE).astype(jnp.int32)
        used = (head_row * H < width * heads).astype(jnp.float32)
        mixed[:, lanes] = total * used
        last = cum_pair[BLK - 1 : BLK, :]
        ending = jnp.exp(last - cum_pair) * rate_pair
        state[:, lanes] = jnp.exp(last) * now + dot32(maps_in_t, (wide * ending).astype(low))
        return 0

    lax.fori_loop(0, heads // 2, pair, 0)


def mixer_back_kernel(
    heads, count, opens, v_ref, v_tail, s_ref, s_tail, tx, ts, table, ybar, entered,
    inner_low, small_low, tx_grad, ts_grad, table_grad,
    window, window_s, ahead, ahead_s, state_grad, cum_wide, rate_wide,
    cum_rows, z_rows, cross_grad, maps_grad, column_sum, outer_sum, rate_sum, last_sum,
):
    low = jnp.bfloat16
    step = pl.program_id(0)
    block = count - 1 - step
    opened = opens[block] == 1

    @pl.when(step == 0)
    def _():
        ahead[BLK : BLK + 8, :] = jnp.zeros_like(ahead[BLK : BLK + 8, :])
        ahead_s[BLK : BLK + 8, :] = jnp.zeros_like(ahead_s[BLK : BLK + 8, :])
        state_grad[...] = jnp.zeros_like(state_grad)
        tx_grad[...] = jnp.zeros_like(tx_grad)
        ts_grad[...] = jnp.zeros_like(ts_grad)
        table_grad[...] = jnp.zeros_like(table_grad)
        z_rows[...] = jnp.zeros_like(z_rows)

    @pl.when(opened)
    def _():
        window[0:8, :] = jnp.zeros_like(window[0:8, :])
        window_s[0:8, :] = jnp.zeros_like(window_s[0:8, :])

    @pl.when(jnp.logical_not(opened))
    def _():
        window[0:8, :] = v_tail[...]
        window_s[0:8, :] = s_tail[:, : 2 * NS]

    window[8 : 8 + BLK, :] = v_ref[...]
    window_s[8 : 8 + BLK, :] = s_ref[:, : 2 * NS]
    pre_s = filtered(window_s, ts, slice(None))
    share_s = jax.nn.sigmoid(pre_s)
    shared = (pre_s * share_s).astype(low)
    slope_s = share_s * (1.0 + pre_s * (1.0 - share_s))
    maps_in, maps_out = shared[:, :NS], shared[:, NS:]
    maps_out_t = jnp.transpose(maps_out.astype(jnp.float32)).astype(low)
    shifted, rates, decay, cumulated = step_parts(s_ref[:, 2 * NS :], table, heads)
    cum_rows[...] = jnp.transpose(cumulated)[: cum_rows.shape[0]]
    spread_columns(cumulated, cum_wide, heads)
    spread_columns(rates, rate_wide, heads)
    crossing = dot32(maps_in, maps_out, NT)
    for held in (cross_grad, maps_grad, column_sum, outer_sum, rate_sum, last_sum):
        held[...] = jnp.zeros_like(held)

    def pair(index, _):
        lanes = pl.ds(pl.multiple_of(index * LANES, LANES), LANES)
        pre = filtered(window, tx, lanes)
        share = jax.nn.sigmoid(pre)
        values = (pre * share).astype(low)
        slope = share * (1.0 + pre * (1.0 - share))
        lane = lax.broadcasted_iota(jnp.int32, (BLK, LANES), 1)
        side = lane < P_SIZE
        upper = triangle(True)
        cum_pair = jnp.where(side, cum_wide[2 * index], cum_wide[2 * index + 1])
        rate_pair = jnp.where(side, rate_wide[2 * index], rate_wide[2 * index + 1])
        back = ybar[:, lanes]
        back_low = back.astype(low)
        wide = values.astype(jnp.float32)
        now = entered[0, :, lanes]
        now_low = now.astype(low)
        after = state_grad[:, lanes]
        after_low = after.astype(low)
        grown = jnp.exp(cum_pair)
        last = cum_pair[BLK - 1 : BLK, :]
        total_decay = jnp.exp(last)
        ending = jnp.exp(last - cum_pair) * rate_pair
        outer = dot32(maps_out, now_low)
        inward = dot32(maps_in, after_low)
        back_grown = back * grown
        back_grown_low = back_grown.astype(low)
        maps_grad[:, NS:] += dot32(back_grown_low, now_low, NT)
        maps_grad[:, :NS] += dot32((wide * ending).astype(low), after_low, NT)
        state_grad[:, lanes] = total_decay * after + dot32(maps_out_t, back_grown_low)
        grad = ending * inward + tx[6:7, lanes] * back
        pick = (
            lax.broadcasted_iota(jnp.int32, (LANES, LANES), 1)
            == 2 * index + (lax.broadcasted_iota(jnp.int32, (LANES, LANES), 0) >= P_SIZE).astype(jnp.int32)
        ).astype(low)

        def to_heads(value):
            high = value.astype(low)
            rest = (value - high.astype(jnp.float32)).astype(low)
            return dot32(high, pick) + dot32(rest, pick)

        outer_sum[...] += to_heads(back_grown * outer)
        rate_sum[...] += to_heads(wide * inward)
        kept = jnp.sum(total_decay * after * now, axis=0, keepdims=True)
        last_sum[...] += to_heads(jnp.broadcast_to(kept, (8, LANES)))
        tx_grad[6:7, lanes] += jnp.sum(back * wide, axis=0, keepdims=True)
        zero = jnp.zeros_like(values)
        for half in range(2):
            head = 2 * index + half
            own = side if half == 0 else jnp.logical_not(side)
            column = cum_wide[head]
            rate = rate_wide[head]
            spread = cum_rows[pl.ds(head, 1), :] - jnp.concatenate([column, column], axis=1)
            decays = jnp.exp(jnp.where(upper, spread, FAR))
            weighted = decays * jnp.concatenate([rate, rate], axis=1)
            products = dot32(jnp.where(own, values, zero), back_low, NT)
            summed = jnp.sum(products * (crossing * decays), axis=1, keepdims=True)
            column_sum[...] += jnp.where(lane == head, summed, 0.0)
            mixing = crossing * weighted
            z_rows[pl.ds(head, 1), :] = jnp.sum(products * mixing, axis=0, keepdims=True)
            cross_grad[...] += products * weighted
            grad = grad + dot32(mixing.astype(low), jnp.where(own, back_low, zero))
        back_pre = grad * slope
        ahead[0:BLK, lanes] = back_pre
        spent = tx[KC - 1 : KC, lanes] * back_pre
        for offset in range(1, KC):
            spent = spent + tx[KC - 1 - offset : KC - offset, lanes] * ahead[offset : offset + BLK, lanes]
        inner_low[:, lanes] = spent.astype(low)
        for position in range(KC):
            tx_grad[position : position + 1, lanes] += jnp.sum(
                back_pre * window[5 + position : 5 + position + BLK, lanes], axis=0, keepdims=True
            )
        tx_grad[KC : KC + 1, lanes] += jnp.sum(back_pre, axis=0, keepdims=True)
        return 0

    lax.fori_loop(0, heads // 2, pair, 0)
    cross = cross_grad[...]
    cross_low = cross.astype(low)
    maps_grad[:, :NS] += dot32(cross_low, maps_out)
    maps_grad[:, NS:] += dot32(jnp.transpose(cross).astype(low), maps_in)
    back_pre_s = maps_grad[...] * slope_s
    ahead_s[0:BLK, :] = back_pre_s
    spent_s = ts[KC - 1 : KC, :] * back_pre_s
    for offset in range(1, KC):
        spent_s = spent_s + ts[KC - 1 - offset : KC - offset, :] * ahead_s[offset : offset + BLK, :]
    small_low[:, : 2 * NS] = spent_s.astype(low)
    for position in range(KC):
        ts_grad[position : position + 1, :] += jnp.sum(
            back_pre_s * window_s[5 + position : 5 + position + BLK, :], axis=0, keepdims=True
        )
    ts_grad[KC : KC + 1, :] += jnp.sum(back_pre_s, axis=0, keepdims=True)
    lane = lax.broadcasted_iota(jnp.int32, (BLK, LANES), 1)
    falling = jnp.exp(cumulated[BLK - 1 : BLK, :] - cumulated)
    ended = rate_sum[...] * falling
    ended_rate = ended * rates
    own_sum = column_sum[...]
    cum_grad = jnp.transpose(z_rows[...]) + outer_sum[...] - rates * own_sum - ended_rate
    final = last_sum[0:1, :] + jnp.sum(ended_rate, axis=0, keepdims=True)
    place = lax.broadcasted_iota(jnp.int32, (BLK, LANES), 0)
    cum_grad = cum_grad + jnp.where(place == BLK - 1, final, 0.0)
    log_grad = jnp.dot(
        triangle(True).astype(jnp.float32),
        cum_grad,
        precision=HIGHEST,
        preferred_element_type=jnp.float32,
    )
    rate_grad = own_sum + ended + decay * log_grad
    raw_grad = jnp.where(lane < heads, rate_grad * jax.nn.sigmoid(shifted), 0.0)
    small_low[:, 2 * NS :] = raw_grad.astype(low)
    table_grad[0:1, :] += jnp.sum(raw_grad, axis=0, keepdims=True)
    table_grad[1:2, :] += decay * jnp.sum(rates * log_grad, axis=0, keepdims=True)

    @pl.when(opened)
    def _():
        ahead[BLK : BLK + 8, :] = jnp.zeros_like(ahead[BLK : BLK + 8, :])
        ahead_s[BLK : BLK + 8, :] = jnp.zeros_like(ahead_s[BLK : BLK + 8, :])
        state_grad[...] = jnp.zeros_like(state_grad)

    @pl.when(jnp.logical_not(opened))
    def _():
        ahead[BLK : BLK + 8, :] = ahead[0:8, :]
        ahead_s[BLK : BLK + 8, :] = ahead_s[0:8, :]


VMEM_LIMIT = 56 * 1024 * 1024


def mixer(opens, widths, inner, small, tx, ts, table, interpret=False):
    tokens, channels = inner.shape
    heads, count = channels // P_SIZE, tokens // BLK
    whole = lambda rows, columns: pl.BlockSpec((rows, columns), lambda i, *_: (0, 0))
    rows = lambda columns: pl.BlockSpec((BLK, columns), lambda i, *_: (i, 0))
    wide = pltpu.VMEM((heads, BLK, LANES), jnp.float32)
    row_pad = -(-heads // 8) * 8
    return pl.pallas_call(
        functools.partial(mixer_kernel, heads),
        out_shape=(
            jax.ShapeDtypeStruct((tokens, channels), jnp.float32),
            jax.ShapeDtypeStruct((count, NS, channels), jnp.float32),
        ),
        grid_spec=pltpu.PrefetchScalarGridSpec(
            num_scalar_prefetch=2,
            grid=(count,),
            in_specs=[rows(channels), rows(3 * LANES), whole(8, channels), whole(8, 2 * NS), whole(8, LANES)],
            out_specs=[rows(channels), pl.BlockSpec((1, NS, channels), lambda i, *_: (i, 0, 0))],
            scratch_shapes=[
                pltpu.VMEM((BLK + 8, channels), jnp.float32),
                pltpu.VMEM((BLK + 8, 2 * NS), jnp.float32),
                pltpu.VMEM((NS, channels), jnp.float32),
                pltpu.VMEM((8, LANES), jnp.bfloat16),
                wide,
                wide,
                pltpu.VMEM((row_pad, BLK), jnp.float32),
                pltpu.VMEM((row_pad, BLK), jnp.float32),
            ],
        ),
        compiler_params=pltpu.CompilerParams(vmem_limit_bytes=VMEM_LIMIT),
        name="mixer",
        interpret=interpret,
    )(opens, widths, inner, small, tx, ts, table)


def mixer_back(opens, inner, small, tx, ts, table, ybar, entered, interpret=False):
    tokens, channels = inner.shape
    heads, count = channels // P_SIZE, tokens // BLK
    per = BLK // 8
    turn = lambda i: count - 1 - i
    whole = lambda rows, columns: pl.BlockSpec((rows, columns), lambda i, *_: (0, 0))
    rows = lambda columns: pl.BlockSpec((BLK, columns), lambda i, *_: (turn(i), 0))
    tail = lambda columns: pl.BlockSpec(
        (8, columns), lambda i, *_: (jnp.maximum(turn(i) * per - 1, 0), 0)
    )
    wide = pltpu.VMEM((heads, BLK, LANES), jnp.float32)
    row_pad = -(-heads // 8) * 8
    column = pltpu.VMEM((BLK, LANES), jnp.float32)
    return pl.pallas_call(
        functools.partial(mixer_back_kernel, heads, count),
        out_shape=(
            jax.ShapeDtypeStruct((tokens, channels), jnp.bfloat16),
            jax.ShapeDtypeStruct((tokens, 3 * LANES), jnp.bfloat16),
            jax.ShapeDtypeStruct((8, channels), jnp.float32),
            jax.ShapeDtypeStruct((8, 2 * NS), jnp.float32),
            jax.ShapeDtypeStruct((8, LANES), jnp.float32),
        ),
        grid_spec=pltpu.PrefetchScalarGridSpec(
            num_scalar_prefetch=1,
            grid=(count,),
            in_specs=[
                rows(channels),
                tail(channels),
                rows(3 * LANES),
                tail(3 * LANES),
                whole(8, channels),
                whole(8, 2 * NS),
                whole(8, LANES),
                rows(channels),
                pl.BlockSpec((1, NS, channels), lambda i, *_: (turn(i), 0, 0)),
            ],
            out_specs=[rows(channels), rows(3 * LANES), whole(8, channels), whole(8, 2 * NS), whole(8, LANES)],
            scratch_shapes=[
                pltpu.VMEM((BLK + 8, channels), jnp.float32),
                pltpu.VMEM((BLK + 8, 2 * NS), jnp.float32),
                pltpu.VMEM((BLK + 8, channels), jnp.float32),
                pltpu.VMEM((BLK + 8, 2 * NS), jnp.float32),
                pltpu.VMEM((NS, channels), jnp.float32),
                wide,
                wide,
                pltpu.VMEM((row_pad, BLK), jnp.float32),
                pltpu.VMEM((LANES, BLK), jnp.float32),
                pltpu.VMEM((BLK, BLK), jnp.float32),
                pltpu.VMEM((BLK, 2 * NS), jnp.float32),
                column,
                column,
                column,
                pltpu.VMEM((8, LANES), jnp.float32),
            ],
        ),
        compiler_params=pltpu.CompilerParams(vmem_limit_bytes=VMEM_LIMIT),
        name="mixer_back",
        interpret=interpret,
    )(opens, inner, inner, small, small, tx, ts, table, ybar, entered)


Y_SIZE = 2


def swap_pairs(size):
    return [(i, i ^ 1) for i in range(size)]


def gather_dp(shard, axis):
    count = lax.axis_size("dp")
    if count != 8:
        return lax.all_gather(shard, "dp", axis=axis, tiled=True)
    rows = count // Y_SIZE
    index = lax.axis_index("dp")
    row, column = index // Y_SIZE, index % Y_SIZE
    width = shard.shape[axis]
    held = {0: shard}
    for shift in range(1, rows):
        perm = [(i, (i + shift * Y_SIZE) % count) for i in range(count)]
        held[shift] = lax.ppermute(shard, "dp", perm)
    shape = list(shard.shape)
    shape[axis] = width * count
    full = jnp.zeros(shape, shard.dtype)
    for shift in range(rows):
        other = lax.ppermute(held[shift], "dp", swap_pairs(count))
        base = ((row - shift) % rows) * Y_SIZE
        full = lax.dynamic_update_slice_in_dim(full, held[shift], (base + column) * width, axis)
        full = lax.dynamic_update_slice_in_dim(full, other, (base + 1 - column) * width, axis)
    return full


def reduce_dp(value, axis):
    count = lax.axis_size("dp")
    low = jnp.bfloat16
    if count != 8:
        return lax.psum_scatter(
            value.astype(low), "dp", scatter_dimension=axis, tiled=True
        ).astype(jnp.float32)
    rows = count // Y_SIZE
    index = lax.axis_index("dp")
    row, column = index // Y_SIZE, index % Y_SIZE
    width = value.shape[axis] // count
    total = None
    for shift in (1, 2, 3, 0):
        base = ((row + shift) % rows) * Y_SIZE
        away = lax.dynamic_slice_in_dim(value, (base + 1 - column) * width, width, axis)
        kept = lax.dynamic_slice_in_dim(value, (base + column) * width, width, axis)
        came = lax.ppermute(away.astype(low), "dp", swap_pairs(count))
        pair = kept + came.astype(jnp.float32)
        if shift:
            perm = [(i, (i + shift * Y_SIZE) % count) for i in range(count)]
            pair = lax.ppermute(pair.astype(low), "dp", perm).astype(jnp.float32)
        total = pair if total is None else total + pair
    return total


def reduce_head(value):
    count = lax.axis_size("head")
    low = jnp.bfloat16
    if count != 4:
        return lax.psum_scatter(value, "head", scatter_dimension=0, tiled=False)
    index = lax.axis_index("head")
    side, core = index // 2, index % 2
    both = value.reshape(2, 2, *value.shape[1:])
    away = lax.dynamic_index_in_dim(both, 1 - core, 1, keepdims=False)
    kept = lax.dynamic_index_in_dim(both, core, 1, keepdims=False)
    came = lax.ppermute(away.astype(low), "head", swap_pairs(count))
    pair = kept + came.astype(jnp.float32)
    away = lax.dynamic_index_in_dim(pair, 1 - side, 0, keepdims=False)
    kept = lax.dynamic_index_in_dim(pair, side, 0, keepdims=False)
    came = lax.ppermute(away.astype(low), "head", [(i, (i + 2) % 4) for i in range(count)])
    return kept + came.astype(jnp.float32)


def gather_head(piece, axis):
    count = lax.axis_size("head")
    if count != 4:
        return lax.all_gather(piece, "head", axis=axis, tiled=True)
    index = lax.axis_index("head")
    width = piece.shape[axis]
    near = lax.ppermute(piece, "head", swap_pairs(count))
    first = index % 2 == 0
    pair = jnp.concatenate(
        [jnp.where(first, piece, near), jnp.where(first, near, piece)], axis=axis
    )
    far = lax.ppermute(pair, "head", [(i, (i + 2) % 4) for i in range(count)])
    lower = index < 2
    return jnp.concatenate(
        [jnp.where(lower, pair, far), jnp.where(lower, far, pair)], axis=axis
    )


def body(
    inputs,
    cotangent,
    token_valid,
    block_opens,
    block_widths,
    weight_inner,
    weight_step,
    weight_output,
    weight_state,
    norm_gain,
    channel_table,
    head_table,
    state_filter,
    momentum_inner,
    momentum_step,
    momentum_output,
    momentum_state,
    momentum_gain,
    momentum_channel,
    momentum_head,
    momentum_filter,
    average_inner,
    average_step,
    average_output,
    average_state,
    average_gain,
    average_channel,
    average_head,
    average_filter,
):
    low = jnp.bfloat16
    full_type = jnp.float32
    count_dp = lax.axis_size("dp")
    count_head = lax.axis_size("head")
    tokens, channels = inputs.shape[0], weight_inner.shape[2]
    heads_own = weight_step.shape[1]
    rows_all, state_rows = weight_state.shape[0], state_filter.shape[0]
    width_state = weight_state.shape[1]
    filter_block = jnp.pad(state_filter.astype(low), ((0, rows_all - state_rows), (0, 0)))
    shared_piece = jnp.concatenate(
        [weight_state.astype(low), norm_gain.astype(low)[:, None], filter_block], axis=1
    )
    shared_rows = gather_head(shared_piece, 0)
    small_rows = jnp.concatenate(
        [shared_rows[:, :width_state], weight_step.astype(low), shared_rows[:, width_state:]],
        axis=1,
    )
    small_rows = jnp.pad(small_rows, ((0, 0), (0, width_state + LANES - small_rows.shape[1])))
    inner_value = gather_dp(weight_inner[:, 1].astype(low), 0)
    small_full = gather_dp(small_rows, 0)
    inner_gate = gather_dp(weight_inner[:, 0].astype(low), 0)
    output_full = gather_dp(weight_output.astype(low), 1)
    at_gain = width_state + heads_own
    gain_full = small_full[:, at_gain]
    filter_full = small_full[:, at_gain + 1 : at_gain + 1 + KC + 1]
    filter_full = filter_full.reshape(-1, rows_all, KC + 1)[:, :state_rows].reshape(-1, KC + 1)
    channel_used = rounded(channel_table)
    head_values = rounded(head_table)
    gathered = lax.all_gather(inputs, "head", axis=1, tiled=True)
    masked = cotangent * token_valid.astype(low)[:, None]
    shard_piece = lax.all_gather(masked, "head", axis=1, tiled=True)
    tokens_full = gathered.astype(full_type)
    inverse = lax.rsqrt(jnp.mean(tokens_full * tokens_full, axis=1) + EPS)
    gain_float = gain_full.astype(full_type)
    normed = (tokens_full * inverse[:, None] * gain_float[None, :]).astype(low)
    inner_x = jnp.dot(normed, inner_value, preferred_element_type=full_type)
    small_x = jnp.dot(normed, small_full, preferred_element_type=full_type)
    widths = jnp.repeat(block_widths, BLK)
    channel_head = jnp.arange(channels) // P_SIZE
    used = (channel_head[None, :] * H < widths[:, None] * heads_own).astype(full_type)
    norm_counts = widths.astype(full_type) * P_SIZE
    valid_rows = token_valid.astype(full_type)
    gate_gain = channel_used[KC + 1]
    skip_wide = jnp.repeat(head_values[2], P_SIZE)
    taps_x = jnp.concatenate(
        [channel_used, skip_wide[None, :], jnp.zeros((1, channels), full_type)], axis=0
    )
    taps_s = jnp.pad(filter_full.astype(full_type).T, ((0, 8 - KC - 1), (0, 0)))
    table = jnp.pad(head_values, ((0, 5), (0, LANES - heads_own)))
    mixed, entered = mixer(block_opens, block_widths, inner_x, small_x, taps_x, taps_s, table)
    gate_values = jnp.dot(normed, inner_gate, preferred_element_type=full_type)
    gate_share = jax.nn.sigmoid(gate_values)
    gate_silu = gate_values * gate_share
    gated = mixed * gate_silu
    local_sq = jnp.sum(gated * gated, axis=1)
    grad_normal = jnp.einsum(
        "tw,cw->tc", shard_piece, output_full, preferred_element_type=full_type
    )
    grad_gained = grad_normal * gate_gain[None, :]
    local_dot = jnp.sum(grad_gained * gated, axis=1)
    total_sq, total_dot = lax.psum(jnp.stack([local_sq, local_dot]), "head")
    norm_scale = lax.rsqrt(total_sq / norm_counts + EPS)
    projected = (gated * norm_scale[:, None] * gate_gain[None, :]).astype(low)
    partial_out = jnp.dot(projected, output_full, preferred_element_type=full_type)
    branch = lax.psum_scatter(
        partial_out.astype(low), "head", scatter_dimension=1, tiled=True
    ).astype(full_type)
    own_inputs = inputs.astype(full_type)
    layer_output = (own_inputs + valid_rows[:, None] * branch).astype(low)
    block_grad = jnp.einsum("tc,tw->cw", projected, shard_piece, preferred_element_type=full_type)
    grad_gate_gain = jnp.sum(grad_normal * gated * norm_scale[:, None], axis=0)
    scale_back = norm_scale * norm_scale * norm_scale / norm_counts * total_dot
    back_gated = grad_gained * norm_scale[:, None] - gated * scale_back[:, None]
    ybar = back_gated * gate_silu * used
    gate_slope = gate_share * (1.0 + gate_values * (1.0 - gate_share))
    gate_low = (back_gated * mixed * gate_slope).astype(low)
    inner_low, small_low, taps_grad, state_taps, table_grad = mixer_back(
        block_opens, inner_x, small_x, taps_x, taps_s, table, ybar, entered
    )
    grad_gate_w = jnp.einsum("td,tc->dc", normed, gate_low, preferred_element_type=full_type)
    grad_inner_w = jnp.einsum("td,tc->dc", normed, inner_low, preferred_element_type=full_type)
    grad_small = jnp.einsum("td,ts->ds", normed, small_low, preferred_element_type=full_type)
    grad_normed = jnp.einsum("tc,dc->td", gate_low, inner_gate, preferred_element_type=full_type)
    grad_normed = grad_normed + jnp.einsum(
        "tc,dc->td", inner_low, inner_value, preferred_element_type=full_type
    )
    grad_normed = grad_normed + jnp.einsum(
        "ts,ds->td", small_low, small_full, preferred_element_type=full_type
    )
    own_grad = lax.psum_scatter(
        grad_normed.astype(low), "head", scatter_dimension=1, tiled=True
    ).astype(full_type)
    own_width = inputs.shape[1]
    start_column = lax.axis_index("head") * own_width
    own_gain = lax.dynamic_slice_in_dim(gain_float, start_column, own_width)
    scaled = own_grad * own_gain[None, :]
    row_part = jnp.sum(scaled * own_inputs, axis=1)
    grad_gain_own = jnp.sum(own_grad * own_inputs * inverse[:, None], axis=0)
    row_total = lax.psum(row_part, "head")
    inverse_cube = inverse * inverse * inverse
    grad_input = (
        cotangent.astype(full_type)
        + inverse[:, None] * scaled
        - own_inputs * (inverse_cube * row_total / D)[:, None]
    )
    grad_gain_full = lax.dynamic_update_slice_in_dim(
        jnp.zeros((D,), full_type), grad_gain_own, start_column, 0
    )
    grad_channel = jnp.concatenate([taps_grad[: KC + 1], grad_gate_gain[None, :]], axis=0)
    grad_skip = jnp.sum(taps_grad[KC + 2].reshape(heads_own, P_SIZE), axis=1)
    grad_head = jnp.concatenate([table_grad[:2, :heads_own], grad_skip[None, :]], axis=0)
    grad_filter = state_taps[: KC + 1].T
    output_reduced = reduce_dp(block_grad, 1)
    gate_reduced = reduce_dp(grad_gate_w, 0)
    inner_reduced = reduce_dp(grad_inner_w, 0)
    inner_reduced = jnp.stack([gate_reduced, inner_reduced], axis=1)
    filter_part = jnp.pad(
        grad_filter.reshape(count_dp, count_head, state_rows * (KC + 1)),
        ((0, 0), (0, 0), (0, rows_all - state_rows * (KC + 1))),
    ).reshape(D, 1)
    shared_part = jnp.concatenate(
        [grad_small[:, :width_state], grad_gain_full[:, None], filter_part], axis=1
    ).reshape(count_dp, count_head, rows_all, width_state + 2)
    shared_own = reduce_head(jnp.swapaxes(shared_part, 0, 1))
    grad_step = grad_small[:, width_state : width_state + heads_own]
    table_part = jnp.concatenate([grad_channel.reshape(-1), grad_head.reshape(-1)])
    table_width = -(-table_part.shape[0] // rows_all)
    table_part = jnp.pad(table_part, (0, table_width * rows_all - table_part.shape[0]))
    table_part = jnp.broadcast_to(
        table_part.reshape(1, rows_all, table_width), (count_dp, rows_all, table_width)
    )
    step_part = grad_step.reshape(count_dp, rows_all, -1)
    small_part = jnp.concatenate([shared_own, step_part, table_part], axis=2)
    small_own = reduce_dp(small_part.reshape(count_dp * rows_all, -1), 0)
    state_reduced = small_own[:, :width_state]
    gain_reduced = small_own[:, width_state]
    filter_reduced = small_own[: state_rows * (KC + 1), width_state + 1].reshape(state_rows, KC + 1)
    at = width_state + 2
    step_reduced = small_own[:, at : at + step_part.shape[2]].reshape(-1, heads_own)
    table_own = small_own[:, at + step_part.shape[2] :].reshape(-1)
    channel_size = grad_channel.shape[0] * grad_channel.shape[1]
    channel_reduced = table_own[:channel_size].reshape(grad_channel.shape)
    head_reduced = table_own[channel_size : channel_size + grad_head.size].reshape(grad_head.shape)
    total_tokens = inputs.shape[0] * lax.axis_size("dp")
    matrix_rate = RATE_MATRIX / math.sqrt(total_tokens)
    vector_rate = RATE_VECTOR / math.sqrt(total_tokens)
    new_inner = advance(weight_inner, inner_reduced, momentum_inner, average_inner, matrix_rate)
    new_step = advance(weight_step, step_reduced, momentum_step, average_step, matrix_rate)
    new_output = advance(
        weight_output, output_reduced, momentum_output, average_output, matrix_rate
    )
    new_state = advance(weight_state, state_reduced, momentum_state, average_state, matrix_rate)
    new_gain = advance(norm_gain, gain_reduced, momentum_gain, average_gain, vector_rate)
    new_channel = advance(
        channel_table, channel_reduced, momentum_channel, average_channel, vector_rate
    )
    new_head = advance(head_table, head_reduced, momentum_head, average_head, vector_rate)
    new_filter = advance(state_filter, filter_reduced, momentum_filter, average_filter, vector_rate)
    return (
        layer_output,
        grad_input,
        new_inner[0],
        new_inner[1],
        new_inner[2],
        new_step[0],
        new_step[1],
        new_step[2],
        new_output[0],
        new_output[1],
        new_output[2],
        new_state[0],
        new_state[1],
        new_state[2],
        new_gain[0],
        new_gain[1],
        new_gain[2],
        new_channel[0],
        new_channel[1],
        new_channel[2],
        new_head[0],
        new_head[1],
        new_head[2],
        new_filter[0],
        new_filter[1],
        new_filter[2],
    )


def solution(mesh):
    in_specs = (
        P("dp", "head"),
        P("dp", "head"),
        P("dp"),
        P("dp"),
        P("dp"),
        P("dp", None, "head"),
        P("dp", "head"),
        P("head", "dp"),
        P(("dp", "head"), None),
        P(("dp", "head")),
        P(None, "head"),
        P(None, "head"),
        P(("dp", "head"), None),
        P("dp", None, "head"),
        P("dp", "head"),
        P("head", "dp"),
        P(("dp", "head"), None),
        P(("dp", "head")),
        P(None, "head"),
        P(None, "head"),
        P(("dp", "head"), None),
        P("dp", None, "head"),
        P("dp", "head"),
        P("head", "dp"),
        P(("dp", "head"), None),
        P(("dp", "head")),
        P(None, "head"),
        P(None, "head"),
        P(("dp", "head"), None),
    )
    out_specs = (
        P("dp", "head"),
        P("dp", "head"),
        P("dp", None, "head"),
        P("dp", None, "head"),
        P("dp", None, "head"),
        P("dp", "head"),
        P("dp", "head"),
        P("dp", "head"),
        P("head", "dp"),
        P("head", "dp"),
        P("head", "dp"),
        P(("dp", "head"), None),
        P(("dp", "head"), None),
        P(("dp", "head"), None),
        P(("dp", "head")),
        P(("dp", "head")),
        P(("dp", "head")),
        P(None, "head"),
        P(None, "head"),
        P(None, "head"),
        P(None, "head"),
        P(None, "head"),
        P(None, "head"),
        P(("dp", "head"), None),
        P(("dp", "head"), None),
        P(("dp", "head"), None),
    )
    return jax.shard_map(body, mesh=mesh, in_specs=in_specs, out_specs=out_specs, check_vma=False)
```

time: 878 us -> 679 us (0.77)
  matrix products: 197 us -> 89.3 us
  other arithmetic: 155 us -> 57.2 us
  local copies, waits for them, and re-layouts: 146 us -> 76.2 us
  Pallas kernels: 0 us -> 68.2 us
  waiting for transfers between devices: 205 us -> 240 us
  starting transfers between devices: 128 us -> 111 us
    dot_general x26 -> x11, matrix products: 185 us -> 75.3 us  [the longest x1 10.7 us: body(): jnp.dot(projected, output_full, preferred_element_type=full_type)]
    pallas_call x0 -> x2, Pallas kernels: none -> 68.2 us  [the longest x1 43.4 us: mixer_back(): pl.pallas_call(functools.partial(mixer_back_kernel, heads, count), out_sh...]
    reduce_sum x12 -> x1, other arithmetic: 44.5 us -> 0.12 us  [body(): grad_skip = jnp.sum(taps_grad[KC + 2].reshape(heads_own, P_SIZE), axis=1)]
    reshape x20 -> x0, local copies, waits for them, and re-layouts: 21.2 us -> none  [the longest x2 6.4 us: state_mixer(): values = signal_x.reshape(blocks_here, BLK, heads_here, P_SIZE)]
    another operation x7 -> x1, other arithmetic: 20 us -> 0.01 us  [body(): total_sq, total_dot = lax.psum(jnp.stack([local_sq, local_dot]), 'head')]
    mul x9 -> x5, other arithmetic: 20.5 us -> 1.2 us  [the longest x1 1.17 us: body(): masked = cotangent * token_valid.astype(low)[:, None]]
    unnamed x290 -> x108, local copies, waits for them, and re-layouts: 35.9 us -> 18.9 us
    ppermute x12, waiting for transfers between devices: 18.7 us -> 33.6 us  [reduce_dp(): pair = lax.ppermute(pair.astype(low), 'dp', perm).astype(jnp.float32)]
  transfers between devices with their start and end apart: 64 -> 64, of which waited for: 25 -> 29; matrix products, arithmetic and copies ran while one was open for 29% -> 24% of each run, Pallas kernels for 0% -> 4%
where the time goes in v2:
time: 679 us; the launch traced here: 670 us
  waiting for transfers between devices  240 us (35%)
  starting transfers between devices  111 us (16%)
  matrix products  89.3 us (13%)
  local copies, waits for them, and re-layouts  76.2 us (11%)
  Pallas kernels  68.2 us (10%)
  other arithmetic  57.2 us (8%)
  between operations  15.7 us (2%)
  blocking collectives  11.9 us (2%)
    ppermute x16, waiting for transfers between devices, reduce_dp(): came = lax.ppermute(away.astype(low), 'dp', swap_pairs(count))  78.4 us
    ppermute x12, waiting for transfers between devices, gather_dp(): held[shift] = lax.ppermute(shard, 'dp', perm)  69.9 us
    ppermute x16, waiting for transfers between devices, gather_dp(): other = lax.ppermute(held[shift], 'dp', swap_pairs(count))  52.5 us
    ppermute x12, starting transfers between devices, gather_dp(): held[shift] = lax.ppermute(shard, 'dp', perm)  45 us
    pallas_call x1, Pallas kernels, mixer_back(): pl.pallas_call(functools.partial(mixer_back_kernel, heads, count), out_sh...  43.4 us
    ppermute x12, waiting for transfers between devices, reduce_dp(): pair = lax.ppermute(pair.astype(low), 'dp', perm).astype(jnp.float32)  33.6 us
    ppermute x12, starting transfers between devices, reduce_dp(): pair = lax.ppermute(pair.astype(low), 'dp', perm).astype(jnp.float32)  31.7 us
    pallas_call x1, Pallas kernels, mixer(): pl.pallas_call(functools.partial(mixer_kernel, heads), out_shape=(jax.Sha...  24.8 us
  transfers between devices with their start and end apart: 64, of which 29 were waited for; matrix products, arithmetic and copies ran while one was open for 24% of the time, Pallas kernels for 4%

profile of v2, /device:TPU:0, one launch (start us, length us, event | category | flops | bytes accessed | tf_op | source)
XLA Modules:
  0.0 670.1 jit_solution(5305815179850573471)
XLA Ops:
  11.2 3.0 collective-permute-start.16
  16.4 2.6 broadcast.143.clone
  19.9 2.6 broadcast.143.clone.1
  23.6 2.5 broadcast_in_dim.56
  30.3 5.1 collective-permute-done.1
  37.8 2.6 collective-permute-start.5
  42.2 3.6 collective-permute-done.3
  46.4 7.2 %collective-permute-start.17 = (bf16[256,1024]{1,0:T(8,128)(2,1)}, bf16[256,1024]{1,0:T(8,128)(2,1)}, u32[]{:S(2)}, u32[]{:S(2)}) collective-permute-start(bf16[256,1024]{1,0:T(8,128)(2,1)} %get-tuple-element.182), channel_id=1, source_target_pairs={{0,8},{4,12},{8,16},{12,20},{16,24},{20,28},{24,0},{28,4},{1,9},{5... | collective-permute-start | bytes 1572872 | tf_op jit(solution)/shard_map/ppermute | solution.py:438
  62.3 10.6 %collective-permute-start.19 = (bf16[256,1024]{1,0:T(8,128)(2,1)}, bf16[256,1024]{1,0:T(8,128)(2,1)}, u32[]{:S(2)}, u32[]{:S(2)}) collective-permute-start(bf16[256,1024]{1,0:T(8,128)(2,1)} %get-tuple-element.182), channel_id=1, source_target_pairs={{0,16},{4,20},{8,24},{12,28},{16,0},{20,4},{24,8},{28,12},{1,17},{... | collective-permute-start | bytes 1572872 | tf_op jit(solution)/shard_map/ppermute | solution.py:438
  76.5 5.3 collective-permute-start.10
  86.2 32.3 %collective-permute-done.19 = bf16[256,1024]{1,0:T(8,128)(2,1)} collective-permute-done((bf16[256,1024]{1,0:T(8,128)(2,1)}, bf16[256,1024]{1,0:T(8,128)(2,1)}, u32[]{:S(2)}, u32[]{:S(2)}) %collective-permute-start.19) | collective-permute-done | bytes 524320 | tf_op jit(solution)/shard_map/ppermute | solution.py:438
  130.5 3.1 collective-permute-done.18
  136.3 2.4 collective-permute-start.14
  138.7 29.4 %collective-permute-done.12 = bf16[256,1024]{1,0:T(8,128)(2,1)S(1)} collective-permute-done((bf16[256,1024]{1,0:T(8,128)(2,1)}, bf16[256,1024]{1,0:T(8,128)(2,1)S(1)}, u32[]{:S(2)}, u32[]{:S(2)}) %collective-permute-start.12) | collective-permute-done | bytes 524320 | tf_op jit(solution)/shard_map/ppermute | solution.py:438
  168.2 13.3 %collective-permute-start.28 = (bf16[1024,256]{1,0:T(8,128)(2,1)S(1)}, bf16[1024,256]{1,0:T(8,128)(2,1)S(1)}, u32[]{:S(2)}, u32[]{:S(2)}) collective-permute-start(bf16[1024,256]{1,0:T(8,128)(2,1)S(1)} %get-tuple-element.147), channel_id=1, source_target_pairs={{0,24},{4,28},{8,0},{12,4},{16,8},{20,12},{24,16},{28,20},{1,25},{... | collective-permute-start | bytes 1572872 | tf_op jit(solution)/shard_map/ppermute | solution.py:438
  190.9 2.7 collective-permute-done.28
  198.7 8.9 %collective-permute-done.25 = bf16[1024,256]{1,0:T(8,128)(2,1)S(1)} collective-permute-done((bf16[1024,256]{1,0:T(8,128)(2,1)S(1)}, bf16[1024,256]{1,0:T(8,128)(2,1)S(1)}, u32[]{:S(2)}, u32[]{:S(2)}) %collective-permute-start.25) | collective-permute-done | bytes 524320 | tf_op jit(solution)/shard_map/ppermute | solution.py:443
  209.3 9.5 %collective-permute-done.27 = bf16[1024,256]{1,0:T(8,128)(2,1)S(1)} collective-permute-done((bf16[1024,256]{1,0:T(8,128)(2,1)S(1)}, bf16[1024,256]{1,0:T(8,128)(2,1)S(1)}, u32[]{:S(2)}, u32[]{:S(2)}) %collective-permute-start.27) | collective-permute-done | bytes 524320 | tf_op jit(solution)/shard_map/ppermute | solution.py:443
  220.6 9.5 %collective-permute-done.22 = bf16[256,1024]{1,0:T(8,128)(2,1)S(1)} collective-permute-done((bf16[256,1024]{1,0:T(8,128)(2,1)S(1)}, bf16[256,1024]{1,0:T(8,128)(2,1)S(1)}, u32[]{:S(2)}, u32[]{:S(2)}) %collective-permute-start.22) | collective-permute-done | bytes 524320 | tf_op jit(solution)/shard_map/ppermute | solution.py:443
  230.9 10.4 %collective-permute-done.15 = bf16[256,1024]{1,0:T(8,128)(2,1)S(1)} collective-permute-done((bf16[256,1024]{1,0:T(8,128)(2,1)S(1)}, bf16[256,1024]{1,0:T(8,128)(2,1)S(1)}, u32[]{:S(2)}, u32[]{:S(2)}) %collective-permute-start.15) | collective-permute-done | bytes 524320 | tf_op jit(solution)/shard_map/ppermute | solution.py:443
  242.1 9.0 %collective-permute-done.29 = bf16[1024,256]{1,0:T(8,128)(2,1)S(1)} collective-permute-done((bf16[1024,256]{1,0:T(8,128)(2,1)S(1)}, bf16[1024,256]{1,0:T(8,128)(2,1)S(1)}, u32[]{:S(2)}, u32[]{:S(2)}) %collective-permute-start.29) | collective-permute-done | bytes 524320 | tf_op jit(solution)/shard_map/ppermute | solution.py:443
  252.0 3.2 fusion
  255.5 3.5 fusion.40.s_ref.s_tail
  259.0 8.6 %fusion.42.v_ref.v_tail = f32[1024,1024]{1,0:T(8,128)} fusion(bf16[2048,1024]{1,0:T(8,128)(2,1)} %constant_dynamic-update-slice_fusion.17, bf16[1024,2048]{1,0:T(8,128)(2,1)S(1)} %copy-done.10, f32[2048]{0:T(1024)S(1)} %bitcast.97, f32[1024]{0:T(1024)S(1)} %add_rsqrt_fusion.1), kind=kOutput, calls=%fused_computation.199 | convolution fusion | flops 4303355904 | bytes 12595200 | tf_op jit(solution)/shard_map/dot_general | solution.py:577
  267.6 24.8 %mixer.1 = (f32[1024,1024]{1,0:T(8,128)}, f32[4,128,1024]{2,1,0:T(8,128)}) custom-call(s32[4]{0:T(128)} %opens.3, s32[4]{0:T(128)} %widths.1, f32[1024,1024]{1,0:T(8,128)} %fusion.42.v_ref.v_tail, f32[1024,384]{1,0:T(8,128)} %fusion.40.s_ref.s_tail, f32[8,1024]{1,0:T(8,128)} %maximum_maximum_fusion.tx, f32[8,256]{1,0:T(8,128)} %pad_convert_fusion.ts, ...), custom_call_target="tpu_custom_call" | custom-call | tf_op jit(solution)/shard_map/mixer/pallas_call | solution.py:331
  292.4 8.5 %fusion.38 = f32[1024,1024]{1,0:T(8,128)} fusion(bf16[2048,1024]{1,0:T(8,128)(2,1)} %constant_dynamic-update-slice_fusion.9, bf16[1024,2048]{1,0:T(8,128)(2,1)S(1)} %copy-done.10, f32[2048]{0:T(1024)S(1)} %bitcast.98, f32[1024]{0:T(1024)S(1)} %add_rsqrt_fusion.1), kind=kOutput, calls=%fused_computation.197 | convolution fusion | flops 4303355904 | bytes 12595200 | tf_op jit(solution)/shard_map/dot_general | solution.py:592
  300.9 13.9 %multiply_reduce_fusion.2 = (f32[1024]{0:T(1024)S(1)}, f32[1024]{0:T(1024)S(1)}, f32[1024,1024]{1,0:T(8,128)}, f32[1024,1024]{1,0:T(8,128)}) fusion(f32[1024]{0:T(1024)S(1)} %bitcast.82, f32[1024,1024]{1,0:T(8,128)} %get-tuple-element.33, f32[1024,1024]{1,0:T(8,128)} %fusion.38, bf16[1024,2048]{1,0:T(8,128)(2,1)} %all-gather.5.cloned.1.call-done, ...), kind=kOutput, calls=%fused_computation.12 | convolution fusion | flops 4305451008 | bytes 25178112 | tf_op jit(solution)/shard_map/tw,cw->tc/dot_general | solution.py:597
  314.9 5.8 psum.14
  320.7 9.4 %multiply_convert_fusion = (bf16[1024,1024]{1,0:T(8,128)(2,1)S(1)}, f32[1024,1024]{1,0:T(8,128)}, f32[1024]{0:T(1024)S(1)}) fusion(f32[1024,1024]{1,0:T(8,128)} %fusion.38, f32[1024,1024]{1,0:T(8,128)} %get-tuple-element.33, f32[1024,1024]{1,0:T(8,128)} %get-tuple-element.145, f32[1024]{0:T(1024)S(1)} %get-tuple-element.188, f32[1024]{0:T(1024)S(1)} %get-tuple-element.189, ...), kind=kLoop, calls=%fused_computation.8 | loop fusion | flops 22019072 | bytes 23093248 | tf_op jit(solution)/shard_map/convert_element_type | solution.py:617
  330.0 9.7 %fusion.47 = f32[1024,2048]{1,0:T(8,128)} fusion(bf16[1024,1024]{1,0:T(8,128)(2,1)S(1)} %get-tuple-element.148, bf16[2048,1024]{1,0:T(8,128)(2,1)} %constant_dynamic-update-slice_fusion.9), kind=kOutput, calls=%fused_computation.202 | convolution fusion | flops 4294967296 | bytes 14680064 | tf_op jit(solution)/shard_map/tc,dc->td/dot_general | solution.py:624
  339.8 43.4 %mixer_back.1 = (bf16[1024,1024]{1,0:T(8,128)(2,1)}, bf16[1024,384]{1,0:T(8,128)(2,1)}, f32[8,1024]{1,0:T(8,128)}, f32[8,256]{1,0:T(8,128)}, f32[8,128]{1,0:T(8,128)}) custom-call(s32[4]{0:T(128)} %opens.3, f32[1024,1024]{1,0:T(8,128)} %fusion.42.v_ref.v_tail, f32[1024,1024]{1,0:T(8,128)} %fusion.42.v_ref.v_tail, f32[1024,384]{1,0:T(8,128)} %fusion.40.s_ref.s_tail, ...), custom_call_target="tpu_custom_call" | custom-call | tf_op jit(solution)/shard_map/mixer_back/pallas_call | solution.py:372
  383.2 7.2 %fusion.48 = f32[1024,2048]{1,0:T(8,128)S(1)} fusion(bf16[1024,1024]{1,0:T(8,128)(2,1)} %get-tuple-element.35, bf16[2048,1024]{1,0:T(8,128)(2,1)} %constant_dynamic-update-slice_fusion.17), kind=kOutput, calls=%fused_computation.203 | convolution fusion | flops 4294967296 | bytes 14680064 | tf_op jit(solution)/shard_map/tc,dc->td/dot_general | solution.py:625
  390.4 4.6 add_convert_fusion
  395.4 10.7 %convolution_convert_fusion = bf16[1024,2048]{1,0:T(8,128)(2,1)} fusion(bf16[1024,2048]{1,0:T(8,128)(2,1)} %constant_dynamic-update-slice_fusion.1, f32[1024,1024]{1,0:T(8,128)} %get-tuple-element.145, f32[1024]{0:T(1024)S(1)} %get-tuple-element.189, f32[1024]{0:T(1024)S(1)} %bitcast.84), kind=kOutput, calls=%fused_computation.15 | convolution fusion | flops 4300210176 | bytes 12591104 | tf_op jit(solution)/shard_map/dot_general | solution.py:605
  406.1 7.6 %fusion.34 = f32[2048,1024]{1,0:T(8,128)S(1)} fusion(bf16[1024,1024]{1,0:T(8,128)(2,1)} %get-tuple-element.35, bf16[1024,2048]{1,0:T(8,128)(2,1)} %all-gather.3.cloned.1.call-done, f32[2048]{0:T(1024)S(1)} %bitcast.99, f32[1024]{0:T(1024)S(1)} %add_rsqrt_fusion.1), kind=kOutput, calls=%fused_computation.195 | convolution fusion | flops 4303355904 | bytes 14692352 | tf_op jit(solution)/shard_map/td,tc->dc/dot_general | solution.py:622
  419.2 4.9 fusion.36
  429.4 7.4 %fusion.31 = f32[1024,2048]{1,0:T(8,128)} fusion(bf16[1024,2048]{1,0:T(8,128)(2,1)S(1)} %copy-done.15, f32[1024,1024]{1,0:T(8,128)S(1)} %copy-done, f32[1024]{0:T(1024)S(1)} %get-tuple-element.189, f32[1024]{0:T(1024)S(1)} %bitcast.85), kind=kOutput, calls=%fused_computation.193 | convolution fusion | flops 4298113024 | bytes 16785408 | tf_op jit(solution)/shard_map/tc,tw->cw/dot_general | solution.py:611
  436.9 2.7 fusion.32
  440.6 3.7 dynamic-slice_convert_fusion.3
  445.9 6.9 %collective-permute-done.41 = bf16[256,1024]{1,0:T(8,128)(2,1)} collective-permute-done((bf16[256,1024]{1,0:T(8,128)(2,1)}, bf16[256,1024]{1,0:T(8,128)(2,1)}, u32[]{:S(2)}, u32[]{:S(2)}) %collective-permute-start.41) | collective-permute-done | bytes 524320 | tf_op jit(solution)/shard_map/ppermute | solution.py:466
  453.0 11.0 %collective-permute-done.39 = bf16[256,1024]{1,0:T(8,128)(2,1)} collective-permute-done((bf16[256,1024]{1,0:T(8,128)(2,1)}, bf16[256,1024]{1,0:T(8,128)(2,1)}, u32[]{:S(2)}, u32[]{:S(2)}) %collective-permute-start.39) | collective-permute-done | bytes 524320 | tf_op jit(solution)/shard_map/ppermute | solution.py:466
  464.3 3.8 add_convert_fusion.6
  469.8 5.4 collective-permute-done.30
  475.5 10.9 %collective-permute-done.34 = bf16[256,1024]{1,0:T(8,128)(2,1)S(1)} collective-permute-done((bf16[256,1024]{1,0:T(8,128)(2,1)S(1)}, bf16[256,1024]{1,0:T(8,128)(2,1)S(1)}, u32[]{:S(2)}, u32[]{:S(2)}) %collective-permute-start.34) | collective-permute-done | bytes 524320 | tf_op jit(solution)/shard_map/ppermute | solution.py:466
  486.8 10.9 %collective-permute-done.32 = bf16[256,1024]{1,0:T(8,128)(2,1)S(1)} collective-permute-done((bf16[256,1024]{1,0:T(8,128)(2,1)S(1)}, bf16[256,1024]{1,0:T(8,128)(2,1)S(1)}, u32[]{:S(2)}, u32[]{:S(2)}) %collective-permute-start.32) | collective-permute-done | bytes 524320 | tf_op jit(solution)/shard_map/ppermute | solution.py:466
  500.5 8.3 %collective-permute-done.53 = bf16[1024,256]{1,0:T(8,128)(2,1)S(1)} collective-permute-done((bf16[1024,256]{1,0:T(8,128)(2,1)}, bf16[1024,256]{1,0:T(8,128)(2,1)S(1)}, u32[]{:S(2)}, u32[]{:S(2)}) %collective-permute-start.53) | collective-permute-done | bytes 524320 | tf_op jit(solution)/shard_map/ppermute | solution.py:466
  508.9 2.9 add_convert_fusion.9
  511.8 8.5 %collective-permute-done.57 = bf16[1024,256]{1,0:T(8,128)(2,1)} collective-permute-done((bf16[1024,256]{1,0:T(8,128)(2,1)}, bf16[1024,256]{1,0:T(8,128)(2,1)}, u32[]{:S(2)}, u32[]{:S(2)}) %collective-permute-start.57) | collective-permute-done | bytes 524320 | tf_op jit(solution)/shard_map/ppermute | solution.py:466
  520.4 11.0 %collective-permute-done.55 = bf16[1024,256]{1,0:T(8,128)(2,1)} collective-permute-done((bf16[1024,256]{1,0:T(8,128)(2,1)}, bf16[1024,256]{1,0:T(8,128)(2,1)}, u32[]{:S(2)}, u32[]{:S(2)}) %collective-permute-start.55) | collective-permute-done | bytes 524320 | tf_op jit(solution)/shard_map/ppermute | solution.py:466
  533.5 3.5 add_convert_fusion.3
  537.3 2.8 add_bitcast_fusion
  540.1 2.5 collective-permute-done.36
  544.2 20.0 %collective-permute-start.56 = (bf16[1024,256]{1,0:T(8,128)(2,1)}, bf16[1024,256]{1,0:T(8,128)(2,1)}, u32[]{:S(2)}, u32[]{:S(2)}) collective-permute-start(bf16[1024,256]{1,0:T(8,128)(2,1)} %get-tuple-element.153), channel_id=1, source_target_pairs={{0,16},{4,20},{8,24},{12,28},{16,0},{20,4},{24,8},{28,12},{1,17},{... | collective-permute-start | bytes 1572872 | tf_op jit(solution)/shard_map/ppermute | solution.py:470
  564.2 30.0 %collective-permute-done.33 = bf16[256,1024]{1,0:T(8,128)(2,1)S(1)} collective-permute-done((bf16[256,1024]{1,0:T(8,128)(2,1)S(1)}, bf16[256,1024]{1,0:T(8,128)(2,1)S(1)}, u32[]{:S(2)}, u32[]{:S(2)}) %collective-permute-start.33) | collective-permute-done | bytes 524320 | tf_op jit(solution)/shard_map/ppermute | solution.py:470
  594.5 2.6 add_bitcast_fusion.1
  606.5 2.5 fusion.11
  609.0 2.9 copy.143
  612.0 2.9 copy.144
  614.9 2.9 copy.145
  621.5 4.1 multiply_add_fusion
  625.6 6.1 psum.15
  640.8 2.9 collective-permute-start.51
  643.6 3.7 collective-permute-start.49
  649.5 3.3 fusion.6
  (344 shorter events, 127.0 us)
Async XLA Ops:
  7.3 244.8 %all-gather.3.cloned.1.call-start = ((), (), s32[]{:S(2)}) async-start(), calls=%async_computation.2 | async-start | bytes 5242880 | tf_op jit(solution)/shard_map/all_gather | solution.py:570
  8.0 292.9 %all-gather.5.cloned.1.call-start = ((), (), s32[]{:S(2)}) async-start(), calls=%async_computation.3 | async-start | bytes 5242880 | tf_op jit(solution)/shard_map/all_gather | solution.py:572
  11.2 71.8 %collective-permute-start.16 = (bf16[256,1024]{1,0:T(8,128)(2,1)}, bf16[256,1024]{1,0:T(8,128)(2,1)S(1)}, u32[]{:S(2)}, u32[]{:S(2)}) collective-permute-start(bf16[256,1024]{1,0:T(8,128)(2,1)} %get-tuple-element.182), channel_id=1, source_target_pairs={{0,4},{4,0},{8,12},{12,8},{16,20},{20,16},{24,28},{28,24},{1,5},{5... | collective-permute-start | bytes 1572872 | tf_op jit(solution)/shard_map/ppermute | solution.py:443
  14.4 13.3 %collective-permute-start = (bf16[64,262]{1,0:T(8,128)(2,1)S(1)}, bf16[64,262]{1,0:T(8,128)(2,1)S(1)}, u32[]{:S(2)}, u32[]{:S(2)}) collective-permute-start(bf16[64,262]{1,0:T(8,128)(2,1)S(1)} %fusion.22), channel_id=1, source_target_pairs={{0,1},{1,0},{2,3},{3,2},{4,5},{5,4},{6,7},{7,6},{8,9},{9,8},{10,11... | collective-permute-start | bytes 100616 | tf_op jit(solution)/shard_map/ppermute | solution.py:499
  16.3 580.9 %reduce-scatter.5.cloned.1.call-start = ((), (), s32[]{:S(2)}) async-start(), calls=%async_computation.5 | async-start | bytes 5242880 | tf_op jit(solution)/shard_map/reduce_scatter | solution.py:631
  27.8 7.6 %collective-permute-start.1 = (bf16[128,262]{1,0:T(8,128)(2,1)S(1)}, bf16[128,262]{1,0:T(8,128)(2,1)S(1)}, u32[]{:S(2)}, u32[]{:S(2)}) collective-permute-start(bf16[128,262]{1,0:T(8,128)(2,1)S(1)} %pad_maximum_fusion.2), channel_id=1, source_target_pairs={{0,2},{1,3},{2,0},{3,1},{4,6},{5,7},{6,4},{7,5},{8,10},{9,11},{10,... | collective-permute-start | bytes 201224 | tf_op jit(solution)/shard_map/ppermute | solution.py:504
  35.6 23.9 %collective-permute-start.2 = (bf16[256,384]{1,0:T(8,128)(2,1)S(1)}, bf16[256,384]{1,0:T(8,128)(2,1)}, u32[]{:S(2)}, u32[]{:S(2)}) collective-permute-start(bf16[256,384]{1,0:T(8,128)(2,1)S(1)} %pad.27), channel_id=1, source_target_pairs={{0,4},{4,0},{8,12},{12,8},{16,20},{20,16},{24,28},{28,24},{1,5},{5... | collective-permute-start | bytes 589832 | tf_op jit(solution)/shard_map/ppermute | solution.py:443
  35.7 10.0 %collective-permute-start.3 = (bf16[256,384]{1,0:T(8,128)(2,1)S(1)}, bf16[256,384]{1,0:T(8,128)(2,1)S(1)}, u32[]{:S(2)}, u32[]{:S(2)}) collective-permute-start(bf16[256,384]{1,0:T(8,128)(2,1)S(1)} %pad.27), channel_id=1, source_target_pairs={{0,8},{4,12},{8,16},{12,20},{16,24},{20,28},{24,0},{28,4},{1,9},{5... | collective-permute-start | bytes 589832 | tf_op jit(solution)/shard_map/ppermute | solution.py:438
  37.8 16.8 %collective-permute-start.5 = (bf16[256,384]{1,0:T(8,128)(2,1)S(1)}, bf16[256,384]{1,0:T(8,128)(2,1)}, u32[]{:S(2)}, u32[]{:S(2)}) collective-permute-start(bf16[256,384]{1,0:T(8,128)(2,1)S(1)} %pad.27), channel_id=1, source_target_pairs={{0,16},{4,20},{8,24},{12,28},{16,0},{20,4},{24,8},{28,12},{1,17},{... | collective-permute-start | bytes 589832 | tf_op jit(solution)/shard_map/ppermute | solution.py:438
  40.4 16.8 %collective-permute-start.7 = (bf16[256,384]{1,0:T(8,128)(2,1)S(1)}, bf16[256,384]{1,0:T(8,128)(2,1)S(1)}, u32[]{:S(2)}, u32[]{:S(2)}) collective-permute-start(bf16[256,384]{1,0:T(8,128)(2,1)S(1)} %pad.27), channel_id=1, source_target_pairs={{0,24},{4,28},{8,0},{12,4},{16,8},{20,12},{24,16},{28,20},{1,25},{... | collective-permute-start | bytes 589832 | tf_op jit(solution)/shard_map/ppermute | solution.py:438
  46.4 38.3 %collective-permute-start.17 = (bf16[256,1024]{1,0:T(8,128)(2,1)}, bf16[256,1024]{1,0:T(8,128)(2,1)}, u32[]{:S(2)}, u32[]{:S(2)}) collective-permute-start(bf16[256,1024]{1,0:T(8,128)(2,1)} %get-tuple-element.182), channel_id=1, source_target_pairs={{0,8},{4,12},{8,16},{12,20},{16,24},{20,28},{24,0},{28,4},{1,9},{5... | collective-permute-start | bytes 1572872 | tf_op jit(solution)/shard_map/ppermute | solution.py:438
  54.6 7.6 %collective-permute-start.4 = (bf16[256,384]{1,0:T(8,128)(2,1)}, bf16[256,384]{1,0:T(8,128)(2,1)}, u32[]{:S(2)}, u32[]{:S(2)}) collective-permute-start(bf16[256,384]{1,0:T(8,128)(2,1)} %copy-done.32), channel_id=1, source_target_pairs={{0,4},{4,0},{8,12},{12,8},{16,20},{20,16},{24,28},{28,24},{1,5},{5... | collective-permute-start | bytes 589832 | tf_op jit(solution)/shard_map/ppermute | solution.py:443
  57.9 16.1 %collective-permute-start.6 = (bf16[256,384]{1,0:T(8,128)(2,1)}, bf16[256,384]{1,0:T(8,128)(2,1)}, u32[]{:S(2)}, u32[]{:S(2)}) collective-permute-start(bf16[256,384]{1,0:T(8,128)(2,1)} %collective-permute-done.5), channel_id=1, source_target_pairs={{0,4},{4,0},{8,12},{12,8},{16,20},{20,16},{24,28},{28,24},{1,5},{5... | collective-permute-start | bytes 589832 | tf_op jit(solution)/shard_map/ppermute | solution.py:443
  59.6 16.9 %collective-permute-start.8 = (bf16[256,384]{1,0:T(8,128)(2,1)}, bf16[256,384]{1,0:T(8,128)(2,1)}, u32[]{:S(2)}, u32[]{:S(2)}) collective-permute-start(bf16[256,384]{1,0:T(8,128)(2,1)} %copy-done.31), channel_id=1, source_target_pairs={{0,4},{4,0},{8,12},{12,8},{16,20},{20,16},{24,28},{28,24},{1,5},{5... | collective-permute-start | bytes 589832 | tf_op jit(solution)/shard_map/ppermute | solution.py:443
  62.3 56.2 %collective-permute-start.19 = (bf16[256,1024]{1,0:T(8,128)(2,1)}, bf16[256,1024]{1,0:T(8,128)(2,1)}, u32[]{:S(2)}, u32[]{:S(2)}) collective-permute-start(bf16[256,1024]{1,0:T(8,128)(2,1)} %get-tuple-element.182), channel_id=1, source_target_pairs={{0,16},{4,20},{8,24},{12,28},{16,0},{20,4},{24,8},{28,12},{1,17},{... | collective-permute-start | bytes 1572872 | tf_op jit(solution)/shard_map/ppermute | solution.py:438
  74.0 47.8 %collective-permute-start.9 = (bf16[256,1024]{1,0:T(8,128)(2,1)}, bf16[256,1024]{1,0:T(8,128)(2,1)}, u32[]{:S(2)}, u32[]{:S(2)}) collective-permute-start(bf16[256,1024]{1,0:T(8,128)(2,1)} %get-tuple-element.183), channel_id=1, source_target_pairs={{0,4},{4,0},{8,12},{12,8},{16,20},{20,16},{24,28},{28,24},{1,5},{5... | collective-permute-start | bytes 1572872 | tf_op jit(solution)/shard_map/ppermute | solution.py:443
  76.5 45.3 %collective-permute-start.10 = (bf16[256,1024]{1,0:T(8,128)(2,1)}, bf16[256,1024]{1,0:T(8,128)(2,1)}, u32[]{:S(2)}, u32[]{:S(2)}) collective-permute-start(bf16[256,1024]{1,0:T(8,128)(2,1)} %get-tuple-element.183), channel_id=1, source_target_pairs={{0,8},{4,12},{8,16},{12,20},{16,24},{20,28},{24,0},{28,4},{1,9},{5... | collective-permute-start | bytes 1572872 | tf_op jit(solution)/shard_map/ppermute | solution.py:438
  83.1 38.8 %collective-permute-start.23 = (bf16[1024,256]{1,0:T(8,128)(2,1)S(1)}, bf16[1024,256]{1,0:T(8,128)(2,1)}, u32[]{:S(2)}, u32[]{:S(2)}) collective-permute-start(bf16[1024,256]{1,0:T(8,128)(2,1)S(1)} %get-tuple-element.147), channel_id=1, source_target_pairs={{0,4},{4,0},{8,12},{12,8},{16,20},{20,16},{24,28},{28,24},{1,5},{5... | collective-permute-start | bytes 1572872 | tf_op jit(solution)/shard_map/ppermute | solution.py:443
  84.7 41.6 %collective-permute-start.24 = (bf16[1024,256]{1,0:T(8,128)(2,1)S(1)}, bf16[1024,256]{1,0:T(8,128)(2,1)S(1)}, u32[]{:S(2)}, u32[]{:S(2)}) collective-permute-start(bf16[1024,256]{1,0:T(8,128)(2,1)S(1)} %get-tuple-element.147), channel_id=1, source_target_pairs={{0,8},{4,12},{8,16},{12,20},{16,24},{20,28},{24,0},{28,4},{1,9},{5... | collective-permute-start | bytes 1572872 | tf_op jit(solution)/shard_map/ppermute | solution.py:438
  118.5 15.1 %collective-permute-start.18 = (bf16[256,1024]{1,0:T(8,128)(2,1)}, bf16[256,1024]{1,0:T(8,128)(2,1)S(1)}, u32[]{:S(2)}, u32[]{:S(2)}) collective-permute-start(bf16[256,1024]{1,0:T(8,128)(2,1)} %collective-permute-done.17), channel_id=1, source_target_pairs={{0,4},{4,0},{8,12},{12,8},{16,20},{20,16},{24,28},{28,24},{1,5},{5... | collective-permute-start | bytes 1572872 | tf_op jit(solution)/shard_map/ppermute | solution.py:443
  121.8 14.6 %collective-permute-start.21 = (bf16[256,1024]{1,0:T(8,128)(2,1)}, bf16[256,1024]{1,0:T(8,128)(2,1)S(1)}, u32[]{:S(2)}, u32[]{:S(2)}) collective-permute-start(bf16[256,1024]{1,0:T(8,128)(2,1)} %get-tuple-element.182), channel_id=1, source_target_pairs={{0,24},{4,28},{8,0},{12,4},{16,8},{20,12},{24,16},{28,20},{1,25},{... | collective-permute-start | bytes 1572872 | tf_op jit(solution)/shard_map/ppermute | solution.py:438
  121.8 46.4 %collective-permute-start.12 = (bf16[256,1024]{1,0:T(8,128)(2,1)}, bf16[256,1024]{1,0:T(8,128)(2,1)S(1)}, u32[]{:S(2)}, u32[]{:S(2)}) collective-permute-start(bf16[256,1024]{1,0:T(8,128)(2,1)} %get-tuple-element.183), channel_id=1, source_target_pairs={{0,16},{4,20},{8,24},{12,28},{16,0},{20,4},{24,8},{28,12},{1,17},{... | collective-permute-start | bytes 1572872 | tf_op jit(solution)/shard_map/ppermute | solution.py:438
  121.9 59.6 %collective-permute-start.11 = (bf16[256,1024]{1,0:T(8,128)(2,1)}, bf16[256,1024]{1,0:T(8,128)(2,1)S(1)}, u32[]{:S(2)}, u32[]{:S(2)}) collective-permute-start(bf16[256,1024]{1,0:T(8,128)(2,1)} %collective-permute-done.10), channel_id=1, source_target_pairs={{0,4},{4,0},{8,12},{12,8},{16,20},{20,16},{24,28},{28,24},{1,5},{5... | collective-permute-start | bytes 1572872 | tf_op jit(solution)/shard_map/ppermute | solution.py:443
  126.4 58.5 %collective-permute-start.20 = (bf16[256,1024]{1,0:T(8,128)(2,1)}, bf16[256,1024]{1,0:T(8,128)(2,1)S(1)}, u32[]{:S(2)}, u32[]{:S(2)}) collective-permute-start(bf16[256,1024]{1,0:T(8,128)(2,1)} %collective-permute-done.19), channel_id=1, source_target_pairs={{0,4},{4,0},{8,12},{12,8},{16,20},{20,16},{24,28},{28,24},{1,5},{5... | collective-permute-start | bytes 1572872 | tf_op jit(solution)/shard_map/ppermute | solution.py:443
  133.6 54.5 %collective-permute-start.26 = (bf16[1024,256]{1,0:T(8,128)(2,1)S(1)}, bf16[1024,256]{1,0:T(8,128)(2,1)S(1)}, u32[]{:S(2)}, u32[]{:S(2)}) collective-permute-start(bf16[1024,256]{1,0:T(8,128)(2,1)S(1)} %get-tuple-element.147), channel_id=1, source_target_pairs={{0,16},{4,20},{8,24},{12,28},{16,0},{20,4},{24,8},{28,12},{1,17},{... | collective-permute-start | bytes 1572872 | tf_op jit(solution)/shard_map/ppermute | solution.py:438
  136.3 53.1 %collective-permute-start.14 = (bf16[256,1024]{1,0:T(8,128)(2,1)}, bf16[256,1024]{1,0:T(8,128)(2,1)S(1)}, u32[]{:S(2)}, u32[]{:S(2)}) collective-permute-start(bf16[256,1024]{1,0:T(8,128)(2,1)} %get-tuple-element.183), channel_id=1, source_target_pairs={{0,24},{4,28},{8,0},{12,4},{16,8},{20,12},{24,16},{28,20},{1,25},{... | collective-permute-start | bytes 1572872 | tf_op jit(solution)/shard_map/ppermute | solution.py:438
  168.2 25.5 %collective-permute-start.28 = (bf16[1024,256]{1,0:T(8,128)(2,1)S(1)}, bf16[1024,256]{1,0:T(8,128)(2,1)S(1)}, u32[]{:S(2)}, u32[]{:S(2)}) collective-permute-start(bf16[1024,256]{1,0:T(8,128)(2,1)S(1)} %get-tuple-element.147), channel_id=1, source_target_pairs={{0,24},{4,28},{8,0},{12,4},{16,8},{20,12},{24,16},{28,20},{1,25},{... | collective-permute-start | bytes 1572872 | tf_op jit(solution)/shard_map/ppermute | solution.py:438
  181.5 14.8 %collective-permute-start.13 = (bf16[256,1024]{1,0:T(8,128)(2,1)S(1)}, bf16[256,1024]{1,0:T(8,128)(2,1)S(1)}, u32[]{:S(2)}, u32[]{:S(2)}) collective-permute-start(bf16[256,1024]{1,0:T(8,128)(2,1)S(1)} %collective-permute-done.12), channel_id=1, source_target_pairs={{0,4},{4,0},{8,12},{12,8},{16,20},{20,16},{24,28},{28,24},{1,5},{5... | collective-permute-start | bytes 1572872 | tf_op jit(solution)/shard_map/ppermute | solution.py:443
  184.9 22.7 %collective-permute-start.25 = (bf16[1024,256]{1,0:T(8,128)(2,1)S(1)}, bf16[1024,256]{1,0:T(8,128)(2,1)S(1)}, u32[]{:S(2)}, u32[]{:S(2)}) collective-permute-start(bf16[1024,256]{1,0:T(8,128)(2,1)S(1)} %collective-permute-done.24), channel_id=1, source_target_pairs={{0,4},{4,0},{8,12},{12,8},{16,20},{20,16},{24,28},{28,24},{1,5},{5... | collective-permute-start | bytes 1572872 | tf_op jit(solution)/shard_map/ppermute | solution.py:443
  188.0 30.8 %collective-permute-start.27 = (bf16[1024,256]{1,0:T(8,128)(2,1)S(1)}, bf16[1024,256]{1,0:T(8,128)(2,1)S(1)}, u32[]{:S(2)}, u32[]{:S(2)}) collective-permute-start(bf16[1024,256]{1,0:T(8,128)(2,1)S(1)} %collective-permute-done.26), channel_id=1, source_target_pairs={{0,4},{4,0},{8,12},{12,8},{16,20},{20,16},{24,28},{28,24},{1,5},{5... | collective-permute-start | bytes 1572872 | tf_op jit(solution)/shard_map/ppermute | solution.py:443
  189.4 40.7 %collective-permute-start.22 = (bf16[256,1024]{1,0:T(8,128)(2,1)S(1)}, bf16[256,1024]{1,0:T(8,128)(2,1)S(1)}, u32[]{:S(2)}, u32[]{:S(2)}) collective-permute-start(bf16[256,1024]{1,0:T(8,128)(2,1)S(1)} %collective-permute-done.21), channel_id=1, source_target_pairs={{0,4},{4,0},{8,12},{12,8},{16,20},{20,16},{24,28},{28,24},{1,5},{5... | collective-permute-start | bytes 1572872 | tf_op jit(solution)/shard_map/ppermute | solution.py:443
  193.6 47.7 %collective-permute-start.15 = (bf16[256,1024]{1,0:T(8,128)(2,1)S(1)}, bf16[256,1024]{1,0:T(8,128)(2,1)S(1)}, u32[]{:S(2)}, u32[]{:S(2)}) collective-permute-start(bf16[256,1024]{1,0:T(8,128)(2,1)S(1)} %collective-permute-done.14), channel_id=1, source_target_pairs={{0,4},{4,0},{8,12},{12,8},{16,20},{20,16},{24,28},{28,24},{1,5},{5... | collective-permute-start | bytes 1572872 | tf_op jit(solution)/shard_map/ppermute | solution.py:443
  196.3 54.8 %collective-permute-start.29 = (bf16[1024,256]{1,0:T(8,128)(2,1)S(1)}, bf16[1024,256]{1,0:T(8,128)(2,1)S(1)}, u32[]{:S(2)}, u32[]{:S(2)}) collective-permute-start(bf16[1024,256]{1,0:T(8,128)(2,1)S(1)} %collective-permute-done.28), channel_id=1, source_target_pairs={{0,4},{4,0},{8,12},{12,8},{16,20},{20,16},{24,28},{28,24},{1,5},{5... | collective-permute-start | bytes 1572872 | tf_op jit(solution)/shard_map/ppermute | solution.py:443
  395.0 254.4 %reduce-scatter.3.cloned.1.call-start = ((), (), s32[]{:S(2)}) async-start(), calls=%async_computation.4 | async-start | bytes 5242880 | tf_op jit(solution)/shard_map/reduce_scatter | solution.py:606
  415.1 52.9 %collective-permute-start.43 = (bf16[256,1024]{1,0:T(8,128)(2,1)}, bf16[256,1024]{1,0:T(8,128)(2,1)}, u32[]{:S(2)}, u32[]{:S(2)}) collective-permute-start(bf16[256,1024]{1,0:T(8,128)(2,1)} %get-tuple-element.169), channel_id=1, source_target_pairs={{0,4},{4,0},{8,12},{12,8},{16,20},{20,16},{24,28},{28,24},{1,5},{5... | collective-permute-start | bytes 1572872 | tf_op jit(solution)/shard_map/ppermute | solution.py:466
  415.4 29.0 %collective-permute-start.37 = (bf16[256,1024]{1,0:T(8,128)(2,1)}, bf16[256,1024]{1,0:T(8,128)(2,1)}, u32[]{:S(2)}, u32[]{:S(2)}) collective-permute-start(bf16[256,1024]{1,0:T(8,128)(2,1)} %get-tuple-element.168), channel_id=1, source_target_pairs={{0,4},{4,0},{8,12},{12,8},{16,20},{20,16},{24,28},{28,24},{1,5},{5... | collective-permute-start | bytes 1572872 | tf_op jit(solution)/shard_map/ppermute | solution.py:466
  417.2 35.6 %collective-permute-start.41 = (bf16[256,1024]{1,0:T(8,128)(2,1)}, bf16[256,1024]{1,0:T(8,128)(2,1)}, u32[]{:S(2)}, u32[]{:S(2)}) collective-permute-start(bf16[256,1024]{1,0:T(8,128)(2,1)} %get-tuple-element.170), channel_id=1, source_target_pairs={{0,4},{4,0},{8,12},{12,8},{16,20},{20,16},{24,28},{28,24},{1,5},{5... | collective-permute-start | bytes 1572872 | tf_op jit(solution)/shard_map/ppermute | solution.py:466
  418.6 45.4 %collective-permute-start.39 = (bf16[256,1024]{1,0:T(8,128)(2,1)}, bf16[256,1024]{1,0:T(8,128)(2,1)}, u32[]{:S(2)}, u32[]{:S(2)}) collective-permute-start(bf16[256,1024]{1,0:T(8,128)(2,1)} %get-tuple-element.171), channel_id=1, source_target_pairs={{0,4},{4,0},{8,12},{12,8},{16,20},{20,16},{24,28},{28,24},{1,5},{5... | collective-permute-start | bytes 1572872 | tf_op jit(solution)/shard_map/ppermute | solution.py:466
  425.6 49.7 %collective-permute-start.30 = (bf16[256,1024]{1,0:T(8,128)(2,1)}, bf16[256,1024]{1,0:T(8,128)(2,1)}, u32[]{:S(2)}, u32[]{:S(2)}) collective-permute-start(bf16[256,1024]{1,0:T(8,128)(2,1)} %get-tuple-element.161), channel_id=1, source_target_pairs={{0,4},{4,0},{8,12},{12,8},{16,20},{20,16},{24,28},{28,24},{1,5},{5... | collective-permute-start | bytes 1572872 | tf_op jit(solution)/shard_map/ppermute | solution.py:466
  444.4 42.0 %collective-permute-start.34 = (bf16[256,1024]{1,0:T(8,128)(2,1)S(1)}, bf16[256,1024]{1,0:T(8,128)(2,1)S(1)}, u32[]{:S(2)}, u32[]{:S(2)}) collective-permute-start(bf16[256,1024]{1,0:T(8,128)(2,1)S(1)} %copy-done.26), channel_id=1, source_target_pairs={{0,4},{4,0},{8,12},{12,8},{16,20},{20,16},{24,28},{28,24},{1,5},{5... | collective-permute-start | bytes 1572872 | tf_op jit(solution)/shard_map/ppermute | solution.py:466
  452.8 44.8 %collective-permute-start.32 = (bf16[256,1024]{1,0:T(8,128)(2,1)S(1)}, bf16[256,1024]{1,0:T(8,128)(2,1)S(1)}, u32[]{:S(2)}, u32[]{:S(2)}) collective-permute-start(bf16[256,1024]{1,0:T(8,128)(2,1)S(1)} %copy-done.25), channel_id=1, source_target_pairs={{0,4},{4,0},{8,12},{12,8},{16,20},{20,16},{24,28},{28,24},{1,5},{5... | collective-permute-start | bytes 1572872 | tf_op jit(solution)/shard_map/ppermute | solution.py:466
  464.0 44.8 %collective-permute-start.53 = (bf16[1024,256]{1,0:T(8,128)(2,1)}, bf16[1024,256]{1,0:T(8,128)(2,1)S(1)}, u32[]{:S(2)}, u32[]{:S(2)}) collective-permute-start(bf16[1024,256]{1,0:T(8,128)(2,1)} %get-tuple-element.154), channel_id=1, source_target_pairs={{0,4},{4,0},{8,12},{12,8},{16,20},{20,16},{24,28},{28,24},{1,5},{5... | collective-permute-start | bytes 1572872 | tf_op jit(solution)/shard_map/ppermute | solution.py:466
  468.0 52.2 %collective-permute-start.57 = (bf16[1024,256]{1,0:T(8,128)(2,1)}, bf16[1024,256]{1,0:T(8,128)(2,1)}, u32[]{:S(2)}, u32[]{:S(2)}) collective-permute-start(bf16[1024,256]{1,0:T(8,128)(2,1)} %get-tuple-element.156), channel_id=1, source_target_pairs={{0,4},{4,0},{8,12},{12,8},{16,20},{20,16},{24,28},{28,24},{1,5},{5... | collective-permute-start | bytes 1572872 | tf_op jit(solution)/shard_map/ppermute | solution.py:466
  475.3 56.2 %collective-permute-start.55 = (bf16[1024,256]{1,0:T(8,128)(2,1)}, bf16[1024,256]{1,0:T(8,128)(2,1)}, u32[]{:S(2)}, u32[]{:S(2)}) collective-permute-start(bf16[1024,256]{1,0:T(8,128)(2,1)} %get-tuple-element.157), channel_id=1, source_target_pairs={{0,4},{4,0},{8,12},{12,8},{16,20},{20,16},{24,28},{28,24},{1,5},{5... | collective-permute-start | bytes 1572872 | tf_op jit(solution)/shard_map/ppermute | solution.py:466
  486.4 45.4 %collective-permute-start.42 = (bf16[256,1024]{1,0:T(8,128)(2,1)}, bf16[256,1024]{1,0:T(8,128)(2,1)S(1)}, u32[]{:S(2)}, u32[]{:S(2)}) collective-permute-start(bf16[256,1024]{1,0:T(8,128)(2,1)} %get-tuple-element.166), channel_id=1, source_target_pairs={{0,24},{4,28},{8,0},{12,4},{16,8},{20,12},{24,16},{28,20},{1,25},{... | collective-permute-start | bytes 1572872 | tf_op jit(solution)/shard_map/ppermute | solution.py:470
  498.4 33.4 %collective-permute-start.40 = (bf16[256,1024]{1,0:T(8,128)(2,1)}, bf16[256,1024]{1,0:T(8,128)(2,1)S(1)}, u32[]{:S(2)}, u32[]{:S(2)}) collective-permute-start(bf16[256,1024]{1,0:T(8,128)(2,1)} %get-tuple-element.167), channel_id=1, source_target_pairs={{0,16},{4,20},{8,24},{12,28},{16,0},{20,4},{24,8},{28,12},{1,17},{... | collective-permute-start | bytes 1572872 | tf_op jit(solution)/shard_map/ppermute | solution.py:470
  508.9 28.2 %collective-permute-start.38 = (bf16[256,1024]{1,0:T(8,128)(2,1)}, bf16[256,1024]{1,0:T(8,128)(2,1)S(1)}, u32[]{:S(2)}, u32[]{:S(2)}) collective-permute-start(bf16[256,1024]{1,0:T(8,128)(2,1)} %get-tuple-element.165), channel_id=1, source_target_pairs={{0,8},{4,12},{8,16},{12,20},{16,24},{20,28},{24,0},{28,4},{1,9},{5... | collective-permute-start | bytes 1572872 | tf_op jit(solution)/shard_map/ppermute | solution.py:470
  520.2 22.4 %collective-permute-start.36 = (bf16[256,1024]{1,0:T(8,128)(2,1)}, bf16[256,1024]{1,0:T(8,128)(2,1)S(1)}, u32[]{:S(2)}, u32[]{:S(2)}) collective-permute-start(bf16[256,1024]{1,0:T(8,128)(2,1)} %get-tuple-element.162), channel_id=1, source_target_pairs={{0,4},{4,0},{8,12},{12,8},{16,20},{20,16},{24,28},{28,24},{1,5},{5... | collective-permute-start | bytes 1572872 | tf_op jit(solution)/shard_map/ppermute | solution.py:466
  531.4 12.8 %collective-permute-start.35 = (bf16[256,1024]{1,0:T(8,128)(2,1)S(1)}, bf16[256,1024]{1,0:T(8,128)(2,1)S(1)}, u32[]{:S(2)}, u32[]{:S(2)}) collective-permute-start(bf16[256,1024]{1,0:T(8,128)(2,1)S(1)} %get-tuple-element.159), channel_id=1, source_target_pairs={{0,24},{4,28},{8,0},{12,4},{16,8},{20,12},{24,16},{28,20},{1,25},{... | collective-permute-start | bytes 1572872 | tf_op jit(solution)/shard_map/ppermute | solution.py:470
  531.8 62.5 %collective-permute-start.33 = (bf16[256,1024]{1,0:T(8,128)(2,1)S(1)}, bf16[256,1024]{1,0:T(8,128)(2,1)S(1)}, u32[]{:S(2)}, u32[]{:S(2)}) collective-permute-start(bf16[256,1024]{1,0:T(8,128)(2,1)S(1)} %get-tuple-element.160), channel_id=1, source_target_pairs={{0,16},{4,20},{8,24},{12,28},{16,0},{20,4},{24,8},{28,12},{1,17},{... | collective-permute-start | bytes 1572872 | tf_op jit(solution)/shard_map/ppermute | solution.py:470
  531.8 62.7 %collective-permute-start.31 = (bf16[256,1024]{1,0:T(8,128)(2,1)S(1)}, bf16[256,1024]{1,0:T(8,128)(2,1)S(1)}, u32[]{:S(2)}, u32[]{:S(2)}) collective-permute-start(bf16[256,1024]{1,0:T(8,128)(2,1)S(1)} %get-tuple-element.158), channel_id=1, source_target_pairs={{0,8},{4,12},{8,16},{12,20},{16,24},{20,28},{24,0},{28,4},{1,9},{5... | collective-permute-start | bytes 1572872 | tf_op jit(solution)/shard_map/ppermute | solution.py:470
  537.0 83.2 %collective-permute-start.59 = (bf16[1024,256]{1,0:T(8,128)(2,1)}, bf16[1024,256]{1,0:T(8,128)(2,1)}, u32[]{:S(2)}, u32[]{:S(2)}) collective-permute-start(bf16[1024,256]{1,0:T(8,128)(2,1)} %get-tuple-element.155), channel_id=1, source_target_pairs={{0,4},{4,0},{8,12},{12,8},{16,20},{20,16},{24,28},{28,24},{1,5},{5... | collective-permute-start | bytes 1572872 | tf_op jit(solution)/shard_map/ppermute | solution.py:466
  542.6 77.6 %collective-permute-start.58 = (bf16[1024,256]{1,0:T(8,128)(2,1)}, bf16[1024,256]{1,0:T(8,128)(2,1)}, u32[]{:S(2)}, u32[]{:S(2)}) collective-permute-start(bf16[1024,256]{1,0:T(8,128)(2,1)} %get-tuple-element.152), channel_id=1, source_target_pairs={{0,24},{4,28},{8,0},{12,4},{16,8},{20,12},{24,16},{28,20},{1,25},{... | collective-permute-start | bytes 1572872 | tf_op jit(solution)/shard_map/ppermute | solution.py:470
  544.2 77.3 %collective-permute-start.56 = (bf16[1024,256]{1,0:T(8,128)(2,1)}, bf16[1024,256]{1,0:T(8,128)(2,1)}, u32[]{:S(2)}, u32[]{:S(2)}) collective-permute-start(bf16[1024,256]{1,0:T(8,128)(2,1)} %get-tuple-element.153), channel_id=1, source_target_pairs={{0,16},{4,20},{8,24},{12,28},{16,0},{20,4},{24,8},{28,12},{1,17},{... | collective-permute-start | bytes 1572872 | tf_op jit(solution)/shard_map/ppermute | solution.py:470
  594.3 27.2 %collective-permute-start.54 = (bf16[1024,256]{1,0:T(8,128)(2,1)}, bf16[1024,256]{1,0:T(8,128)(2,1)}, u32[]{:S(2)}, u32[]{:S(2)}) collective-permute-start(bf16[1024,256]{1,0:T(8,128)(2,1)} %get-tuple-element.151), channel_id=1, source_target_pairs={{0,8},{4,12},{8,16},{12,20},{16,24},{20,28},{24,0},{28,4},{1,9},{5... | collective-permute-start | bytes 1572872 | tf_op jit(solution)/shard_map/ppermute | solution.py:470
  604.8 13.1 %collective-permute-start.44 = (bf16[2,8,64,258]{3,2,1,0:T(8,128)(2,1)S(1)}, bf16[2,8,64,258]{3,2,1,0:T(8,128)(2,1)S(1)}, u32[]{:S(2)}, u32[]{:S(2)}) collective-permute-start(bf16[2,8,64,258]{3,2,1,0:T(8,128)(2,1)S(1)} %fusion.13), channel_id=1, source_target_pairs={{0,1},{1,0},{2,3},{3,2},{4,5},{5,4},{6,7},{7,6},{8,9},{9,8},{10,11... | collective-permute-start | bytes 1585160 | tf_op jit(solution)/shard_map/ppermute | solution.py:485
  618.8 12.8 %collective-permute-start.45 = (bf16[8,64,258]{2,1,0:T(8,128)(2,1)}, bf16[8,64,258]{2,1,0:T(8,128)(2,1)S(1)}, u32[]{:S(2)}, u32[]{:S(2)}) collective-permute-start(bf16[8,64,258]{2,1,0:T(8,128)(2,1)} %fusion.15), channel_id=1, source_target_pairs={{0,2},{1,3},{2,0},{3,1},{4,6},{5,7},{6,4},{7,5},{8,10},{9,11},{10,... | collective-permute-start | bytes 792584 | tf_op jit(solution)/shard_map/ppermute | solution.py:489
  632.9 5.0 collective-permute-start.46
  633.5 5.8 collective-permute-start.50
  634.9 5.2 collective-permute-start.48
  635.5 17.3 %collective-permute-start.52 = (bf16[64,419]{1,0:T(8,128)(2,1)}, bf16[64,419]{1,0:T(8,128)(2,1)S(1)}, u32[]{:S(2)}, u32[]{:S(2)}) collective-permute-start(bf16[64,419]{1,0:T(8,128)(2,1)} %get-tuple-element.177), channel_id=1, source_target_pairs={{0,4},{4,0},{8,12},{12,8},{16,20},{20,16},{24,28},{28,24},{1,5},{5... | collective-permute-start | bytes 160904 | tf_op jit(solution)/shard_map/ppermute | solution.py:466
  640.8 12.0 %collective-permute-start.51 = (bf16[64,419]{1,0:T(8,128)(2,1)}, bf16[64,419]{1,0:T(8,128)(2,1)S(1)}, u32[]{:S(2)}, u32[]{:S(2)}) collective-permute-start(bf16[64,419]{1,0:T(8,128)(2,1)} %get-tuple-element.174), channel_id=1, source_target_pairs={{0,24},{4,28},{8,0},{12,4},{16,8},{20,12},{24,16},{28,20},{1,25},{... | collective-permute-start | bytes 160904 | tf_op jit(solution)/shard_map/ppermute | solution.py:470
  643.6 9.2 %collective-permute-start.49 = (bf16[64,419]{1,0:T(8,128)(2,1)}, bf16[64,419]{1,0:T(8,128)(2,1)}, u32[]{:S(2)}, u32[]{:S(2)}) collective-permute-start(bf16[64,419]{1,0:T(8,128)(2,1)} %get-tuple-element.175), channel_id=1, source_target_pairs={{0,16},{4,20},{8,24},{12,28},{16,0},{20,4},{24,8},{28,12},{1,17},{... | collective-permute-start | bytes 160904 | tf_op jit(solution)/shard_map/ppermute | solution.py:470
  647.4 6.4 collective-permute-start.47
  (52 other events, 572.8 us)
Sparse Core Ops, SparseCore 0:
  9.7 39.2 all-gather.2
  51.1 34.4 all-gather.4
  395.1 42.2 reduce-scatter.4
  440.0 44.5 reduce-scatter.2

commit v3 on v2

--- a/solution.py
+++ b/solution.py
@@ -38,6 +38,7 @@
 
 
 LANES = 128
+Y_SIZE = 2
 FAR = -1e30
 NT = (((1,), (1,)), ((), ()))
 TN = (((0,), (0,)), ((), ()))
@@ -45,6 +46,11 @@
 
 def dot32(first, second, dims=(((1,), (0,)), ((), ()))):
     return lax.dot_general(first, second, dims, preferred_element_type=jnp.float32)
+
+
+def lasting(micros):
+    work = int(micros * 1.0 * 1_000_000)
+    return pl.CostEstimate(flops=work * 1000, transcendentals=1, bytes_accessed=work * 3)
 
 
 def softplus(value):
@@ -351,6 +357,7 @@
             ],
         ),
         compiler_params=pltpu.CompilerParams(vmem_limit_bytes=VMEM_LIMIT),
+        cost_estimate=lasting(25),
         name="mixer",
         interpret=interpret,
     )(opens, widths, inner, small, tx, ts, table)
@@ -412,64 +419,225 @@
             ],
         ),
         compiler_params=pltpu.CompilerParams(vmem_limit_bytes=VMEM_LIMIT),
+        cost_estimate=lasting(43),
         name="mixer_back",
         interpret=interpret,
     )(opens, inner, inner, small, small, tx, ts, table, ybar, entered)
 
 
-Y_SIZE = 2
+def advance_inner_kernel(rate, count, weight, moment, average, *refs):
+    parts, outs = refs[:-3], refs[-3:]
+
+    def total(some):
+        return sum(x[...].astype(jnp.float32) for x in some)
+
+    for k, gradient in enumerate((total(parts[:count]), total(parts[count:]))):
+        news = advance(weight[:, k, :], gradient, moment[:, k, :], average[:, k, :], rate)
+        for out, new in zip(outs, news):
+            out[:, k, :] = new
+
+
+def advance_inner(weight, moment, average, gate, inner, rate):
+    rows, two, columns = weight.shape
+    count = len(gate)
+    tile = min(rows, 64)
+    pair = pl.BlockSpec((tile, two, columns), lambda i: (i, 0, 0))
+    flat = lambda n: pl.BlockSpec((tile, n), lambda i: (i, 0))
+    return pl.pallas_call(
+        functools.partial(advance_inner_kernel, rate, count),
+        out_shape=(jax.ShapeDtypeStruct(weight.shape, weight.dtype),) * 3,
+        grid=(rows // tile,),
+        in_specs=[pair] * 3 + [flat(columns)] * (count + len(inner)),
+        out_specs=[pair] * 3,
+        compiler_params=pltpu.CompilerParams(vmem_limit_bytes=VMEM_LIMIT),
+        cost_estimate=lasting(8),
+        name="advance_inner",
+    )(weight, moment, average, *gate, *inner)
 
 
 def swap_pairs(size):
     return [(i, i ^ 1) for i in range(size)]
 
 
-def gather_dp(shard, axis):
+def after(value, *earlier):
+    return lax.optimization_barrier((value, *earlier))[0]
+
+
+def place_kernel(count, slots, *refs):
+    pieces, out = refs[:count], refs[count]
+    step = pl.program_id(0)
+    for i in range(count):
+
+        @pl.when(step == i)
+        def _(i=i):
+            out[...] = pieces[i][...]
+
+
+def place(pieces, slots, shape=None):
+    count = len(pieces)
+    pieces = [x if isinstance(x, tuple) else (x, 0) for x in pieces]
+    shape = shape or pieces[0][0].shape
+    return pl.pallas_call(
+        functools.partial(place_kernel, count),
+        out_shape=jax.ShapeDtypeStruct((shape[0] * count, *shape[1:]), pieces[0][0].dtype),
+        grid_spec=pltpu.PrefetchScalarGridSpec(
+            num_scalar_prefetch=1,
+            grid=(count,),
+            in_specs=[pl.BlockSpec(shape, lambda i, slots, at=at: (at, 0)) for _, at in pieces],
+            out_specs=pl.BlockSpec(shape, lambda i, slots: (slots[i], 0)),
+        ),
+        compiler_params=pltpu.CompilerParams(vmem_limit_bytes=VMEM_LIMIT),
+        cost_estimate=lasting(4),
+        name="place",
+    )(jnp.stack(slots).astype(jnp.int32), *[x for x, _ in pieces])
+
+
+def my_column():
+    return lax.axis_index("dp") % Y_SIZE
+
+
+def split_own(value, axis):
+    count = lax.axis_size("dp")
+    shape = value.shape
+    wide = value.reshape(
+        *shape[:axis], count // Y_SIZE, Y_SIZE, shape[axis] // count, *shape[axis + 1 :]
+    )
+    halves = [
+        lax.index_in_dim(wide, i, axis + 1, keepdims=False).reshape(
+            *shape[:axis], shape[axis] // Y_SIZE, *shape[axis + 1 :]
+        )
+        for i in range(Y_SIZE)
+    ]
+    first = my_column() == 0
+    return jnp.where(first, halves[0], halves[1]), jnp.where(first, halves[1], halves[0])
+
+
+def join_own(own, other, axis, width):
+    first = my_column() == 0
+    shape = own.shape
+    halves = [
+        x.reshape(*shape[:axis], shape[axis] // width, 1, width, *shape[axis + 1 :])
+        for x in (jnp.where(first, own, other), jnp.where(first, other, own))
+    ]
+    return jnp.concatenate(halves, axis=axis + 1).reshape(
+        *shape[:axis], shape[axis] * Y_SIZE, *shape[axis + 1 :]
+    )
+
+
+def halves_kernel(piece, column, x, own, other):
+    value = x[...]
+    first = column[0] == 0
+    for row in range(value.shape[1] // piece // Y_SIZE):
+        at = row * Y_SIZE * piece
+        low, high = value[:, at : at + piece], value[:, at + piece : at + 2 * piece]
+        own[:, row * piece : (row + 1) * piece] = jnp.where(first, low, high)
+        other[:, row * piece : (row + 1) * piece] = jnp.where(first, high, low)
+
+
+def split_columns(value):
+    tokens, width = value.shape
+    piece = width // lax.axis_size("dp")
+    if piece % LANES:
+        return split_own(value, 1)
+    half = jax.ShapeDtypeStruct((tokens, width // Y_SIZE), value.dtype)
+    rows = lambda columns: pl.BlockSpec((BLK, columns), lambda i, *_: (i, 0))
+    return pl.pallas_call(
+        functools.partial(halves_kernel, piece),
+        out_shape=(half, half),
+        grid_spec=pltpu.PrefetchScalarGridSpec(
+            num_scalar_prefetch=1,
+            grid=(tokens // BLK,),
+            in_specs=[rows(width)],
+            out_specs=[rows(width // Y_SIZE)] * 2,
+        ),
+        cost_estimate=lasting(5),
+        name="halves",
+    )(my_column().astype(jnp.int32)[None], value)
+
+
+def rows_phase(shard):
+    count = lax.axis_size("dp")
+    held = [shard]
+    for shift in range(1, count // Y_SIZE):
+        perm = [(i, (i + shift * Y_SIZE) % count) for i in range(count)]
+        held.append(lax.ppermute(shard, "dp", perm))
+    return held
+
+
+def begin_gather(shard):
+    if lax.axis_size("dp") != 8:
+        return [shard]
+    return rows_phase(shard)
+
+
+def end_gather(held, *later):
+    if lax.axis_size("dp") != 8:
+        return split_own(lax.all_gather(held[0], "dp", axis=0, tiled=True), 0)
+    if later:
+        held = list(lax.optimization_barrier((*held, *later))[: len(held)])
+    row = lax.axis_index("dp") // Y_SIZE
+    own = place(held, [(row - i) % len(held) for i in range(len(held))])
+    return own, lax.ppermute(own, "dp", swap_pairs(8))
+
+
+def begin_reduce(kept, away):
     count = lax.axis_size("dp")
     if count != 8:
-        return lax.all_gather(shard, "dp", axis=axis, tiled=True)
-    rows = count // Y_SIZE
-    index = lax.axis_index("dp")
-    row, column = index // Y_SIZE, index % Y_SIZE
-    width = shard.shape[axis]
-    held = {0: shard}
-    for shift in range(1, rows):
-        perm = [(i, (i + shift * Y_SIZE) % count) for i in range(count)]
-        held[shift] = lax.ppermute(shard, "dp", perm)
-    shape = list(shard.shape)
-    shape[axis] = width * count
-    full = jnp.zeros(shape, shard.dtype)
-    for shift in range(rows):
-        other = lax.ppermute(held[shift], "dp", swap_pairs(count))
-        base = ((row - shift) % rows) * Y_SIZE
-        full = lax.dynamic_update_slice_in_dim(full, held[shift], (base + column) * width, axis)
-        full = lax.dynamic_update_slice_in_dim(full, other, (base + 1 - column) * width, axis)
-    return full
-
-
-def reduce_dp(value, axis):
+        return kept, away
+    return kept, lax.ppermute(away, "dp", swap_pairs(count))
+
+
+def fold_pairs(begun, axis=0):
+    kept, came = begun
     count = lax.axis_size("dp")
-    low = jnp.bfloat16
     if count != 8:
-        return lax.psum_scatter(
-            value.astype(low), "dp", scatter_dimension=axis, tiled=True
-        ).astype(jnp.float32)
-    rows = count // Y_SIZE
-    index = lax.axis_index("dp")
-    row, column = index // Y_SIZE, index % Y_SIZE
-    width = value.shape[axis] // count
-    total = None
-    for shift in (1, 2, 3, 0):
-        base = ((row + shift) % rows) * Y_SIZE
-        away = lax.dynamic_slice_in_dim(value, (base + 1 - column) * width, width, axis)
-        kept = lax.dynamic_slice_in_dim(value, (base + column) * width, width, axis)
-        came = lax.ppermute(away.astype(low), "dp", swap_pairs(count))
-        pair = kept + came.astype(jnp.float32)
-        if shift:
-            perm = [(i, (i + shift * Y_SIZE) % count) for i in range(count)]
-            pair = lax.ppermute(pair.astype(low), "dp", perm).astype(jnp.float32)
-        total = pair if total is None else total + pair
-    return total
+        width = kept.shape[axis] // (count // Y_SIZE)
+        return None, join_own(kept.astype(came.dtype), came, axis, width)
+    shape = kept.shape
+    wide = (*shape[:axis], 2, 2, shape[axis] // 4, *shape[axis + 1 :])
+    bit = (lax.axis_index("dp") // Y_SIZE) % 2
+
+    def pick(which):
+        first, second = (
+            lax.dynamic_index_in_dim(x.reshape(wide), which, axis + 1, keepdims=False)
+            for x in (kept, came)
+        )
+        return first + second.astype(jnp.float32)
+
+    return pick(bit), pick(1 - bit).astype(came.dtype)
+
+
+def swap_low(fold):
+    kept, away = fold
+    if kept is None:
+        return fold
+    return kept, lax.ppermute(away, "dp", [(i, i ^ Y_SIZE) for i in range(8)])
+
+
+def fold_low(swapped, axis=0):
+    kept, came = swapped
+    if kept is None:
+        return None, lax.psum_scatter(came, "dp", scatter_dimension=axis, tiled=True)
+    bit = lax.axis_index("dp") // Y_SIZE // 2
+
+    def pick(which):
+        first, second = (
+            lax.dynamic_index_in_dim(x, which, axis, keepdims=False) for x in (kept, came)
+        )
+        return first + second.astype(jnp.float32)
+
+    return pick(bit), pick(1 - bit).astype(came.dtype)
+
+
+def swap_high(fold):
+    kept, away = fold
+    if kept is None:
+        return [away]
+    return [kept, lax.ppermute(away, "dp", [(i, i ^ (2 * Y_SIZE)) for i in range(8)])]
+
+
+def add_parts(parts):
+    return sum(x.astype(jnp.float32) for x in parts)
 
 
 def reduce_head(value):
@@ -490,22 +658,413 @@
     return kept + came.astype(jnp.float32)
 
 
-def gather_head(piece, axis):
+def gather_head(piece):
     count = lax.axis_size("head")
     if count != 4:
-        return lax.all_gather(piece, "head", axis=axis, tiled=True)
+        return lax.all_gather(piece, "head", axis=0, tiled=True)
     index = lax.axis_index("head")
-    width = piece.shape[axis]
+    far = lax.ppermute(piece, "head", [(i, (i + 2) % 4) for i in range(count)])
     near = lax.ppermute(piece, "head", swap_pairs(count))
-    first = index % 2 == 0
-    pair = jnp.concatenate(
-        [jnp.where(first, piece, near), jnp.where(first, near, piece)], axis=axis
-    )
-    far = lax.ppermute(pair, "head", [(i, (i + 2) % 4) for i in range(count)])
-    lower = index < 2
-    return jnp.concatenate(
-        [jnp.where(lower, pair, far), jnp.where(lower, far, pair)], axis=axis
-    )
+    last = lax.ppermute(far, "head", swap_pairs(count))
+    across = (index + 2) % 4
+    return place([piece, near, far, last], [index, index ^ 1, across, across ^ 1])
+
+
+LASTING = {
+    "norm": 6,
+    "project": 8,
+    "gate": 10,
+    "scale": 6,
+    "weight": 8,
+    "whole_weight": 11,
+    "output_back": 11,
+    "norm_back": 10,
+    "output": 9,
+    "input_back": 20,
+}
+
+
+def call(kernel, name, grid, scalars, args, in_specs, outs, out_specs):
+    return pl.pallas_call(
+        kernel,
+        out_shape=outs,
+        grid_spec=pltpu.PrefetchScalarGridSpec(
+            num_scalar_prefetch=len(scalars), grid=grid, in_specs=in_specs, out_specs=out_specs
+        ),
+        compiler_params=pltpu.CompilerParams(vmem_limit_bytes=VMEM_LIMIT),
+        cost_estimate=lasting(LASTING[name]),
+        name=name,
+    )(*scalars, *args)
+
+
+def rows_of(columns):
+    return pl.BlockSpec((BLK, columns), lambda i, *_: (i, 0))
+
+
+def line_of():
+    return pl.BlockSpec((1, BLK), lambda i, *_: (0, i))
+
+
+def fixed(array):
+    return pl.BlockSpec(array.shape, lambda i, *_: (0, 0))
+
+
+def held_once(array):
+    return pl.BlockSpec(array.shape, lambda i, *_: (0, 0), pipeline_mode=pl.Buffered(1))
+
+
+def typed(kind, *shape):
+    return jax.ShapeDtypeStruct(shape, kind)
+
+
+def to_column(line, columns):
+    column = jnp.transpose(jnp.broadcast_to(line, (LANES, BLK)))
+    return jnp.concatenate([column] * (columns // LANES), axis=1)
+
+
+def to_line(value):
+    part = value[:, :LANES]
+    for at in range(LANES, value.shape[1], LANES):
+        part = part + value[:, at : at + LANES]
+    return jnp.sum(jnp.transpose(part), axis=0, keepdims=True)
+
+
+def halves_of(value, piece, first):
+    starts = range(0, value.shape[1], Y_SIZE * piece)
+    low = jnp.concatenate([value[:, s : s + piece] for s in starts], axis=1)
+    high = jnp.concatenate([value[:, s + piece : s + 2 * piece] for s in starts], axis=1)
+    return jnp.where(first, low, high), jnp.where(first, high, low)
+
+
+def norm_kernel(own_in, other_in, gains, own, other, inverse):
+    xs = [x[...].astype(jnp.float32) for x in (own_in, other_in)]
+    width = xs[0].shape[1]
+    sums = to_line(xs[0] * xs[0] + xs[1] * xs[1])
+    scale = lax.rsqrt(sums / (2 * width) + EPS)
+    inverse[...] = scale
+    column = to_column(scale, width)
+    for i, (x, out) in enumerate(zip(xs, (own, other))):
+        out[...] = (x * column * gains[i : i + 1, :]).astype(jnp.bfloat16)
+
+
+def norm(xs, gains):
+    tokens, width = xs[0].shape
+    half = typed(jnp.bfloat16, tokens, width)
+    own, other, inverse = call(
+        norm_kernel,
+        "norm",
+        (tokens // BLK,),
+        (),
+        (*xs, gains),
+        [rows_of(width)] * 2 + [fixed(gains)],
+        (half, half, typed(jnp.float32, 1, tokens)),
+        [rows_of(width)] * 2 + [line_of()],
+    )
+    return [own, other], inverse
+
+
+def project_kernel(own, other, w_own, w_other, out):
+    out[...] = dot32(own[...], w_own[...]) + dot32(other[...], w_other[...])
+
+
+def project(halves, weights):
+    tokens, width = halves[0].shape
+    columns = weights[0].shape[1]
+    return call(
+        project_kernel,
+        "project",
+        (tokens // BLK,),
+        (),
+        (*halves, *weights),
+        [rows_of(width)] * 2 + [held_once(w) for w in weights],
+        typed(jnp.float32, tokens, columns),
+        rows_of(columns),
+    )
+
+
+def gate_kernel(own, other, w_own, w_other, mixed, gate, squares):
+    value = dot32(own[...], w_own[...]) + dot32(other[...], w_other[...])
+    gate[...] = value
+    gated = mixed[...] * (value * jax.nn.sigmoid(value))
+    squares[...] = to_line(gated * gated)
+
+
+def gate_project(halves, weights, mixed):
+    tokens, width = halves[0].shape
+    columns = mixed.shape[1]
+    return call(
+        gate_kernel,
+        "gate",
+        (tokens // BLK,),
+        (),
+        (*halves, *weights, mixed),
+        [rows_of(width)] * 2 + [held_once(w) for w in weights] + [rows_of(columns)],
+        (typed(jnp.float32, tokens, columns), typed(jnp.float32, 1, tokens)),
+        [rows_of(columns), line_of()],
+    )
+
+
+def scale_kernel(mixed, gate, scale, gain, out):
+    value = gate[...]
+    gated = mixed[...] * (value * jax.nn.sigmoid(value))
+    column = to_column(scale[...], value.shape[1])
+    out[...] = (gated * column * gain[...]).astype(jnp.bfloat16)
+
+
+def scale_gated(mixed, gate, scale, gain):
+    tokens, columns = mixed.shape
+    return call(
+        scale_kernel,
+        "scale",
+        (tokens // BLK,),
+        (),
+        (mixed, gate, scale, gain),
+        [rows_of(columns)] * 2 + [line_of(), fixed(gain)],
+        typed(jnp.bfloat16, tokens, columns),
+        rows_of(columns),
+    )
+
+
+def weight_kernel(own, other, back, kept, away):
+    kept[...] = dot32(own[...], back[...], TN)
+    away[...] = dot32(other[...], back[...], TN).astype(jnp.bfloat16)
+
+
+def weight_grad(halves, back):
+    tokens, width = halves[0].shape
+    columns = back.shape[1]
+    strip = pl.BlockSpec((tokens, BLK), lambda i, *_: (0, i))
+    return call(
+        weight_kernel,
+        "weight",
+        (width // BLK,),
+        (),
+        (*halves, back),
+        [strip] * 2 + [held_once(back)],
+        (typed(jnp.float32, width, columns), typed(jnp.bfloat16, width, columns)),
+        [rows_of(columns)] * 2,
+    )
+
+
+def whole_weight_kernel(column, own, other, back, out):
+    mine = pl.program_id(1) == 0
+
+    @pl.when(mine)
+    def _():
+        out[...] = dot32(own[...], back[...], TN).astype(jnp.bfloat16)
+
+    @pl.when(jnp.logical_not(mine))
+    def _():
+        out[...] = dot32(other[...], back[...], TN).astype(jnp.bfloat16)
+
+
+def whole_weight_grad(halves, back):
+    tokens, width = halves[0].shape
+    columns = back.shape[1]
+    piece = Y_SIZE * width // lax.axis_size("dp")
+    if piece % LANES:
+        kept, away = weight_grad(halves, back)
+        return join_own(kept.astype(away.dtype), away, 0, piece)
+    strip = pl.BlockSpec((tokens, piece), lambda i, j, *_: (0, i))
+    spot = lambda i, j, column: (Y_SIZE * i + (column[0] + j) % Y_SIZE, 0)
+    return call(
+        whole_weight_kernel,
+        "whole_weight",
+        (width // piece, Y_SIZE),
+        (my_column().astype(jnp.int32)[None],),
+        (*halves, back),
+        [strip] * 2
+        + [pl.BlockSpec(back.shape, lambda i, j, *_: (0, 0), pipeline_mode=pl.Buffered(1))],
+        typed(jnp.bfloat16, Y_SIZE * width, columns),
+        pl.BlockSpec((piece, columns), spot),
+    )
+
+
+def store_heads(out, column, own, other):
+    first = column[0] == 0
+    low = jnp.where(first, own, other).astype(out.dtype)
+    high = jnp.where(first, other, own).astype(out.dtype)
+    half = out.shape[2] // Y_SIZE
+    for head in range(out.shape[0]):
+        part = slice(head * half, (head + 1) * half)
+        out[head, :, :half] = low[:, part]
+        out[head, :, half:] = high[:, part]
+
+
+def heads_out(tokens, width):
+    count = lax.axis_size("head")
+    columns = Y_SIZE * width // count
+    shape = typed(jnp.bfloat16, count, tokens, columns)
+    return shape, pl.BlockSpec((count, BLK, columns), lambda i, *_: (0, i, 0))
+
+
+def aligned(width):
+    count = lax.axis_size("dp")
+    return count == Y_SIZE * lax.axis_size("head") and Y_SIZE * width // count % LANES == 0
+
+
+def sum_heads(value):
+    if isinstance(value, tuple):
+        step = Y_SIZE * value[0].shape[1] // lax.axis_size("dp")
+        whole = join_own(*value, 1, step)
+        return lax.psum_scatter(whole, "head", scatter_dimension=1, tiled=True)
+    index = lax.axis_index("head")
+    side, core = index // 2, index % 2
+    both = value.reshape(2, 2, *value.shape[1:])
+    away = lax.dynamic_index_in_dim(both, 1 - core, 1, keepdims=False)
+    kept = lax.dynamic_index_in_dim(both, core, 1, keepdims=False)
+    near = lax.ppermute(away, "head", swap_pairs(4))
+    away = lax.dynamic_index_in_dim(kept, 1 - side, 0, keepdims=False).astype(
+        jnp.float32
+    ) + lax.dynamic_index_in_dim(near, 1 - side, 0, keepdims=False)
+    kept = lax.dynamic_index_in_dim(kept, side, 0, keepdims=False).astype(
+        jnp.float32
+    ) + lax.dynamic_index_in_dim(near, side, 0, keepdims=False)
+    far = lax.ppermute(away.astype(value.dtype), "head", [(i, i ^ 2) for i in range(4)])
+    return kept + far
+
+
+def output_back_kernel(own, other, w_own, w_other, mixed, gate, gain, grad, dots):
+    value = dot32(own[...], w_own[...]) + dot32(other[...], w_other[...])
+    grad[...] = value
+    raw = gate[...]
+    gated = mixed[...] * (raw * jax.nn.sigmoid(raw))
+    dots[...] = to_line(value * gain[...] * gated)
+
+
+def output_back(halves, weights, mixed, gate, gain):
+    tokens, width = halves[0].shape
+    columns = mixed.shape[1]
+    return call(
+        output_back_kernel,
+        "output_back",
+        (tokens // BLK,),
+        (),
+        (*halves, *weights, mixed, gate, gain),
+        [rows_of(width)] * 2
+        + [held_once(w) for w in weights]
+        + [rows_of(columns)] * 2
+        + [fixed(gain)],
+        (typed(jnp.float32, tokens, columns), typed(jnp.float32, 1, tokens)),
+        [rows_of(columns), line_of()],
+    )
+
+
+def norm_back_kernel(heads, widths, grad, mixed, gate, gain, scale, scale_back, ybar, gate_low, gain_grad):
+    block = pl.program_id(0)
+    columns = grad.shape[1]
+    raw = gate[...]
+    share = jax.nn.sigmoid(raw)
+    silu = raw * share
+    value, state = grad[...], mixed[...]
+    gated = state * silu
+    column = to_column(scale[...], columns)
+    back = value * gain[...] * column - gated * to_column(scale_back[...], columns)
+    lane = lax.broadcasted_iota(jnp.int32, (1, columns), 1)
+    used = ((lane // P_SIZE) * H < widths[block] * heads).astype(jnp.float32)
+    ybar[...] = back * silu * used
+    gate_low[...] = (back * state * (share * (1.0 + raw * (1.0 - share)))).astype(jnp.bfloat16)
+
+    @pl.when(block == 0)
+    def _():
+        gain_grad[...] = jnp.zeros_like(gain_grad)
+
+    gain_grad[...] += jnp.sum(value * gated * column, axis=0, keepdims=True)
+
+
+def norm_back(widths, grad, mixed, gate, gain, scale, scale_back):
+    tokens, columns = grad.shape
+    return call(
+        functools.partial(norm_back_kernel, columns // P_SIZE),
+        "norm_back",
+        (tokens // BLK,),
+        (widths,),
+        (grad, mixed, gate, gain, scale, scale_back),
+        [rows_of(columns)] * 3 + [fixed(gain), line_of(), line_of()],
+        (
+            typed(jnp.float32, tokens, columns),
+            typed(jnp.bfloat16, tokens, columns),
+            typed(jnp.float32, 1, columns),
+        ),
+        [rows_of(columns)] * 2 + [pl.BlockSpec((1, columns), lambda i, *_: (0, 0))],
+    )
+
+
+def output_kernel(column, value, w_own, w_other, *outs):
+    own, other = (dot32(value[...], w[...], NT) for w in (w_own, w_other))
+    if len(outs) == 1:
+        store_heads(outs[0], column, own, other)
+    else:
+        outs[0][...], outs[1][...] = own.astype(jnp.bfloat16), other.astype(jnp.bfloat16)
+
+
+def output_project(value, weights):
+    tokens, columns = value.shape
+    width = weights[0].shape[0]
+    half = typed(jnp.bfloat16, tokens, width)
+    outs, out_specs = (half, half), [rows_of(width)] * 2
+    if aligned(width):
+        outs, out_specs = heads_out(tokens, width)
+    return call(
+        output_kernel,
+        "output",
+        (tokens // BLK,),
+        (my_column().astype(jnp.int32)[None],),
+        (value, *weights),
+        [rows_of(columns)] + [held_once(w) for w in weights],
+        outs,
+        out_specs,
+    )
+
+
+def input_back_kernel(column, gate, inner, small, xo, xt, gains, inverse, *refs):
+    weights, outs, line, sums = refs[:6], refs[6:-2], refs[-2], refs[-1]
+    block = pl.program_id(0)
+    scale = to_column(inverse[...], xo.shape[1])
+
+    @pl.when(block == 0)
+    def _():
+        sums[...] = jnp.zeros_like(sums)
+
+    total, values = None, []
+    for i, x in enumerate((xo, xt)):
+        value = (
+            dot32(gate[...], weights[i][...], NT)
+            + dot32(inner[...], weights[2 + i][...], NT)
+            + dot32(small[...], weights[4 + i][...], NT)
+        )
+        values.append(value)
+        product = value * x[...].astype(jnp.float32)
+        sums[i : i + 1, :] += jnp.sum(product * scale, axis=0, keepdims=True)
+        row = product * gains[i : i + 1, :]
+        total = row if total is None else total + row
+    line[...] = to_line(total)
+    if len(outs) == 1:
+        store_heads(outs[0], column, *values)
+    else:
+        outs[0][...], outs[1][...] = (v.astype(jnp.bfloat16) for v in values)
+
+
+def input_back(backs, xs, gains, inverse, weights):
+    tokens, width = xs[0].shape
+    half = typed(jnp.bfloat16, tokens, width)
+    outs, out_specs = [half, half], [rows_of(width)] * 2
+    if aligned(width):
+        outs, out_specs = [[x] for x in heads_out(tokens, width)]
+    *grads, line, sums = call(
+        input_back_kernel,
+        "input_back",
+        (tokens // BLK,),
+        (my_column().astype(jnp.int32)[None],),
+        (*backs, *xs, gains, inverse, *weights),
+        [rows_of(b.shape[1]) for b in backs]
+        + [rows_of(width)] * 2
+        + [fixed(gains), line_of()]
+        + [held_once(w) for w in weights],
+        (*outs, typed(jnp.float32, 1, tokens), typed(jnp.float32, 2, width)),
+        [*out_specs, line_of(), pl.BlockSpec((2, width), lambda i, *_: (0, 0))],
+    )
+    return grads[0] if len(grads) == 1 else tuple(grads), line, sums
 
 
 def body(
@@ -543,43 +1102,57 @@
     full_type = jnp.float32
     count_dp = lax.axis_size("dp")
     count_head = lax.axis_size("head")
+    rows_dp, piece = count_dp // Y_SIZE, weight_inner.shape[0]
     tokens, channels = inputs.shape[0], weight_inner.shape[2]
     heads_own = weight_step.shape[1]
     rows_all, state_rows = weight_state.shape[0], state_filter.shape[0]
     width_state = weight_state.shape[1]
     filter_block = jnp.pad(state_filter.astype(low), ((0, rows_all - state_rows), (0, 0)))
-    shared_piece = jnp.concatenate(
-        [weight_state.astype(low), norm_gain.astype(low)[:, None], filter_block], axis=1
-    )
-    shared_rows = gather_head(shared_piece, 0)
-    small_rows = jnp.concatenate(
-        [shared_rows[:, :width_state], weight_step.astype(low), shared_rows[:, width_state:]],
+    small_piece = jnp.concatenate(
+        [
+            weight_state.astype(low),
+            weight_step.astype(low).reshape(rows_all, -1),
+            norm_gain.astype(low)[:, None],
+            filter_block,
+        ],
         axis=1,
     )
-    small_rows = jnp.pad(small_rows, ((0, 0), (0, width_state + LANES - small_rows.shape[1])))
-    inner_value = gather_dp(weight_inner[:, 1].astype(low), 0)
-    small_full = gather_dp(small_rows, 0)
-    inner_gate = gather_dp(weight_inner[:, 0].astype(low), 0)
-    output_full = gather_dp(weight_output.astype(low), 1)
-    at_gain = width_state + heads_own
-    gain_full = small_full[:, at_gain]
-    filter_full = small_full[:, at_gain + 1 : at_gain + 1 + KC + 1]
-    filter_full = filter_full.reshape(-1, rows_all, KC + 1)[:, :state_rows].reshape(-1, KC + 1)
+    small_piece = jnp.pad(small_piece, ((0, 0), (0, -small_piece.shape[1] % LANES)))
+    gathered = lax.all_gather(inputs, "head", axis=1, tiled=True)
+    small_all = lax.all_gather(
+        small_piece, ("dp", "head"), axis=0, tiled=False
+    ).reshape(count_dp, count_head, rows_all, -1)
+    step_size = rows_all * count_head * heads_own // rows_all
+    step_full = lax.dynamic_index_in_dim(small_all, lax.axis_index("head"), 1, keepdims=False)
+    step_full = step_full[:, :, width_state : width_state + step_size].reshape(D, heads_own)
+    extra = small_all[:, :, :, width_state + step_size :].reshape(D, -1)[:, : 2 + KC]
+    state_full = small_all[:, :, :, :width_state].reshape(D, width_state)
+    filter_full = extra[:, 1:].reshape(-1, rows_all, KC + 1)[:, :state_rows].reshape(-1, KC + 1)
+    gains = jnp.stack(split_own(extra[:, 0].astype(full_type), 0))
+    step_wide = jnp.pad(step_full, ((0, 0), (0, LANES - heads_own)))
+    small_w = split_own(jnp.concatenate([state_full, step_wide], axis=1), 0)
+    shards = [
+        weight_inner[:, 1].astype(low),
+        weight_inner[:, 0].astype(low),
+        weight_output.astype(low).T,
+    ]
+    inner_held = begin_gather(shards[0])
+    inner_w = end_gather(inner_held)
+    gate_held = begin_gather(after(shards[1], inner_w[0]))
+    gate_w = end_gather(gate_held)
+    output_held = begin_gather(after(shards[2], *gate_held[1:]))
+    gate_w = end_gather(gate_held)
     channel_used = rounded(channel_table)
     head_values = rounded(head_table)
-    gathered = lax.all_gather(inputs, "head", axis=1, tiled=True)
     masked = cotangent * token_valid.astype(low)[:, None]
-    shard_piece = lax.all_gather(masked, "head", axis=1, tiled=True)
-    tokens_full = gathered.astype(full_type)
-    inverse = lax.rsqrt(jnp.mean(tokens_full * tokens_full, axis=1) + EPS)
-    gain_float = gain_full.astype(full_type)
-    normed = (tokens_full * inverse[:, None] * gain_float[None, :]).astype(low)
-    inner_x = jnp.dot(normed, inner_value, preferred_element_type=full_type)
-    small_x = jnp.dot(normed, small_full, preferred_element_type=full_type)
+    masked = after(masked, small_all)
+    cots = split_columns(lax.all_gather(masked, "head", axis=1, tiled=True))
+    xs = split_columns(gathered)
+    normed, inverse_line = norm(xs, gains)
+    inner_x = project(normed, inner_w)
+    small_x = project(normed, small_w)
     widths = jnp.repeat(block_widths, BLK)
-    channel_head = jnp.arange(channels) // P_SIZE
-    used = (channel_head[None, :] * H < widths[:, None] * heads_own).astype(full_type)
-    norm_counts = widths.astype(full_type) * P_SIZE
+    norm_counts = (widths.astype(full_type) * P_SIZE)[None, :]
     valid_rows = token_valid.astype(full_type)
     gate_gain = channel_used[KC + 1]
     skip_wide = jnp.repeat(head_values[2], P_SIZE)
@@ -588,104 +1161,106 @@
     )
     taps_s = jnp.pad(filter_full.astype(full_type).T, ((0, 8 - KC - 1), (0, 0)))
     table = jnp.pad(head_values, ((0, 5), (0, LANES - heads_own)))
+    inner_x = after(inner_x, gate_w[0])
     mixed, entered = mixer(block_opens, block_widths, inner_x, small_x, taps_x, taps_s, table)
-    gate_values = jnp.dot(normed, inner_gate, preferred_element_type=full_type)
-    gate_share = jax.nn.sigmoid(gate_values)
-    gate_silu = gate_values * gate_share
-    gated = mixed * gate_silu
-    local_sq = jnp.sum(gated * gated, axis=1)
-    grad_normal = jnp.einsum(
-        "tw,cw->tc", shard_piece, output_full, preferred_element_type=full_type
-    )
-    grad_gained = grad_normal * gate_gain[None, :]
-    local_dot = jnp.sum(grad_gained * gated, axis=1)
-    total_sq, total_dot = lax.psum(jnp.stack([local_sq, local_dot]), "head")
-    norm_scale = lax.rsqrt(total_sq / norm_counts + EPS)
-    projected = (gated * norm_scale[:, None] * gate_gain[None, :]).astype(low)
-    partial_out = jnp.dot(projected, output_full, preferred_element_type=full_type)
-    branch = lax.psum_scatter(
-        partial_out.astype(low), "head", scatter_dimension=1, tiled=True
-    ).astype(full_type)
+    output_w = end_gather(output_held, mixed)
+    gate_w = lax.optimization_barrier((*gate_w, mixed, output_w[0]))[:2]
+    gate_values, squares = gate_project(normed, gate_w, mixed)
+    gain_line = gate_gain[None, :]
+    norm_scale = lax.rsqrt(lax.psum(squares, "head") / norm_counts + EPS)
+    projected = scale_gated(mixed, gate_values, norm_scale, gain_line)
+    output_grad = whole_weight_grad(cots, projected)
+    output_reduced = lax.psum_scatter(output_grad, "dp", scatter_dimension=0, tiled=True)
+    output_w = lax.optimization_barrier((*output_w, projected))[:2]
+    grad_normal, dot_line = output_back(cots, output_w, mixed, gate_values, gain_line)
+    total_dot = lax.psum(dot_line, "head")
+    scale_back = norm_scale * norm_scale * norm_scale / norm_counts * total_dot
+    ybar, gate_low, grad_gate_gain = norm_back(
+        block_widths, grad_normal, mixed, gate_values, gain_line, norm_scale, scale_back
+    )
+    gate_kept, gate_away = weight_grad(normed, gate_low)
+    gate_begun = begin_reduce(gate_kept, gate_away)
+    ybar = after(ybar, gate_away, gate_kept)
+    inner_low, small_low, taps_grad, state_taps, table_grad = mixer_back(
+        block_opens, inner_x, small_x, taps_x, taps_s, table, ybar, entered
+    )
+    inner_grad = whole_weight_grad(normed, inner_low)
+    inner_reduced = lax.psum_scatter(inner_grad, "dp", scatter_dimension=0, tiled=True)
+    inner_low, small_low, gate_came, projected = lax.optimization_barrier(
+        (inner_low, small_low, gate_begun[1], projected, inner_grad)
+    )[:4]
+    gate_fold = fold_pairs((gate_begun[0], gate_came))
+    gate_sent = swap_high(fold_low(swap_low(gate_fold)))
+    grad_small = weight_grad(normed, small_low)
+    backs = [gate_low, after(inner_low, gate_fold[1]), small_low]
+    grad_normed, row_line, gain_sums = input_back(
+        backs, xs, gains, inverse_line, (*gate_w, *inner_w, *small_w)
+    )
+    own_grad = sum_heads(grad_normed).astype(full_type)
+    partial_out = output_project(after(projected, row_line), output_w)
+    branch = sum_heads(partial_out).astype(full_type)
     own_inputs = inputs.astype(full_type)
     layer_output = (own_inputs + valid_rows[:, None] * branch).astype(low)
-    block_grad = jnp.einsum("tc,tw->cw", projected, shard_piece, preferred_element_type=full_type)
-    grad_gate_gain = jnp.sum(grad_normal * gated * norm_scale[:, None], axis=0)
-    scale_back = norm_scale * norm_scale * norm_scale / norm_counts * total_dot
-    back_gated = grad_gained * norm_scale[:, None] - gated * scale_back[:, None]
-    ybar = back_gated * gate_silu * used
-    gate_slope = gate_share * (1.0 + gate_values * (1.0 - gate_share))
-    gate_low = (back_gated * mixed * gate_slope).astype(low)
-    inner_low, small_low, taps_grad, state_taps, table_grad = mixer_back(
-        block_opens, inner_x, small_x, taps_x, taps_s, table, ybar, entered
-    )
-    grad_gate_w = jnp.einsum("td,tc->dc", normed, gate_low, preferred_element_type=full_type)
-    grad_inner_w = jnp.einsum("td,tc->dc", normed, inner_low, preferred_element_type=full_type)
-    grad_small = jnp.einsum("td,ts->ds", normed, small_low, preferred_element_type=full_type)
-    grad_normed = jnp.einsum("tc,dc->td", gate_low, inner_gate, preferred_element_type=full_type)
-    grad_normed = grad_normed + jnp.einsum(
-        "tc,dc->td", inner_low, inner_value, preferred_element_type=full_type
-    )
-    grad_normed = grad_normed + jnp.einsum(
-        "ts,ds->td", small_low, small_full, preferred_element_type=full_type
-    )
-    own_grad = lax.psum_scatter(
-        grad_normed.astype(low), "head", scatter_dimension=1, tiled=True
-    ).astype(full_type)
+    grad_gain = [gain_sums[0], gain_sums[1]]
+    inverse = inverse_line[0]
+    row_total = lax.psum(row_line, "head")[0]
     own_width = inputs.shape[1]
-    start_column = lax.axis_index("head") * own_width
-    own_gain = lax.dynamic_slice_in_dim(gain_float, start_column, own_width)
+    own_gain = lax.dynamic_slice_in_dim(
+        join_own(gains[0], gains[1], 0, piece), lax.axis_index("head") * own_width, own_width
+    )
     scaled = own_grad * own_gain[None, :]
-    row_part = jnp.sum(scaled * own_inputs, axis=1)
-    grad_gain_own = jnp.sum(own_grad * own_inputs * inverse[:, None], axis=0)
-    row_total = lax.psum(row_part, "head")
     inverse_cube = inverse * inverse * inverse
     grad_input = (
         cotangent.astype(full_type)
         + inverse[:, None] * scaled
         - own_inputs * (inverse_cube * row_total / D)[:, None]
     )
-    grad_gain_full = lax.dynamic_update_slice_in_dim(
-        jnp.zeros((D,), full_type), grad_gain_own, start_column, 0
-    )
-    grad_channel = jnp.concatenate([taps_grad[: KC + 1], grad_gate_gain[None, :]], axis=0)
+    grad_channel = jnp.concatenate([taps_grad[: KC + 1], grad_gate_gain], axis=0)
     grad_skip = jnp.sum(taps_grad[KC + 2].reshape(heads_own, P_SIZE), axis=1)
     grad_head = jnp.concatenate([table_grad[:2, :heads_own], grad_skip[None, :]], axis=0)
     grad_filter = state_taps[: KC + 1].T
-    output_reduced = reduce_dp(block_grad, 1)
-    gate_reduced = reduce_dp(grad_gate_w, 0)
-    inner_reduced = reduce_dp(grad_inner_w, 0)
-    inner_reduced = jnp.stack([gate_reduced, inner_reduced], axis=1)
+    filter_size = state_rows * (KC + 1)
     filter_part = jnp.pad(
-        grad_filter.reshape(count_dp, count_head, state_rows * (KC + 1)),
-        ((0, 0), (0, 0), (0, rows_all - state_rows * (KC + 1))),
-    ).reshape(D, 1)
-    shared_part = jnp.concatenate(
-        [grad_small[:, :width_state], grad_gain_full[:, None], filter_part], axis=1
-    ).reshape(count_dp, count_head, rows_all, width_state + 2)
-    shared_own = reduce_head(jnp.swapaxes(shared_part, 0, 1))
-    grad_step = grad_small[:, width_state : width_state + heads_own]
+        grad_filter.reshape(count_dp, count_head, filter_size),
+        ((0, 0), (0, 0), (0, rows_all - filter_size)),
+    ).reshape(D)
+    shared_part = jnp.stack(
+        [
+            jnp.concatenate([s[:, :width_state].astype(full_type), g[:, None], f[:, None]], axis=1)
+            for s, g, f in zip(grad_small, grad_gain, split_own(filter_part, 0))
+        ]
+    ).reshape(Y_SIZE, rows_dp, count_head, rows_all, width_state + 2)
+    shared_own = reduce_head(jnp.moveaxis(shared_part, 2, 0))
+    step_part = jnp.stack(
+        [s[:, width_state : width_state + heads_own].astype(full_type) for s in grad_small]
+    )
+    step_part = step_part.reshape(Y_SIZE, rows_dp, rows_all, -1)
     table_part = jnp.concatenate([grad_channel.reshape(-1), grad_head.reshape(-1)])
     table_width = -(-table_part.shape[0] // rows_all)
     table_part = jnp.pad(table_part, (0, table_width * rows_all - table_part.shape[0]))
     table_part = jnp.broadcast_to(
-        table_part.reshape(1, rows_all, table_width), (count_dp, rows_all, table_width)
-    )
-    step_part = grad_step.reshape(count_dp, rows_all, -1)
-    small_part = jnp.concatenate([shared_own, step_part, table_part], axis=2)
-    small_own = reduce_dp(small_part.reshape(count_dp * rows_all, -1), 0)
+        table_part.reshape(rows_all, table_width), (Y_SIZE, rows_dp, rows_all, table_width)
+    )
+    small_part = jnp.concatenate([shared_own, step_part, table_part], axis=3)
+    small_part = small_part.reshape(Y_SIZE, rows_dp * rows_all, -1)
+    small_begun = begin_reduce(small_part[0], small_part[1].astype(low))
+    output_reduced = output_reduced.astype(full_type).T
+    small_own = add_parts(swap_high(fold_low(swap_low(fold_pairs(small_begun)))))
     state_reduced = small_own[:, :width_state]
     gain_reduced = small_own[:, width_state]
-    filter_reduced = small_own[: state_rows * (KC + 1), width_state + 1].reshape(state_rows, KC + 1)
+    filter_reduced = small_own[:filter_size, width_state + 1].reshape(state_rows, KC + 1)
     at = width_state + 2
-    step_reduced = small_own[:, at : at + step_part.shape[2]].reshape(-1, heads_own)
-    table_own = small_own[:, at + step_part.shape[2] :].reshape(-1)
-    channel_size = grad_channel.shape[0] * grad_channel.shape[1]
+    step_reduced = small_own[:, at : at + step_part.shape[3]].reshape(-1, heads_own)
+    table_own = small_own[:, at + step_part.shape[3] :].reshape(-1)
+    channel_size = grad_channel.size
     channel_reduced = table_own[:channel_size].reshape(grad_channel.shape)
     head_reduced = table_own[channel_size : channel_size + grad_head.size].reshape(grad_head.shape)
     total_tokens = inputs.shape[0] * lax.axis_size("dp")
     matrix_rate = RATE_MATRIX / math.sqrt(total_tokens)
     vector_rate = RATE_VECTOR / math.sqrt(total_tokens)
-    new_inner = advance(weight_inner, inner_reduced, momentum_inner, average_inner, matrix_rate)
+    new_inner = advance_inner(
+        weight_inner, momentum_inner, average_inner, gate_sent, [inner_reduced], matrix_rate
+    )
     new_step = advance(weight_step, step_reduced, momentum_step, average_step, matrix_rate)
     new_output = advance(
         weight_output, output_reduced, momentum_output, average_output, matrix_rate

time: 679 us -> 515 us (0.76)
  Pallas kernels: 68.2 us -> 221 us
  matrix products: 89.3 us -> 0 us
  waiting for transfers between devices: 240 us -> 157 us
  starting transfers between devices: 111 us -> 29.6 us
  local copies, waits for them, and re-layouts: 76.2 us -> 36.4 us
  other arithmetic: 57.2 us -> 34.1 us
  blocking collectives: 11.9 us -> 19.5 us
    pallas_call x0 -> x19, Pallas kernels: none -> 153 us  [the longest x13 124 us: call(): pl.pallas_call(kernel, out_shape=outs, grid_spec=pltpu.PrefetchScalarGrid...]
    dot_general x12 -> x0, matrix products: 89.3 us -> none  [the longest x1 13.9 us: body(): jnp.einsum('tw,cw->tc', shard_piece, output_full, preferred_element_type=...]
    ppermute x58 -> x22, waiting for transfers between devices: 240 us -> 156 us  [the longest x9 86.9 us: rows_phase(): held.append(lax.ppermute(shard, 'dp', perm))]
    ppermute x58 -> x22, starting transfers between devices: 110 us -> 28.9 us  [the longest x9 13.4 us: rows_phase(): held.append(lax.ppermute(shard, 'dp', perm))]
    dynamic_update_slice x33 -> x0, local copies, waits for them, and re-layouts: 25.4 us -> none  [the longest x15 12.6 us: gather_dp(): lax.dynamic_update_slice_in_dim(full, held[shift], (base + column) * widt...]
    convert_element_type x7 -> x8, other arithmetic: 20.2 us -> 8.7 us  [the longest x2 3.82 us: sum_heads(): away.astype(value.dtype)]
    convert_element_type x6 -> x3, local copies, waits for them, and re-layouts: 8.41 us -> 0.2 us  [the longest x1 0.12 us: body(): weight_step.astype(low).reshape(rows_all, -1)]
    psum x2 -> x3, blocking collectives: 11.9 us -> 19.5 us  [the longest x1 6.86 us: body(): row_total = lax.psum(row_line, 'head')[0]]
  transfers between devices with their start and end apart: 64 -> 29, of which waited for: 29 -> 12; matrix products, arithmetic and copies ran while one was open for 24% -> 13% of each run, Pallas kernels for 4% -> 39%
where the time goes in v3:
time: 515 us; the launch traced here: 513 us
  Pallas kernels  221 us (43%)
  waiting for transfers between devices  157 us (30%)
  local copies, waits for them, and re-layouts  36.4 us (7%)
  other arithmetic  34.1 us (7%)
  starting transfers between devices  29.6 us (6%)
  blocking collectives  19.5 us (4%)
  between operations  14.8 us (3%)
    pallas_call x13, Pallas kernels, call(): pl.pallas_call(kernel, out_shape=outs, grid_spec=pltpu.PrefetchScalarGrid...  124 us
    ppermute x9, waiting for transfers between devices, rows_phase(): held.append(lax.ppermute(shard, 'dp', perm))  86.9 us
    pallas_call x1, Pallas kernels, mixer_back(): pl.pallas_call(functools.partial(mixer_back_kernel, heads, count), out_sh...  43 us
    pallas_call x1, Pallas kernels, mixer(): pl.pallas_call(functools.partial(mixer_kernel, heads), out_shape=(jax.Sha...  24.8 us
    ppermute x2, waiting for transfers between devices, sum_heads(): lax.ppermute(away.astype(value.dtype), 'head', [(i, i ^ 2) for i in range...  23.5 us
    ppermute x3, waiting for transfers between devices, end_gather(): return (own, lax.ppermute(own, 'dp', swap_pairs(8)))  19.1 us
    ppermute x9, starting transfers between devices, rows_phase(): held.append(lax.ppermute(shard, 'dp', perm))  13.4 us
    unnamed x121, local copies, waits for them, and re-layouts  13.1 us
  transfers between devices with their start and end apart: 29, of which 12 were waited for; matrix products, arithmetic and copies ran while one was open for 13% of the time, Pallas kernels for 39%

profile of v3, /device:TPU:0, one launch (start us, length us, event | category | flops | bytes accessed | tf_op | source)
XLA Modules:
  0.0 512.5 jit_solution(16505374086128054457)
XLA Ops:
  12.1 2.3 copy.164
  14.5 5.1 collective-permute-start.2
  23.9 9.1 %collective-permute-done.2.refs_3_ = bf16[256,1024]{1,0:T(8,128)(2,1)} collective-permute-done((bf16[256,1024]{1,0:T(8,128)(2,1)S(1)}, bf16[256,1024]{1,0:T(8,128)(2,1)}, u32[]{:S(2)}, u32[]{:S(2)}) %collective-permute-start.2) | collective-permute-done | bytes 524320 | tf_op jit(solution)/shard_map/ppermute | solution.py:563
  33.0 33.4 %collective-permute-done.1.refs_2_ = bf16[256,1024]{1,0:T(8,128)(2,1)} collective-permute-done((bf16[256,1024]{1,0:T(8,128)(2,1)S(1)}, bf16[256,1024]{1,0:T(8,128)(2,1)}, u32[]{:S(2)}, u32[]{:S(2)}) %collective-permute-start.1) | collective-permute-done | bytes 524320 | tf_op jit(solution)/shard_map/ppermute | solution.py:563
  66.4 4.1 place.3.w_own.refs_2_
  70.5 3.3 collective-permute-start.5
  73.8 2.0 collective-permute-start.4
  77.1 1.6 collective-permute-start.3
  78.7 8.2 %collective-permute-done.6.refs_3_ = bf16[256,1024]{1,0:T(8,128)(2,1)S(1)} collective-permute-done((bf16[256,1024]{1,0:T(8,128)(2,1)S(1)}, bf16[256,1024]{1,0:T(8,128)(2,1)S(1)}, u32[]{:S(2)}, u32[]{:S(2)}) %collective-permute-start.6) | collective-permute-done | bytes 524320 | tf_op jit(solution)/shard_map/ppermute | solution.py:563
  86.9 36.1 %collective-permute-done.5.refs_2_ = bf16[256,1024]{1,0:T(8,128)(2,1)} collective-permute-done((bf16[256,1024]{1,0:T(8,128)(2,1)S(1)}, bf16[256,1024]{1,0:T(8,128)(2,1)}, u32[]{:S(2)}, u32[]{:S(2)}) %collective-permute-start.5) | collective-permute-done | bytes 524320 | tf_op jit(solution)/shard_map/ppermute | solution.py:563
  123.0 2.0 collective-permute-start.7
  125.1 4.1 place.4.w_own.refs_0_
  129.2 1.6 collective-permute-start.11
  136.6 1.5 broadcast_select_fusion
  138.2 4.9 halves.2
  143.1 5.8 %norm.1 = (bf16[1024,1024]{1,0:T(8,128)(2,1)}, bf16[1024,1024]{1,0:T(8,128)(2,1)}, f32[1,1024]{1,0:T(1,128)}) custom-call(bf16[1024,1024]{1,0:T(8,128)(2,1)} %get-tuple-element.76.own_in.xo, bf16[1024,1024]{1,0:T(8,128)(2,1)} %get-tuple-element.77.other_in.xt, f32[2,1024]{1,0:T(2,128)} %pad_maximum_fusion.3.gains), custom_call_target="tpu_custom_call" | custom-call | flops 6000000000 | bytes 18000000 | tf_op jit(solution)/shard_map/norm/pallas_call | solution.py:688
  148.9 9.4 %project.2.v_ref.v_tail = f32[1024,1024]{1,0:T(8,128)} custom-call(bf16[1024,1024]{1,0:T(8,128)(2,1)} %get-tuple-element.78.own, bf16[1024,1024]{1,0:T(8,128)(2,1)} %get-tuple-element.79.other, bf16[1024,1024]{1,0:T(8,128)(2,1)} %place.3.w_own.refs_2_, bf16[1024,1024]{1,0:T(8,128)(2,1)} %collective-permute-done.3.w_other.refs_3_), custom_call_target="tpu_custom_call" | custom-call | flops 8000000000 | bytes 24000000 | tf_op jit(solution)/shard_map/project/pallas_call | solution.py:688
  158.2 6.1 %project.3.s_ref.s_tail = f32[1024,384]{1,0:T(8,128)} custom-call(bf16[1024,1024]{1,0:T(8,128)(2,1)} %get-tuple-element.78.own, bf16[1024,1024]{1,0:T(8,128)(2,1)} %get-tuple-element.79.other, bf16[1024,384]{1,0:T(8,128)(2,1)} %bitcast.166, bf16[1024,384]{1,0:T(8,128)(2,1)} %bitcast.164), custom_call_target="tpu_custom_call" | custom-call | flops 8000000000 | bytes 24000000 | tf_op jit(solution)/shard_map/project/pallas_call | solution.py:688
  164.3 24.8 %mixer.1 = (f32[1024,1024]{1,0:T(8,128)}, f32[4,128,1024]{2,1,0:T(8,128)}) custom-call(s32[4]{0:T(128)} %opens.3, s32[4]{0:T(128)} %widths.3, f32[1024,1024]{1,0:T(8,128)} %project.2.v_ref.v_tail, f32[1024,384]{1,0:T(8,128)} %project.3.s_ref.s_tail, f32[8,1024]{1,0:T(8,128)} %maximum_maximum_fusion.1.tx, f32[8,256]{1,0:T(8,128)} %pad_convert_fusion.ts, ...), custom_call_target="tpu_custom_call" | custom-call | flops 24999999488 | bytes 75000000 | tf_op jit(solution)/shard_map/mixer/pallas_call | solution.py:337
  189.2 4.2 place.5.w_own
  193.3 1.9 collective-permute-start.10
  195.9 1.4 copy.149
  199.2 10.2 %gate.1 = (f32[1024,1024]{1,0:T(8,128)}, f32[1,1024]{1,0:T(1,128)}) custom-call(bf16[1024,1024]{1,0:T(8,128)(2,1)} %get-tuple-element.78.own, bf16[1024,1024]{1,0:T(8,128)(2,1)} %get-tuple-element.79.other, bf16[1024,1024]{1,0:T(8,128)(2,1)} %place.4.w_own.refs_0_, bf16[1024,1024]{1,0:T(8,128)(2,1)} %collective-permute-done.11.w_other.refs_1_, ...), custom_call_target="tpu_custom_call" | custom-call | flops 10000000000 | bytes 30000000 | tf_op jit(solution)/shard_map/gate/pallas_call | solution.py:688
  209.5 6.5 %psum.21 = f32[1,1024]{1,0:T(1,128)S(1)} all-reduce(f32[1,1024]{1,0:T(1,128)} %get-tuple-element.94), channel_id=1, replica_groups=mesh['dp'=8,'head'=4] {'head'}, use_global_device_ids=true, to_apply=%region_0.1 | all-reduce | flops 1024 | bytes 8192 | tf_op jit(solution)/shard_map/psum | solution.py:1170
  216.6 6.0 %scale.1.value.back = bf16[1024,1024]{1,0:T(8,128)(2,1)} custom-call(f32[1024,1024]{1,0:T(8,128)} %get-tuple-element.86.mixed, f32[1024,1024]{1,0:T(8,128)} %get-tuple-element.93.gate, f32[1,1024]{1,0:T(1,128)} %add_rsqrt_fusion.scale, f32[1,1024]{1,0:T(1,128)} %slice.164.gain), custom_call_target="tpu_custom_call" | custom-call | flops 6000000000 | bytes 18000000 | tf_op jit(solution)/shard_map/scale/pallas_call | solution.py:688
  222.5 19.1 %collective-permute-done.10.w_other = bf16[1024,1024]{1,0:T(8,128)(2,1)} collective-permute-done((bf16[1024,1024]{1,0:T(8,128)(2,1)}, bf16[1024,1024]{1,0:T(8,128)(2,1)}, u32[]{:S(2)}, u32[]{:S(2)}) %collective-permute-start.10) | collective-permute-done | bytes 2097184 | tf_op jit(solution)/shard_map/ppermute | solution.py:580
  241.6 4.9 halves.3
  246.5 10.8 %whole_weight.3 = bf16[2048,1024]{1,0:T(8,128)(2,1)} custom-call(s32[1]{0:T(128)} %bitcast.column, bf16[1024,1024]{1,0:T(8,128)(2,1)} %get-tuple-element.83.own, bf16[1024,1024]{1,0:T(8,128)(2,1)} %get-tuple-element.84.other, bf16[1024,1024]{1,0:T(8,128)(2,1)} %scale.1.value.back), custom_call_target="tpu_custom_call" | custom-call | flops 11000000512 | bytes 33000000 | tf_op jit(solution)/shard_map/whole_weight/pallas_call | solution.py:688
  257.3 11.1 %output_back.1 = (f32[1024,1024]{1,0:T(8,128)}, f32[1,1024]{1,0:T(1,128)}) custom-call(bf16[1024,1024]{1,0:T(8,128)(2,1)} %get-tuple-element.83.own, bf16[1024,1024]{1,0:T(8,128)(2,1)} %get-tuple-element.84.other, bf16[1024,1024]{1,0:T(8,128)(2,1)} %place.5.w_own, bf16[1024,1024]{1,0:T(8,128)(2,1)} %collective-permute-done.10.w_other, ...), custom_call_target="tpu_custom_call" | custom-call | flops 11000000512 | bytes 33000000 | tf_op jit(solution)/shard_map/output_back/pallas_call | solution.py:688
  268.5 6.2 %psum.22 = f32[1,1024]{1,0:T(1,128)S(1)} all-reduce(f32[1,1024]{1,0:T(1,128)} %get-tuple-element.98), channel_id=1, replica_groups=mesh['dp'=8,'head'=4] {'head'}, use_global_device_ids=true, to_apply=%region_1.2 | all-reduce | flops 1024 | bytes 8192 | tf_op jit(solution)/shard_map/psum | solution.py:1176
  275.2 9.8 %norm_back.1 = (f32[1024,1024]{1,0:T(8,128)}, bf16[1024,1024]{1,0:T(8,128)(2,1)}, f32[1,1024]{1,0:T(1,128)}) custom-call(s32[4]{0:T(128)} %widths.3, f32[1024,1024]{1,0:T(8,128)} %get-tuple-element.97.grad, f32[1024,1024]{1,0:T(8,128)} %get-tuple-element.86.mixed, f32[1024,1024]{1,0:T(8,128)} %get-tuple-element.93.gate, f32[1,1024]{1,0:T(1,128)} %slice.164.gain, ...), custom_call_target="tpu_custom_call" | custom-call | flops 10000000000 | bytes 30000000 | tf_op jit(solution)/shard_map/norm_back/pallas_call | solution.py:688
  285.1 8.2 %weight.3 = (f32[1024,1024]{1,0:T(8,128)}, bf16[1024,1024]{1,0:T(8,128)(2,1)}) custom-call(bf16[1024,1024]{1,0:T(8,128)(2,1)} %get-tuple-element.78.own, bf16[1024,1024]{1,0:T(8,128)(2,1)} %get-tuple-element.79.other, bf16[1024,1024]{1,0:T(8,128)(2,1)} %get-tuple-element.100.back.gate), custom_call_target="tpu_custom_call" | custom-call | flops 8000000000 | bytes 24000000 | tf_op jit(solution)/shard_map/weight/pallas_call | solution.py:688
  293.3 1.7 collective-permute-start.12
  295.0 43.0 %mixer_back.1 = (bf16[1024,1024]{1,0:T(8,128)(2,1)}, bf16[1024,384]{1,0:T(8,128)(2,1)}, f32[8,1024]{1,0:T(8,128)}, f32[8,256]{1,0:T(8,128)}, f32[8,128]{1,0:T(8,128)}) custom-call(s32[4]{0:T(128)} %opens.3, f32[1024,1024]{1,0:T(8,128)} %project.2.v_ref.v_tail, f32[1024,1024]{1,0:T(8,128)} %project.2.v_ref.v_tail, f32[1024,384]{1,0:T(8,128)} %project.3.s_ref.s_tail, ...), custom_call_target="tpu_custom_call" | custom-call | flops 43000000512 | bytes 129000000 | tf_op jit(solution)/shard_map/mixer_back/pallas_call | solution.py:379
  344.8 10.9 %whole_weight.2 = bf16[2048,1024]{1,0:T(8,128)(2,1)} custom-call(s32[1]{0:T(128)} %bitcast.column, bf16[1024,1024]{1,0:T(8,128)(2,1)} %get-tuple-element.78.own, bf16[1024,1024]{1,0:T(8,128)(2,1)} %get-tuple-element.79.other, bf16[1024,1024]{1,0:T(8,128)(2,1)} %get-tuple-element.110.back.inner), custom_call_target="tpu_custom_call" | custom-call | flops 11000000512 | bytes 33000000 | tf_op jit(solution)/shard_map/whole_weight/pallas_call | solution.py:688
  355.7 1.6 collective-permute-done.12
  357.4 6.6 %weight.5 = (f32[1024,384]{1,0:T(8,128)}, bf16[1024,384]{1,0:T(8,128)(2,1)}) custom-call(bf16[1024,1024]{1,0:T(8,128)(2,1)} %get-tuple-element.78.own, bf16[1024,1024]{1,0:T(8,128)(2,1)} %get-tuple-element.79.other, bf16[1024,384]{1,0:T(8,128)(2,1)} %get-tuple-element.111.small.back), custom_call_target="tpu_custom_call" | custom-call | flops 8000000000 | bytes 24000000 | tf_op jit(solution)/shard_map/weight/pallas_call | solution.py:688
  364.0 1.4 slice.130
  366.3 1.3 fusion.11
  367.6 1.7 collective-permute-start.17
  369.3 19.9 %input_back.1 = (bf16[4,1024,512]{2,1,0:T(8,128)(2,1)}, f32[1,1024]{1,0:T(1,128)}, f32[2,1024]{1,0:T(2,128)}) custom-call(s32[1]{0:T(128)} %bitcast.column, bf16[1024,1024]{1,0:T(8,128)(2,1)} %get-tuple-element.100.back.gate, bf16[1024,1024]{1,0:T(8,128)(2,1)} %get-tuple-element.110.back.inner, bf16[1024,384]{1,0:T(8,128)(2,1)} %get-tuple-element.111.small.back, ...), custom_call_target="tpu_custom_call" | custom-call | flops 20000000000 | bytes 60000000 | tf_op jit(solution)/shard_map/input_back/pallas_call | solution.py:688
  391.4 1.7 maximum_maximum_fusion
  393.8 1.5 dynamic-slice_bitcast_fusion
  395.3 8.8 %output.1 = bf16[4,1024,512]{2,1,0:T(8,128)(2,1)} custom-call(s32[1]{0:T(128)} %bitcast.column, bf16[1024,1024]{1,0:T(8,128)(2,1)} %scale.1.value.back, bf16[1024,1024]{1,0:T(8,128)(2,1)} %place.5.w_own, bf16[1024,1024]{1,0:T(8,128)(2,1)} %collective-permute-done.10.w_other), custom_call_target="tpu_custom_call" | custom-call | flops 8999999488 | bytes 27000000 | tf_op jit(solution)/shard_map/output/pallas_call | solution.py:688
  404.8 1.4 copy-done.9
  406.3 1.5 dynamic-slice_bitcast_fusion.1
  410.7 6.9 %psum.23 = f32[1024]{0:T(1024)S(1)} all-reduce(f32[1024]{0:T(1024)S(1)} %bitcast.180), channel_id=1, replica_groups=mesh['dp'=8,'head'=4] {'head'}, use_global_device_ids=true, to_apply=%region_2.3 | all-reduce | flops 1024 | bytes 8192 | tf_op jit(solution)/shard_map/psum | solution.py:1206
  418.1 1.5 collective-permute-start.21
  419.6 9.3 %collective-permute-done.21 = bf16[256,419]{1,0:T(8,128)(2,1)S(1)} collective-permute-done((bf16[256,419]{1,0:T(8,128)(2,1)S(1)}, bf16[256,419]{1,0:T(8,128)(2,1)S(1)}, u32[]{:S(2)}, u32[]{:S(2)}) %collective-permute-start.21) | collective-permute-done | bytes 214560 | tf_op jit(solution)/shard_map/ppermute | solution.py:587
  429.6 5.2 %collective-permute-done.22 = bf16[2,64,419]{2,1,0:T(8,128)(2,1)S(1)} collective-permute-done((bf16[2,64,419]{2,1,0:T(8,128)(2,1)S(1)}, bf16[2,64,419]{2,1,0:T(8,128)(2,1)S(1)}, u32[]{:S(2)}, u32[]{:S(2)}) %collective-permute-start.22) | collective-permute-done | bytes 107296 | tf_op jit(solution)/shard_map/ppermute | solution.py:614
  434.8 1.6 collective-permute-start.23
  436.4 2.7 fusion.16
  439.2 1.3 collective-permute-start.18
  440.5 10.4 %collective-permute-done.23 = bf16[64,419]{1,0:T(8,128)(2,1)S(1)} collective-permute-done((bf16[64,419]{1,0:T(8,128)(2,1)S(1)}, bf16[64,419]{1,0:T(8,128)(2,1)S(1)}, u32[]{:S(2)}, u32[]{:S(2)}) %collective-permute-start.23) | collective-permute-done | bytes 53664 | tf_op jit(solution)/shard_map/ppermute | solution.py:636
  452.7 1.8 fusion.3
  454.8 2.0 fusion.8
  456.8 1.9 collective-permute-start.14
  461.9 12.3 %collective-permute-done.16 = bf16[1024,512]{1,0:T(8,128)(2,1)S(1)} collective-permute-done((bf16[1024,512]{1,0:T(8,128)(2,1)S(1)}, bf16[1024,512]{1,0:T(8,128)(2,1)S(1)}, u32[]{:S(2)}, u32[]{:S(2)}) %collective-permute-start.16) | collective-permute-done | bytes 1048608 | tf_op jit(solution)/shard_map/ppermute | solution.py:923
  474.2 11.2 %collective-permute-done.14 = bf16[1024,512]{1,0:T(8,128)(2,1)S(1)} collective-permute-done((bf16[1024,512]{1,0:T(8,128)(2,1)S(1)}, bf16[1024,512]{1,0:T(8,128)(2,1)S(1)}, u32[]{:S(2)}, u32[]{:S(2)}) %collective-permute-start.14) | collective-permute-done | bytes 1048608 | tf_op jit(solution)/shard_map/ppermute | solution.py:923
  485.5 4.4 fusion.1
  489.9 3.1 multiply_add_fusion
  493.0 2.7 copy.154
  495.6 1.3 copy.152
  498.3 7.7 %advance_inner.1 = (f32[256,2,1024]{2,1,0:T(2,128)}, f32[256,2,1024]{2,1,0:T(2,128)}, f32[256,2,1024]{2,1,0:T(2,128)}) custom-call(f32[256,2,1024]{2,1,0:T(2,128)} %weight.4, f32[256,2,1024]{2,1,0:T(2,128)} %moment.1, f32[256,2,1024]{2,1,0:T(2,128)} %average.1, f32[256,1024]{1,0:T(8,128)} %get-tuple-element.258.refs_0_, ...), custom_call_target="tpu_custom_call" | custom-call | flops 8000000000 | bytes 24000000 | tf_op jit(solution)/shard_map/advance_inner/pallas_call | solution.py:446
  (260 shorter events, 41.9 us)
Async XLA Ops:
  7.2 123.5 %all-gather.9.cloned.1.call-start = ((), (), s32[]{:S(2)}) async-start(), calls=%async_computation.6 | async-start | bytes 1622016 | tf_op jit(solution)/shard_map/all_gather | solution.py:1122
  11.2 127.0 %all-gather.5.cloned.1.call-start = ((), (), s32[]{:S(2)}) async-start(), calls=%async_computation.2 | async-start | bytes 5242880 | tf_op jit(solution)/shard_map/all_gather | solution.py:1121
  12.0 8.6 %copy-start.40 = (f32[3,16]{1,0:T(4,128)S(1)}, f32[3,16]{1,0:T(4,128)}, u32[]{:S(2)}) copy-start(f32[3,16]{1,0:T(4,128)} %param.40) | copy-start | bytes 580
  12.0 9.3 %copy-start.26 = (f32[6,1024]{1,0:T(8,128)S(1)}, f32[6,1024]{1,0:T(8,128)}, u32[]{:S(2)}) copy-start(f32[6,1024]{1,0:T(8,128)} %param.39) | copy-start | bytes 73732
  12.0 9.3 %copy-start.18 = (f32[1024,256]{1,0:T(8,128)S(1)}, f32[1024,256]{1,0:T(8,128)}, u32[]{:S(2)}) copy-start(f32[1024,256]{1,0:T(8,128)} %param.36) | copy-start | bytes 3145732
  12.0 229.6 %all-gather.7.cloned.1.call-start = ((), (), s32[]{:S(2)}) async-start(), calls=%async_computation.3 | async-start | bytes 5242880 | tf_op jit(solution)/shard_map/all_gather | solution.py:1149
  14.3 7.5 %copy-start.54 = (s32[4]{0:T(128)S(1)}, s32[4]{0:T(128)}, u32[]{:S(2)}) copy-start(s32[4]{0:T(128)} %widths.3) | copy-start | bytes 52
  14.3 8.2 %copy-start.46 = (s32[1024]{0:T(1024)S(1)}, s32[1024]{0:T(1024)}, u32[]{:S(2)}) copy-start(s32[1024]{0:T(1024)} %param.31) | copy-start | bytes 12292
  14.4 52.0 %copy-start.24 = (bf16[256,1024]{1,0:T(8,128)(2,1)}, bf16[256,1024]{1,0:T(8,128)(2,1)S(1)}, u32[]{:S(2)}) copy-start(bf16[256,1024]{1,0:T(8,128)(2,1)S(1)} %get-tuple-element.265.refs_0_) | copy-start | bytes 1572868
  14.4 59.4 %copy-start.23 = (bf16[256,1024]{1,0:T(8,128)(2,1)}, bf16[256,1024]{1,0:T(8,128)(2,1)S(1)}, u32[]{:S(2)}) copy-start(bf16[256,1024]{1,0:T(8,128)(2,1)S(1)} %get-tuple-element.80.refs_0_) | copy-start | bytes 1572868
  14.5 18.5 %collective-permute-start.2 = (bf16[256,1024]{1,0:T(8,128)(2,1)S(1)}, bf16[256,1024]{1,0:T(8,128)(2,1)}, u32[]{:S(2)}, u32[]{:S(2)}) collective-permute-start(bf16[256,1024]{1,0:T(8,128)(2,1)S(1)} %get-tuple-element.265.refs_0_), channel_id=1, source_target_pairs={{0,24},{4,28},{8,0},{12,4},{16,8},{20,12},{24,16},{28,20},{1,25},{... | collective-permute-start | bytes 1572872 | tf_op jit(solution)/shard_map/ppermute | solution.py:563
  19.6 46.9 %collective-permute-start.1 = (bf16[256,1024]{1,0:T(8,128)(2,1)S(1)}, bf16[256,1024]{1,0:T(8,128)(2,1)}, u32[]{:S(2)}, u32[]{:S(2)}) collective-permute-start(bf16[256,1024]{1,0:T(8,128)(2,1)S(1)} %get-tuple-element.265.refs_0_), channel_id=1, source_target_pairs={{0,16},{4,20},{8,24},{12,28},{16,0},{20,4},{24,8},{28,12},{1,17},{... | collective-permute-start | bytes 1572872 | tf_op jit(solution)/shard_map/ppermute | solution.py:563
  19.6 46.9 %collective-permute-start = (bf16[256,1024]{1,0:T(8,128)(2,1)S(1)}, bf16[256,1024]{1,0:T(8,128)(2,1)}, u32[]{:S(2)}, u32[]{:S(2)}) collective-permute-start(bf16[256,1024]{1,0:T(8,128)(2,1)S(1)} %get-tuple-element.265.refs_0_), channel_id=1, source_target_pairs={{0,8},{4,12},{8,16},{12,20},{16,24},{20,28},{24,0},{28,4},{1,9},{5... | collective-permute-start | bytes 1572872 | tf_op jit(solution)/shard_map/ppermute | solution.py:563
  21.7 54.1 %copy-start = (f32[1024,256]{0,1:T(8,128)}, f32[1024,256]{0,1:T(8,128)S(1)}, u32[]{:S(2)}) copy-start(f32[1024,256]{0,1:T(8,128)S(1)} %copy.137) | copy-start | bytes 3145732
  70.5 5.4 %copy-start.10 = (bf16[1024,512]{1,0:T(8,128)(2,1)S(1)}, bf16[1024,512]{1,0:T(8,128)(2,1)}, u32[]{:S(2)}) copy-start(bf16[1024,512]{1,0:T(8,128)(2,1)} %param.30) | copy-start | bytes 3145732
  70.5 16.3 %collective-permute-start.6 = (bf16[256,1024]{1,0:T(8,128)(2,1)S(1)}, bf16[256,1024]{1,0:T(8,128)(2,1)S(1)}, u32[]{:S(2)}, u32[]{:S(2)}) collective-permute-start(bf16[256,1024]{1,0:T(8,128)(2,1)S(1)} %get-tuple-element.80.refs_0_), channel_id=1, source_target_pairs={{0,24},{4,28},{8,0},{12,4},{16,8},{20,12},{24,16},{28,20},{1,25},{... | collective-permute-start | bytes 1572872 | tf_op jit(solution)/shard_map/ppermute | solution.py:563
  70.5 52.5 %collective-permute-start.5 = (bf16[256,1024]{1,0:T(8,128)(2,1)S(1)}, bf16[256,1024]{1,0:T(8,128)(2,1)}, u32[]{:S(2)}, u32[]{:S(2)}) collective-permute-start(bf16[256,1024]{1,0:T(8,128)(2,1)S(1)} %get-tuple-element.80.refs_0_), channel_id=1, source_target_pairs={{0,16},{4,20},{8,24},{12,28},{16,0},{20,4},{24,8},{28,12},{1,17},{... | collective-permute-start | bytes 1572872 | tf_op jit(solution)/shard_map/ppermute | solution.py:563
  73.8 49.2 %collective-permute-start.4 = (bf16[256,1024]{1,0:T(8,128)(2,1)S(1)}, bf16[256,1024]{1,0:T(8,128)(2,1)}, u32[]{:S(2)}, u32[]{:S(2)}) collective-permute-start(bf16[256,1024]{1,0:T(8,128)(2,1)S(1)} %get-tuple-element.80.refs_0_), channel_id=1, source_target_pairs={{0,8},{4,12},{8,16},{12,20},{16,24},{20,28},{24,0},{28,4},{1,9},{5... | collective-permute-start | bytes 1572872 | tf_op jit(solution)/shard_map/ppermute | solution.py:563
  75.9 53.2 %copy-start.22 = (bf16[256,1024]{1,0:T(8,128)(2,1)}, bf16[256,1024]{1,0:T(8,128)(2,1)S(1)}, u32[]{:S(2)}) copy-start(bf16[256,1024]{1,0:T(8,128)(2,1)S(1)} %convert_bitcast_fusion.refs_0_) | copy-start | bytes 1572868
  77.1 71.8 %collective-permute-start.3 = (bf16[1024,1024]{1,0:T(8,128)(2,1)}, bf16[1024,1024]{1,0:T(8,128)(2,1)}, u32[]{:S(2)}, u32[]{:S(2)}) collective-permute-start(bf16[1024,1024]{1,0:T(8,128)(2,1)} %place.3.w_own.refs_2_), channel_id=1, source_target_pairs={{0,4},{4,0},{8,12},{12,8},{16,20},{20,16},{24,28},{28,24},{1,5},{5... | collective-permute-start | bytes 6291464 | tf_op jit(solution)/shard_map/ppermute | solution.py:580
  86.9 38.2 %copy-start.53 = (bf16[256,1024]{1,0:T(8,128)(2,1)}, bf16[256,1024]{1,0:T(8,128)(2,1)S(1)}, u32[]{:S(2)}) copy-start(bf16[256,1024]{1,0:T(8,128)(2,1)S(1)} %collective-permute-done.6.refs_3_) | copy-start | bytes 1572868
  123.0 66.1 %collective-permute-start.9 = (bf16[256,1024]{1,0:T(8,128)(2,1)S(1)}, bf16[256,1024]{1,0:T(8,128)(2,1)}, u32[]{:S(2)}, u32[]{:S(2)}) collective-permute-start(bf16[256,1024]{1,0:T(8,128)(2,1)S(1)} %convert_bitcast_fusion.refs_0_), channel_id=1, source_target_pairs={{0,24},{4,28},{8,0},{12,4},{16,8},{20,12},{24,16},{28,20},{1,25},{... | collective-permute-start | bytes 1572872 | tf_op jit(solution)/shard_map/ppermute | solution.py:563
  123.0 66.1 %collective-permute-start.8 = (bf16[256,1024]{1,0:T(8,128)(2,1)S(1)}, bf16[256,1024]{1,0:T(8,128)(2,1)}, u32[]{:S(2)}, u32[]{:S(2)}) collective-permute-start(bf16[256,1024]{1,0:T(8,128)(2,1)S(1)} %convert_bitcast_fusion.refs_0_), channel_id=1, source_target_pairs={{0,16},{4,20},{8,24},{12,28},{16,0},{20,4},{24,8},{28,12},{1,17},{... | collective-permute-start | bytes 1572872 | tf_op jit(solution)/shard_map/ppermute | solution.py:563
  123.0 66.1 %collective-permute-start.7 = (bf16[256,1024]{1,0:T(8,128)(2,1)S(1)}, bf16[256,1024]{1,0:T(8,128)(2,1)}, u32[]{:S(2)}, u32[]{:S(2)}) collective-permute-start(bf16[256,1024]{1,0:T(8,128)(2,1)S(1)} %convert_bitcast_fusion.refs_0_), channel_id=1, source_target_pairs={{0,8},{4,12},{8,16},{12,20},{16,24},{20,28},{24,0},{28,4},{1,9},{5... | collective-permute-start | bytes 1572872 | tf_op jit(solution)/shard_map/ppermute | solution.py:563
  129.2 70.1 %collective-permute-start.11 = (bf16[1024,1024]{1,0:T(8,128)(2,1)}, bf16[1024,1024]{1,0:T(8,128)(2,1)}, u32[]{:S(2)}, u32[]{:S(2)}) collective-permute-start(bf16[1024,1024]{1,0:T(8,128)(2,1)} %place.4.w_own.refs_0_), channel_id=1, source_target_pairs={{0,4},{4,0},{8,12},{12,8},{16,20},{20,16},{24,28},{28,24},{1,5},{5... | collective-permute-start | bytes 6291464 | tf_op jit(solution)/shard_map/ppermute | solution.py:580
  135.4 354.5 %reduce-scatter.5.cloned.1.call-start = ((), (), s32[]{:S(2)}) async-start(), calls=%async_computation.5 | async-start | bytes 4718592 | tf_op jit(solution)/shard_map/reduce_scatter | solution.py:1173
  189.1 6.7 %copy-start.19 = (f32[1024,256]{1,0:T(8,128)S(1)}, f32[1024,256]{1,0:T(8,128)}, u32[]{:S(2)}) copy-start(f32[1024,256]{1,0:T(8,128)} %param.44) | copy-start | bytes 3145732
  193.3 48.3 %collective-permute-start.10 = (bf16[1024,1024]{1,0:T(8,128)(2,1)}, bf16[1024,1024]{1,0:T(8,128)(2,1)}, u32[]{:S(2)}, u32[]{:S(2)}) collective-permute-start(bf16[1024,1024]{1,0:T(8,128)(2,1)} %place.5.w_own), channel_id=1, source_target_pairs={{0,4},{4,0},{8,12},{12,8},{16,20},{20,16},{24,28},{28,24},{1,5},{5... | collective-permute-start | bytes 6291464 | tf_op jit(solution)/shard_map/ppermute | solution.py:580
  257.3 17.4 %copy-start.39 = (f32[1,1024]{1,0:T(1,128)S(1)}, f32[1,1024]{1,0:T(1,128)}, u32[]{:S(2)}) copy-start(f32[1,1024]{1,0:T(1,128)} %add_rsqrt_fusion.scale) | copy-start | bytes 12292
  257.3 241.0 %reduce-scatter.3.cloned.1.call-start = ((), (), s32[]{:S(2)}) async-start(), calls=%async_computation.4 | async-start | bytes 4718592 | tf_op jit(solution)/shard_map/reduce_scatter | solution.py:1188
  293.3 64.0 %collective-permute-start.12 = (bf16[1024,1024]{1,0:T(8,128)(2,1)}, bf16[1024,1024]{1,0:T(8,128)(2,1)S(1)}, u32[]{:S(2)}, u32[]{:S(2)}) collective-permute-start(bf16[1024,1024]{1,0:T(8,128)(2,1)} %get-tuple-element.101), channel_id=1, source_target_pairs={{0,4},{4,0},{8,12},{12,8},{16,20},{20,16},{24,28},{28,24},{1,5},{5... | collective-permute-start | bytes 6291464 | tf_op jit(solution)/shard_map/ppermute | solution.py:587
  295.0 44.8 %copy-start.45 = (f32[1,1024]{1,0:T(1,128)S(1)}, f32[1,1024]{1,0:T(1,128)}, u32[]{:S(2)}) copy-start(f32[1,1024]{1,0:T(1,128)} %get-tuple-element.124) | copy-start | bytes 12292
  357.4 9.0 %copy-start.13 = (bf16[1024,1024]{1,0:T(8,128)(2,1)}, bf16[1024,1024]{1,0:T(8,128)(2,1)S(1)}, u32[]{:S(2)}) copy-start(bf16[1024,1024]{1,0:T(8,128)(2,1)S(1)} %collective-permute-done.12) | copy-start | bytes 6291460
  357.4 9.0 %copy-start.2 = (f32[1024,1024]{1,0:T(8,128)S(1)}, f32[1024,1024]{1,0:T(8,128)}, u32[]{:S(2)}) copy-start(f32[1024,1024]{1,0:T(8,128)} %get-tuple-element.102) | copy-start | bytes 12582916
  367.6 68.8 %collective-permute-start.17 = (bf16[2,256,1024]{2,1,0:T(8,128)(2,1)}, bf16[2,256,1024]{2,1,0:T(8,128)(2,1)}, u32[]{:S(2)}, u32[]{:S(2)}) collective-permute-start(bf16[2,256,1024]{2,1,0:T(8,128)(2,1)} %fusion.11), channel_id=1, source_target_pairs={{0,8},{4,12},{8,0},{12,4},{16,24},{20,28},{24,16},{28,20},{1,9},{5... | collective-permute-start | bytes 3145736 | tf_op jit(solution)/shard_map/ppermute | solution.py:614
  369.3 22.1 %copy-start.15 = (f32[1,4,4,64,1]{4,3,1,0,2:T(8,128)S(1)}, f32[1,4,4,64,1]{4,3,1,0,2:T(8,128)}, u32[]{:S(2)}) copy-start(f32[1,4,4,64,1]{4,3,1,0,2:T(8,128)} %copy.146) | copy-start | bytes 12292
  369.3 22.1 %copy-start.16 = (f32[1,4,4,64,1]{4,3,1,0,2:T(8,128)S(1)}, f32[1,4,4,64,1]{4,3,1,0,2:T(8,128)}, u32[]{:S(2)}) copy-start(f32[1,4,4,64,1]{4,3,1,0,2:T(8,128)} %copy.143) | copy-start | bytes 12292
  369.3 22.1 %copy-start.17 = (bf16[1024,256]{1,0:T(8,128)(2,1)S(1)}, bf16[1024,256]{1,0:T(8,128)(2,1)}, u32[]{:S(2)}) copy-start(bf16[1024,256]{1,0:T(8,128)(2,1)} %slice.135) | copy-start | bytes 1572868
  393.3 10.8 %collective-permute-start.19 = (bf16[2,2,4,64,258]{4,3,2,1,0:T(8,128)(2,1)S(1)}, bf16[2,2,4,64,258]{4,3,2,1,0:T(8,128)(2,1)S(1)}, u32[]{:S(2)}, u32[]{:S(2)}) collective-permute-start(bf16[2,2,4,64,258]{4,3,2,1,0:T(8,128)(2,1)S(1)} %fusion.14), channel_id=1, source_target_pairs={{0,1},{1,0},{2,3},{3,2},{4,5},{5,4},{6,7},{7,6},{8,9},{9,8},{10,11... | collective-permute-start | bytes 1585160 | tf_op jit(solution)/shard_map/ppermute | solution.py:653
  395.3 57.4 %collective-permute-start.15 = (bf16[2,1024,512]{2,1,0:T(8,128)(2,1)}, bf16[2,1024,512]{2,1,0:T(8,128)(2,1)}, u32[]{:S(2)}, u32[]{:S(2)}) collective-permute-start(bf16[2,1024,512]{2,1,0:T(8,128)(2,1)} %dynamic-slice_bitcast_fusion), channel_id=1, source_target_pairs={{0,1},{1,0},{2,3},{3,2},{4,5},{5,4},{6,7},{7,6},{8,9},{9,8},{10,11... | collective-permute-start | bytes 6291464 | tf_op jit(solution)/shard_map/ppermute | solution.py:916
  404.3 13.2 %collective-permute-start.20 = (bf16[2,4,64,258]{3,2,1,0:T(8,128)(2,1)S(1)}, bf16[2,4,64,258]{3,2,1,0:T(8,128)(2,1)S(1)}, u32[]{:S(2)}, u32[]{:S(2)}) collective-permute-start(bf16[2,4,64,258]{3,2,1,0:T(8,128)(2,1)S(1)} %fusion.17), channel_id=1, source_target_pairs={{0,2},{1,3},{2,0},{3,1},{4,6},{5,7},{6,4},{7,5},{8,10},{9,11},{10,... | collective-permute-start | bytes 792584 | tf_op jit(solution)/shard_map/ppermute | solution.py:657
  407.7 47.0 %collective-permute-start.13 = (bf16[2,1024,512]{2,1,0:T(8,128)(2,1)}, bf16[2,1024,512]{2,1,0:T(8,128)(2,1)}, u32[]{:S(2)}, u32[]{:S(2)}) collective-permute-start(bf16[2,1024,512]{2,1,0:T(8,128)(2,1)} %dynamic-slice_bitcast_fusion.1), channel_id=1, source_target_pairs={{0,1},{1,0},{2,3},{3,2},{4,5},{5,4},{6,7},{7,6},{8,9},{9,8},{10,11... | collective-permute-start | bytes 6291464 | tf_op jit(solution)/shard_map/ppermute | solution.py:916
  410.5 7.2 %copy-start.28 = (f32[64,97]{1,0:T(8,128)S(1)}, f32[64,97]{1,0:T(8,128)}, u32[]{:S(2)}) copy-start(f32[64,97]{1,0:T(8,128)} %reshape.341) | copy-start | bytes 74500
  417.5 11.6 %copy-start.14 = (bf16[1024,1024]{1,0:T(8,128)(2,1)S(1)}, bf16[1024,1024]{1,0:T(8,128)(2,1)}, u32[]{:S(2)}) copy-start(bf16[1024,1024]{1,0:T(8,128)(2,1)} %copy-done.13) | copy-start | bytes 6291460
  417.7 11.4 %copy-start.3 = (f32[1024,1024]{1,0:T(8,128)S(1)}, f32[1024,1024]{1,0:T(8,128)}, u32[]{:S(2)}) copy-start(f32[1024,1024]{1,0:T(8,128)} %get-tuple-element.102) | copy-start | bytes 12582916
  418.1 10.9 %collective-permute-start.21 = (bf16[256,419]{1,0:T(8,128)(2,1)S(1)}, bf16[256,419]{1,0:T(8,128)(2,1)S(1)}, u32[]{:S(2)}, u32[]{:S(2)}) collective-permute-start(bf16[256,419]{1,0:T(8,128)(2,1)S(1)} %bitcast.169), channel_id=1, source_target_pairs={{0,4},{4,0},{8,12},{12,8},{16,20},{20,16},{24,28},{28,24},{1,5},{5... | collective-permute-start | bytes 643592 | tf_op jit(solution)/shard_map/ppermute | solution.py:587
  429.0 5.7 %collective-permute-start.22 = (bf16[2,64,419]{2,1,0:T(8,128)(2,1)S(1)}, bf16[2,64,419]{2,1,0:T(8,128)(2,1)S(1)}, u32[]{:S(2)}, u32[]{:S(2)}) collective-permute-start(bf16[2,64,419]{2,1,0:T(8,128)(2,1)S(1)} %get-tuple-element.266), channel_id=1, source_target_pairs={{0,8},{4,12},{8,0},{12,4},{16,24},{20,28},{24,16},{28,20},{1,9},{5... | collective-permute-start | bytes 321800 | tf_op jit(solution)/shard_map/ppermute | solution.py:614
  434.8 17.3 %copy-start.41 = (f32[3,16]{1,0:T(4,128)S(1)}, f32[3,16]{1,0:T(4,128)}, u32[]{:S(2)}) copy-start(f32[3,16]{1,0:T(4,128)} %param.40) | copy-start | bytes 580
  434.8 17.3 %copy-start.48 = (f32[3,16]{1,0:T(4,128)S(1)}, f32[3,16]{1,0:T(4,128)}, u32[]{:S(2)}) copy-start(f32[3,16]{1,0:T(4,128)} %param.56) | copy-start | bytes 580
  434.8 17.3 %copy-start.49 = (f32[3,16]{1,0:T(4,128)S(1)}, f32[3,16]{1,0:T(4,128)}, u32[]{:S(2)}) copy-start(f32[3,16]{1,0:T(4,128)} %param.48) | copy-start | bytes 580
  434.8 16.2 %collective-permute-start.23 = (bf16[64,419]{1,0:T(8,128)(2,1)S(1)}, bf16[64,419]{1,0:T(8,128)(2,1)S(1)}, u32[]{:S(2)}, u32[]{:S(2)}) collective-permute-start(bf16[64,419]{1,0:T(8,128)(2,1)S(1)} %fusion.21), channel_id=1, source_target_pairs={{0,16},{4,20},{8,24},{12,28},{16,0},{20,4},{24,8},{28,12},{1,17},{... | collective-permute-start | bytes 160904 | tf_op jit(solution)/shard_map/ppermute | solution.py:636
  439.2 59.1 %collective-permute-start.18 = (bf16[256,1024]{1,0:T(8,128)(2,1)}, bf16[256,1024]{1,0:T(8,128)(2,1)}, u32[]{:S(2)}, u32[]{:S(2)}) collective-permute-start(bf16[256,1024]{1,0:T(8,128)(2,1)} %get-tuple-element.257), channel_id=1, source_target_pairs={{0,16},{4,20},{8,24},{12,28},{16,0},{20,4},{24,8},{28,12},{1,17},{... | collective-permute-start | bytes 1572872 | tf_op jit(solution)/shard_map/ppermute | solution.py:636
  454.6 5.9 %copy-start.27 = (f32[6,1024]{1,0:T(8,128)S(1)}, f32[6,1024]{1,0:T(8,128)}, u32[]{:S(2)}) copy-start(f32[6,1024]{1,0:T(8,128)} %param.39) | copy-start | bytes 73732
  454.6 5.9 %copy-start.32 = (f32[6,1024]{1,0:T(8,128)S(1)}, f32[6,1024]{1,0:T(8,128)}, u32[]{:S(2)}) copy-start(f32[6,1024]{1,0:T(8,128)} %param.55) | copy-start | bytes 73732
  454.6 5.9 %copy-start.33 = (f32[6,1024]{1,0:T(8,128)S(1)}, f32[6,1024]{1,0:T(8,128)}, u32[]{:S(2)}) copy-start(f32[6,1024]{1,0:T(8,128)} %param.47) | copy-start | bytes 73732
  454.6 6.5 %copy-start.25 = (f32[64,256]{1,0:T(8,128)S(1)}, f32[64,256]{1,0:T(8,128)}, u32[]{:S(2)}) copy-start(f32[64,256]{1,0:T(8,128)} %param.37) | copy-start | bytes 196612
  454.6 6.5 %copy-start.29 = (f32[64,256]{1,0:T(8,128)S(1)}, f32[64,256]{1,0:T(8,128)}, u32[]{:S(2)}) copy-start(f32[64,256]{1,0:T(8,128)} %param.53) | copy-start | bytes 196612
  454.7 6.5 %copy-start.30 = (f32[64,256]{1,0:T(8,128)S(1)}, f32[64,256]{1,0:T(8,128)}, u32[]{:S(2)}) copy-start(f32[64,256]{1,0:T(8,128)} %param.45) | copy-start | bytes 196612
  454.7 30.7 %copy-start.11 = (bf16[1024,512]{1,0:T(8,128)(2,1)S(1)}, bf16[1024,512]{1,0:T(8,128)(2,1)}, u32[]{:S(2)}) copy-start(bf16[1024,512]{1,0:T(8,128)(2,1)} %param.30) | copy-start | bytes 3145732
  454.7 30.7 %copy-start.12 = (bf16[1024,512]{1,0:T(8,128)(2,1)S(1)}, bf16[1024,512]{1,0:T(8,128)(2,1)}, u32[]{:S(2)}) copy-start(bf16[1024,512]{1,0:T(8,128)(2,1)} %param.29) | copy-start | bytes 3145732
  454.7 30.7 %copy-start.35 = (f32[1024]{0:T(1024)S(1)}, f32[1024]{0:T(1024)}, u32[]{:S(2)}) copy-start(f32[1024]{0:T(1024)} %get-tuple-element.268) | copy-start | bytes 12292
  454.7 30.7 %copy-start.42 = (f32[512]{0:T(512)S(1)}, f32[512]{0:T(512)}, u32[]{:S(2)}) copy-start(f32[512]{0:T(512)} %dynamic_slice.132) | copy-start | bytes 6148
  454.7 19.5 %collective-permute-start.16 = (bf16[1024,512]{1,0:T(8,128)(2,1)S(1)}, bf16[1024,512]{1,0:T(8,128)(2,1)S(1)}, u32[]{:S(2)}, u32[]{:S(2)}) collective-permute-start(bf16[1024,512]{1,0:T(8,128)(2,1)S(1)} %fusion.3), channel_id=1, source_target_pairs={{0,2},{1,3},{2,0},{3,1},{4,6},{5,7},{6,4},{7,5},{8,10},{9,11},{10,... | collective-permute-start | bytes 3145736 | tf_op jit(solution)/shard_map/ppermute | solution.py:923
  456.8 28.6 %collective-permute-start.14 = (bf16[1024,512]{1,0:T(8,128)(2,1)S(1)}, bf16[1024,512]{1,0:T(8,128)(2,1)S(1)}, u32[]{:S(2)}, u32[]{:S(2)}) collective-permute-start(bf16[1024,512]{1,0:T(8,128)(2,1)S(1)} %fusion.8), channel_id=1, source_target_pairs={{0,2},{1,3},{2,0},{3,1},{4,6},{5,7},{6,4},{7,5},{8,10},{9,11},{10,... | collective-permute-start | bytes 3145736 | tf_op jit(solution)/shard_map/ppermute | solution.py:923
  (20 other events, 77.5 us)
Sparse Core Ops, SparseCore 0:
  11.5 91.7 all-gather.8
  104.9 33.3 all-gather.4
  140.4 34.4 all-gather.6
  257.4 105.0 reduce-scatter.4
  366.4 112.9 reduce-scatter.2
